TPU v7x, 256 devices: a whole 4x4x8 slice. The times are simulated.
256 devices in a mesh: ctx: 32 (over x, y, core), ch: 8 (over z).
Axes of the slice: x: 4, y: 4, z: 8, core: 2. Of those that a mesh axis runs over, the one named last changes fastest.
Arguments:
- gate_input: bfloat16 [8192, 16384], P('ch', 'ctx'), may hold values from -90 to 90
- key_input: bfloat16 [8192, 16384], P('ch', 'ctx'), may hold values from -6 to 6
- value_input: bfloat16 [8192, 16384], P('ch', 'ctx'), may hold values from -6 to 6
- short_filter: float32 [3, 3, 8192], P(None, None, 'ch'), may hold values from -3.5 to 3.5
- mr_filter: float32 [512, 128], P('ch'), may hold values from -0.5 to 0.5
- mr_skip: float32 [8192], P('ch'), may hold values from -3 to 3
- norm_gain: float32 [8192], P('ch'), may hold values from 0.5 to 1.5
- doc_lengths: int32 [64], replicated, may hold values from 1 to 2048, 16384 in all
Outputs:
- relaid: bfloat16 [8192, 16384], P(('ch', 'ctx'))
Inputs may be any that keep to these rules, and one draw needn't show every extreme that they name: `doc_lengths`: the 64 lengths sum to 16384, and one of them is exactly 2048.
All inputs are finite; a program needn't handle non-finite values.
Results may differ from a plain program's by a relative error of at most 0.0095.
Values may be sent and summed in bfloat16 or wider, within the bound.
No kernel may reach another device: no remote copies, remote signals or barrier semaphores. Data moves between devices by JAX's collectives and lax.ppermute only.
A program may use at most 128 MiB of HBM per device.

v0:
```python
import math

import jax
import jax.numpy as jnp
from jax import lax
from jax.sharding import PartitionSpec as P

D = 8192
GROUP = 16
SHORT = 3
MR = 128


NORM_EPS = 1e-06


def doc_starts(doc_lengths, positions):
    doc_ends = jnp.cumsum(doc_lengths)
    doc_firsts = doc_ends - doc_lengths
    before_row = doc_firsts[:, None] <= positions[None, :]
    return jnp.max(jnp.where(before_row, doc_firsts[:, None], 0), axis=0)


def short_conv(raw_rows, prior_rows, tap_rows, positions, starts):
    row_count = raw_rows.shape[1]
    extended = jnp.concatenate([prior_rows, raw_rows], axis=1).astype(jnp.float32)
    running = jnp.zeros(raw_rows.shape, jnp.float32)
    for tap_lag in range(SHORT):
        lagged = lax.slice_in_dim(
            extended, SHORT - 1 - tap_lag, SHORT - 1 - tap_lag + row_count, axis=1
        )
        in_document = positions - tap_lag >= starts
        running = running + jnp.where(
            in_document[None, :], tap_rows[tap_lag][:, None] * lagged, 0.0
        )
    return running


def features(raw_list, prior_list, short_taps, positions, starts):
    gate_conv = short_conv(raw_list[0], prior_list[0], short_taps[0], positions, starts)
    key_conv = short_conv(raw_list[1], prior_list[1], short_taps[1], positions, starts)
    value_conv = short_conv(raw_list[2], prior_list[2], short_taps[2], positions, starts)
    return (gate_conv, (key_conv * value_conv).astype(jnp.bfloat16))


def toeplitz(taps_bf):
    groups = taps_bf.shape[0]
    padded = jnp.concatenate(
        [jnp.zeros((groups, MR), jnp.bfloat16), taps_bf, jnp.zeros((groups, MR + 1), jnp.bfloat16)],
        axis=1,
    )
    repeated = jnp.tile(padded, (1, 2 * MR))[:, : 2 * MR * 3 * MR].reshape(groups, 2 * MR, 3 * MR)
    return repeated[:, :, 2 * MR :]


def long_conv(values, prior_rows, taps_bf, starts):
    channels, row_count = values.shape
    groups = taps_bf.shape[0]
    members = channels // groups
    tile_count = row_count // MR
    blocked = jnp.concatenate([prior_rows, values], axis=1).reshape(channels, tile_count + 1, MR)
    windows = jnp.concatenate([blocked[:, :-1], blocked[:, 1:]], axis=2).reshape(
        groups, members, tile_count, 2 * MR
    )
    matrices = toeplitz(taps_bf)
    per_step = math.gcd(tile_count, max(1, 64 // groups))
    tile_starts = starts.reshape(tile_count, MR)
    source_offsets = jnp.arange(2 * MR, dtype=jnp.int32) - MR
    step_offsets = jnp.arange(per_step, dtype=jnp.int32) * MR
    zero_bf = jnp.zeros((), jnp.bfloat16)

    def advance(step_index, result):
        block_begin = step_index * per_step
        window_part = lax.dynamic_slice_in_dim(windows, block_begin, per_step, axis=2)
        row_starts = lax.dynamic_slice_in_dim(tile_starts, block_begin, per_step, axis=0)
        tile_first = block_begin * MR + step_offsets
        sources = tile_first[:, None] + source_offsets[None, :]
        allowed = sources[:, :, None] >= row_starts[:, None, :]
        masked = jnp.where(allowed[:, None], matrices[None], zero_bf)
        product = jnp.einsum(
            "gcns,ngst->gcnt", window_part, masked, preferred_element_type=jnp.float32
        )
        return lax.dynamic_update_slice_in_dim(result, product, block_begin, axis=2)

    result = lax.fori_loop(
        0,
        tile_count // per_step,
        advance,
        jnp.zeros((groups, members, tile_count, MR), jnp.float32),
    )
    return result.reshape(channels, row_count)


def row_total(partial_value):
    return lax.psum(partial_value, "ch")


def local(
    gate_input, key_input, value_input, short_filter, mr_filter, mr_skip, norm_gain, doc_lengths
):
    ctx_place = lax.axis_index("ctx")
    stacked = jnp.stack([gate_input, key_input, value_input])
    received = lax.all_to_all(stacked, "ctx", split_axis=1, concat_axis=2, tiled=True)
    narrow = received.shape[1]
    all_rows = received.shape[2]
    chan_offset = ctx_place * narrow
    positions = jnp.arange(all_rows, dtype=jnp.int32)
    starts = doc_starts(doc_lengths, positions)
    short_taps = lax.dynamic_slice_in_dim(short_filter, chan_offset, narrow, axis=2)
    zero_prior = jnp.zeros((narrow, SHORT - 1), jnp.bfloat16)
    gate_conv, product_rows = features(
        [received[0], received[1], received[2]],
        [zero_prior, zero_prior, zero_prior],
        short_taps,
        positions,
        starts,
    )
    group_rows = lax.dynamic_slice_in_dim(
        mr_filter, chan_offset // GROUP, max(1, narrow // GROUP), axis=0
    )
    skip_here = lax.dynamic_slice_in_dim(mr_skip, chan_offset, narrow)
    gain_here = lax.dynamic_slice_in_dim(norm_gain, chan_offset, narrow)
    zero_rows = jnp.zeros((narrow, MR), jnp.bfloat16)
    mixed_rows = long_conv(
        product_rows, zero_rows, group_rows.astype(jnp.bfloat16), starts
    ) + skip_here[:, None] * product_rows.astype(jnp.float32)
    gated = gate_conv * mixed_rows
    shares = lax.psum_scatter(
        jnp.sum(gated * gated, axis=0).astype(jnp.bfloat16), "ctx", scatter_dimension=0, tiled=True
    ).astype(jnp.float32)
    own_scale = lax.rsqrt(row_total(shares) / D + NORM_EPS)
    row_scale = lax.all_gather(own_scale, "ctx", axis=0, tiled=True)
    return (gated * row_scale[None, :] * gain_here[:, None]).astype(jnp.bfloat16)


def solution(mesh):
    in_specs = (
        P("ch", "ctx"),
        P("ch", "ctx"),
        P("ch", "ctx"),
        P(None, None, "ch"),
        P("ch", None),
        P("ch"),
        P("ch"),
        P(),
    )
    out_specs = P(("ch", "ctx"), None)
    return jax.shard_map(local, mesh=mesh, in_specs=in_specs, out_specs=out_specs, check_vma=False)
```

profile of v0, /device:TPU:1, one launch (start us, length us, event | category | flops | bytes accessed | tf_op | source)
XLA Modules:
  0.0 279.0 jit_solution(16619326890867095155)
XLA Ops:
  0.0 0.0 copy-start
  0.0 2.2 pad_maximum_fusion
  2.2 4.7 %copy.30 = bf16[3,1024,512]{2,0,1:T(4,128)(2,1)} copy(bf16[3,1024,512]{2,1,0:T(8,128)(2,1)S(1)} %pad_maximum_fusion) | data formatting | bytes 6291456 | tf_op jit(solution)/shard_map/stack | solution.py:102
  6.9 0.0 copy-start.2
  6.9 8.8 %all-to-all-start = ((bf16[3,1024,512]{2,0,1:T(4,128)(2,1)}), bf16[3,1024,512]{2,0,1:T(4,128)(2,1)}, u32[]{:S(2)}, u32[]{:S(2)}) async-start(bf16[3,1024,512]{2,0,1:T(4,128)(2,1)} %copy.30), calls=%async_computation | async-start | bytes 8388608 | tf_op jit(solution)/shard_map/all_to_all | solution.py:103
  15.7 0.0 copy-start.3
  15.7 0.0 copy-done.2
  15.7 0.1 copy.29
  15.8 0.1 reduce-window.9
  15.9 0.1 reduce
  16.1 0.0 copy-done
  16.2 1.3 tile.10
  17.5 0.3 slice.128
  17.9 0.8 dynamic_slice.34
  18.7 0.8 dynamic_slice.35
  19.4 0.0 copy-done.3
  19.4 0.6 dynamic-slice
  20.6 0.9 fusion.34
  21.5 0.8 select_reduce_fusion
  22.3 45.5 %all-to-all-done = bf16[3,1024,512]{2,0,1:T(4,128)(2,1)} async-done(((bf16[3,1024,512]{2,0,1:T(4,128)(2,1)}), bf16[3,1024,512]{2,0,1:T(4,128)(2,1)}, u32[]{:S(2)}, u32[]{:S(2)}) %all-to-all-start) | async-done | bytes 3145760 | tf_op jit(solution)/shard_map/all_to_all | solution.py:103
  67.9 11.2 %fusion.39 = (bf16[1,32,32,512]{3,0,1,2:T(2,128)(2,1)}, bf16[1,32,32,512]{3,0,1,2:T(2,128)(2,1)S(1)}, bf16[1,32,32,512]{3,0,1,2:T(2,128)(2,1)S(1)}) fusion(bf16[3,32,32,512]{3,0,1,2:T(4,128)(2,1)} %bitcast.6), kind=kLoop, calls=%fused_computation.77 | loop fusion | bytes 6291456 | tf_op jit(solution)/shard_map/slice | solution.py:112
  79.0 1.1 copy.33
  80.1 0.6 copy.43
  80.7 1.1 copy.32
  81.9 0.6 copy.42
  82.4 0.7 pad_convert_fusion
  83.2 2.4 fusion.18
  85.6 0.1 concatenate.22
  85.7 0.5 reshape.144
  86.2 0.6 fusion.40
  86.8 0.3 pad_maximum_fusion.1
  87.1 1.6 broadcast_in_dim.159.clone
  88.7 15.0 %while.16 = (s32[]{:T(128)}, f32[2,16,128,128]{3,2,1,0:T(8,128)}, s32[128,128]{1,0:T(8,128)S(1)}, bf16[2,256,128]{2,1,0:T(8,128)(2,1)S(1)}, bf16[2,16,128,256]{3...) while((s32[]{:T(128)}, f32[2,16,128,128]{3,2,1,0:T(8,128)}, ...), condition=%wide.region_3.4_spmd.clone, body=%wide.region_2.3_spmd.clone.sunk | while | flops 70263112 | bytes 5491127 | solution.py:85
  88.7 0.1 broadcast_add_fusion.2
  88.8 1.4 broadcast_compare_fusion.2
  90.3 1.2 fusion.46
  91.5 1.0 copy_dynamic-update-slice_fusion.2
  92.5 0.1 broadcast_add_fusion.2
  92.5 1.4 broadcast_compare_fusion.2
  94.0 1.2 fusion.46
  95.2 1.0 copy_dynamic-update-slice_fusion.2
  96.2 0.1 broadcast_add_fusion.2
  96.3 1.4 broadcast_compare_fusion.2
  97.7 1.2 fusion.46
  98.9 1.0 copy_dynamic-update-slice_fusion.2
  100.0 0.1 broadcast_add_fusion.2
  100.0 1.4 broadcast_compare_fusion.2
  101.5 1.2 fusion.46
  102.7 1.0 copy_dynamic-update-slice_fusion.2
  103.7 2.7 copy.31
  106.4 0.6 copy.40
  107.0 0.0 copy-start.1
  107.0 0.3 pad_convert_fusion.2
  107.4 1.2 copy-done.1
  108.6 2.3 multiply_reduce_fusion
  110.9 120.1 %all-reduce.4 = bf16[16384]{0:T(1024)(128)(2,1)S(1)} all-reduce(bf16[16384]{0:T(1024)(128)(2,1)S(1)} %get-tuple-element.225), channel_id=2, replica_groups=mesh['ctx'=32,'ch'=8] {'ctx'}, use_global_device_ids=true, to_apply=%region_5.6.clone | all-reduce | flops 16384 | bytes 65536
  231.0 0.1 dynamic-slice_convert_fusion
  231.1 16.5 %psum.7 = f32[512]{0:T(512)S(1)} all-reduce(f32[512]{0:T(512)S(1)} %dynamic-slice_convert_fusion), channel_id=1, replica_groups=mesh['ctx'=32,'ch'=8] {'ch'}, use_global_device_ids=true, to_apply=%region_6.7 | all-reduce | flops 512 | bytes 4096 | tf_op jit(solution)/shard_map/psum | solution.py:95
  247.6 30.2 %all-gather = f32[32,1,512]{2,1,0:T(1,128)S(1)} all-gather(f32[1,1,512]{2,1,0:T(1,128)S(1)} %bitcast.69), channel_id=1, replica_groups=mesh['ctx'=32,'ch'=8] {'ctx'}, dimensions={0}, use_global_device_ids=true | all-gather | bytes 67584 | tf_op jit(solution)/shard_map/all_gather | solution.py:132
  277.8 1.2 multiply_convert_fusion
  (28 shorter events, 0.4 us)
Async XLA Ops:
  0.0 16.1 %copy-start = (f32[64,128]{1,0:T(8,128)S(1)}, f32[64,128]{1,0:T(8,128)}, u32[]{:S(2)}) copy-start(f32[64,128]{1,0:T(8,128)} %param.14) | copy-start | bytes 98308
  6.9 8.8 %copy-start.2 = (s32[64]{0:T(128)S(1)}, s32[64]{0:T(128)}, u32[]{:S(2)}) copy-start(s32[64]{0:T(128)} %param.17) | copy-start | bytes 772
  6.9 61.0 %all-to-all-start = ((bf16[3,1024,512]{2,0,1:T(4,128)(2,1)}), bf16[3,1024,512]{2,0,1:T(4,128)(2,1)}, u32[]{:S(2)}, u32[]{:S(2)}) async-start(bf16[3,1024,512]{2,0,1:T(4,128)(2,1)} %copy.30), calls=%async_computation | async-start | bytes 8388608 | tf_op jit(solution)/shard_map/all_to_all | solution.py:103
  15.7 3.7 %copy-start.3 = (u32[256]{0:T(256)S(1)}, u32[256]{0:T(256)}, u32[]{:S(2)}) copy-start(u32[256]{0:T(256)} %constant.121) | copy-start | bytes 3076
  107.0 1.6 copy-start.1
where the time goes:
time: 279 us
  blocking collectives  167 us (60%)
  waiting for transfers between devices  45.5 us (16%)
  local copies, waits for them, and re-layouts  35.5 us (13%)
  other arithmetic  16.6 us (6%)
  starting transfers between devices  8.79 us (3%)
  matrix products  4.89 us (2%)
    unnamed x1, blocking collectives  120 us
    all_to_all x1, waiting for transfers between devices, local(): lax.all_to_all(stacked, 'ctx', split_axis=1, concat_axis=2, tiled=True)  45.5 us
    all_gather x1, blocking collectives, local(): row_scale = lax.all_gather(own_scale, 'ctx', axis=0, tiled=True)  30.2 us
    psum x1, blocking collectives, row_total(): return lax.psum(partial_value, 'ch')  16.5 us
    slice x2, local copies, waits for them, and re-layouts, local(): received[0]  13.9 us
    all_to_all x1, starting transfers between devices, local(): lax.all_to_all(stacked, 'ctx', split_axis=1, concat_axis=2, tiled=True)  8.79 us
  transfers between devices with their start and end apart: 1, of which 1 were waited for; matrix products, arithmetic and copies ran while one was open for 2% of the time, Pallas kernels for 0%

commit v1 on v0

v1 whole, which is shorter than its diff:
```python
import functools
import math
import jax
import jax.numpy as jnp
from jax import lax
from jax.experimental import pallas as pl
from jax.experimental.pallas import tpu as pltpu
from jax.sharding import PartitionSpec as P

D = 8192
GROUP = 16
MR = 128
EPS = 1e-6
DOCS = 64
F32 = jnp.float32
BF = jnp.bfloat16
CB = 128


def starts_row(docs_ref, base, count):
    pos = lax.broadcasted_iota(jnp.int32, (1, count), 1) + base
    first = jnp.int32(0)
    start = jnp.zeros((1, count), jnp.int32)
    for d in range(DOCS):
        start = jnp.where(pos >= first, first, start)
        first = first + docs_ref[d]
    return pos, start


def columns(sf_ref, skip_ref, gain_ref):
    rows = [sf_ref[0], sf_ref[1], sf_ref[2], skip_ref[...], gain_ref[...],
            jnp.zeros((5, CB), F32)]
    return jnp.concatenate(rows, axis=0).T


def conv3(cur, prev, cols, first, keep1, keep2):
    w = cur.shape[1]
    ext = jnp.concatenate([prev, cur], axis=1)
    one = pltpu.roll(ext, 1, 1)[:, 128:]
    two = pltpu.roll(ext, 2, 1)[:, 128:]
    t0 = cols[:, first:first + 1]
    t1 = cols[:, first + 1:first + 2]
    t2 = cols[:, first + 2:first + 3]
    return t0 * cur + jnp.where(keep1, t1 * one, 0.0) + jnp.where(keep2, t2 * two, 0.0)


def tail_kernel(docs_ref, base_ref, gate_ref, key_ref, value_ref, sf_ref, skip_ref, gain_ref, out_ref):
    base = base_ref[0] + 384
    pos, start = starts_row(docs_ref, base, 128)
    keep1 = jnp.broadcast_to(pos - 1 >= start, (CB, 128))
    keep2 = jnp.broadcast_to(pos - 2 >= start, (CB, 128))
    cols = columns(sf_ref, skip_ref, gain_ref)
    key = key_ref[...].astype(F32)
    value = value_ref[...].astype(F32)
    gate = gate_ref[...].astype(F32)
    kc = conv3(key[:, 128:], key[:, :128], cols, 3, keep1, keep2)
    vc = conv3(value[:, 128:], value[:, :128], cols, 6, keep1, keep2)
    out_ref[:, :128] = (kc * vc).astype(BF)
    lane = lax.broadcasted_iota(jnp.int32, (CB, 128), 1)
    packed = jnp.where(lane >= 126, gate[:, 128:],
                       jnp.where(lane >= 124, pltpu.roll(key[:, 128:], 126, 1),
                                 pltpu.roll(value[:, 128:], 124, 1)))
    out_ref[:, 128:] = packed.astype(BF)


def main_kernel(docs_ref, base_ref, gate_ref, key_ref, value_ref, halo_ref, sf_ref, skip_ref,
                gain_ref, taps_ref, out_ref, sq_ref, masks, prod, mixed):
    n = gate_ref.shape[1]
    tiles = n // 128
    base = base_ref[0]
    pos, start = starts_row(docs_ref, base, n)

    @pl.when(pl.program_id(0) == 0)
    def _():
        s = lax.broadcasted_iota(jnp.int32, (128, 128), 0)
        t = lax.broadcasted_iota(jnp.int32, (128, 128), 1)
        for j in range(tiles):
            first = jnp.broadcast_to(start[:, 128 * j:128 * (j + 1)] - (base + 128 * j), (128, 128))
            prev = (s > t) & (s - 128 >= first)
            here = (s <= t) & (s >= first)
            masks[j, :128, :] = prev.astype(F32).astype(BF)
            masks[j, 128:, :] = here.astype(F32).astype(BF)
        sq_ref[...] = jnp.zeros_like(sq_ref)

    keep1 = jnp.broadcast_to(pos - 1 >= start, (CB, n))
    keep2 = jnp.broadcast_to(pos - 2 >= start, (CB, n))
    cols = columns(sf_ref, skip_ref, gain_ref)
    packed = halo_ref[:, 128:].astype(F32)
    kc = conv3(key_ref[...].astype(F32), pltpu.roll(packed, 2, 1), cols, 3, keep1, keep2)
    vc = conv3(value_ref[...].astype(F32), pltpu.roll(packed, 4, 1), cols, 6, keep1, keep2)
    prod[:, :128] = halo_ref[:, :128]
    prod[:, 128:] = (kc * vc).astype(BF)

    taps = taps_ref[...].astype(BF).astype(F32)
    for g in range(CB // GROUP):
        ring = pltpu.roll(jnp.broadcast_to(taps[g:g + 1], (128, 128)), 0, 1, stride=1, stride_axis=0).astype(BF)
        both = jnp.concatenate([ring, ring], axis=0)
        for j in range(tiles):
            mixed[GROUP * g:GROUP * (g + 1), 128 * j:128 * (j + 1)] = jnp.dot(
                prod[GROUP * g:GROUP * (g + 1), 128 * j:128 * j + 256], both * masks[j],
                preferred_element_type=F32)

    gc = conv3(gate_ref[...].astype(F32), packed, cols, 0, keep1, keep2)
    gated = gc * (mixed[...] + cols[:, 9:10] * prod[:, 128:].astype(F32))
    sq = gated * gated
    acc = sq[:8]
    for i in range(1, CB // 8):
        acc = acc + sq[8 * i:8 * i + 8]
    sq_ref[...] += acc
    out_ref[...] = (gated * cols[:, 10:11]).astype(BF)


def param_specs():
    return [
        pl.BlockSpec((3, 3, CB), lambda i: (0, 0, i)),
        pl.BlockSpec((1, CB), lambda i: (0, i)),
        pl.BlockSpec((1, CB), lambda i: (0, i)),
    ]

SMEM = pl.BlockSpec(memory_space=pltpu.SMEM)

def tail(docs, base, gate, key, value, sf, skip, gain):
    ch, n = gate.shape
    wide = pl.BlockSpec((CB, 256), lambda i: (i, n // 256 - 1))
    return pl.pallas_call(
        tail_kernel, grid=(ch // CB,),
        in_specs=[SMEM, SMEM, wide, wide, wide] + param_specs(),
        out_specs=pl.BlockSpec((CB, 256), lambda i: (i, 0)),
        out_shape=jax.ShapeDtypeStruct((ch, 256), BF), name="tail",
    )(docs, base, gate, key, value, sf, skip, gain)


def main(docs, base, gate, key, value, halo, sf, skip, gain, taps):
    ch, n = gate.shape
    wide = pl.BlockSpec((CB, n), lambda i: (i, 0))
    return pl.pallas_call(
        main_kernel, grid=(ch // CB,),
        in_specs=[SMEM, SMEM, wide, wide, wide, pl.BlockSpec((CB, 256), lambda i: (i, 0))] + param_specs()
        + [pl.BlockSpec((CB // GROUP, MR), lambda i: (i, 0))],
        out_specs=[wide, pl.BlockSpec((8, n), lambda i: (0, 0))],
        out_shape=[jax.ShapeDtypeStruct((ch, n), BF), jax.ShapeDtypeStruct((8, n), F32)],
        scratch_shapes=[pltpu.VMEM((n // 128, 256, 128), BF), pltpu.VMEM((CB, n + 128), BF), pltpu.VMEM((CB, n), F32)],
        compiler_params=pltpu.CompilerParams(vmem_limit_bytes=48 << 20), name="mixer",
    )(docs, base, gate, key, value, halo, sf, skip, gain, taps)


def final_kernel(recv_ref, sums_ref, out_ref):
    per = recv_ref.shape[0]
    n = recv_ref.shape[2]
    for i in range(per):
        scale = lax.rsqrt(sums_ref[i] / D + EPS)
        out_ref[:, n * i:n * (i + 1)] = (recv_ref[i].astype(F32) * scale).astype(BF)


def final(recv, sums, per=8):
    k, c, n = recv.shape
    return pl.pallas_call(
        final_kernel, grid=(k // per,),
        in_specs=[pl.BlockSpec((per, c, n), lambda i: (i, 0, 0)), pl.BlockSpec((per, 1, n), lambda i: (i, 0, 0))],
        out_specs=pl.BlockSpec((c, per * n), lambda i: (0, i)),
        out_shape=jax.ShapeDtypeStruct((c, k * n), BF), name="settle",
    )(recv, sums)


def local(gate, key, value, sf, taps, skip, gain, docs):
    place = lax.axis_index("ctx")
    width = lax.axis_size("ctx")
    ch, n = gate.shape
    base = (place * n).astype(jnp.int32).reshape(1)
    skip, gain = skip.reshape(1, ch), gain.reshape(1, ch)
    ends = tail(docs, base, gate, key, value, sf, skip, gain)
    halo = lax.ppermute(ends, "ctx", [(i, i + 1) for i in range(width - 1)])
    rows, squares = main(docs, base, gate, key, value, halo, sf, skip, gain, taps)
    recv = lax.all_to_all(rows.reshape(width, ch // width, n), "ctx", split_axis=0, concat_axis=0, tiled=True)
    total = lax.psum(jnp.sum(squares, axis=0, keepdims=True), "ch")
    sums = lax.all_to_all(jnp.broadcast_to(total[None], (width, 1, n)), "ctx", split_axis=0, concat_axis=0, tiled=True)
    return final(recv, sums)


def solution(mesh):
    in_specs = (P("ch", "ctx"),) * 3 + (P(None, None, "ch"), P("ch", None), P("ch"), P("ch"), P())
    return jax.shard_map(local, mesh=mesh, in_specs=in_specs, out_specs=P(("ch", "ctx"), None), check_vma=False)
```

time: 279 us -> 90.6 us (0.32)
  blocking collectives: 167 us -> 57.2 us
  waiting for transfers between devices: 45.5 us -> 6.42 us
  local copies, waits for them, and re-layouts: 35.5 us -> 1.04 us
  Pallas kernels: 0 us -> 20.6 us
  other arithmetic: 16.6 us -> 0.02 us
  matrix products: 4.89 us -> 0 us
  starting transfers between devices: 8.79 us -> 4.58 us
    unnamed x1 -> x0, blocking collectives: 120 us -> none
    all_to_all x1 -> x0, waiting for transfers between devices: 45.5 us -> none  [local(): lax.all_to_all(stacked, 'ctx', split_axis=1, concat_axis=2, tiled=True)]
    all_to_all x0 -> x2, blocking collectives: none -> 41 us  [the longest x1 21.7 us: local(): lax.all_to_all(rows.reshape(width, ch // width, n), 'ctx', split_axis=0,...]
    all_gather x1 -> x0, blocking collectives: 30.2 us -> none  [local(): row_scale = lax.all_gather(own_scale, 'ctx', axis=0, tiled=True)]
    pallas_call x0 -> x3, Pallas kernels: none -> 20.6 us  [the longest x1 10.5 us: main(): pl.pallas_call(main_kernel, grid=(ch // CB,), in_specs=[SMEM, SMEM, wide,...]
    slice x7 -> x0, local copies, waits for them, and re-layouts: 17 us -> none  [the longest x2 13.9 us: local(): received[0]]
    all_to_all x1 -> x0, starting transfers between devices: 8.79 us -> none  [local(): lax.all_to_all(stacked, 'ctx', split_axis=1, concat_axis=2, tiled=True)]
    ppermute x0 -> x1, waiting for transfers between devices: none -> 6.42 us  [local(): halo = lax.ppermute(ends, 'ctx', [(i, i + 1) for i in range(width - 1)])]
  transfers between devices with their start and end apart: 1 -> 1, of which waited for: 1 -> 1; matrix products, arithmetic and copies ran while one was open for 2% -> 0% of each run, Pallas kernels for 0% -> 0%
where the time goes in v1:
time: 90.6 us; the launch traced here: 90 us
  blocking collectives  57.2 us (63%)
  Pallas kernels  20.6 us (23%)
  waiting for transfers between devices  6.42 us (7%)
  starting transfers between devices  4.58 us (5%)
  local copies, waits for them, and re-layouts  1.04 us (1%)
    all_to_all x1, blocking collectives, local(): lax.all_to_all(rows.reshape(width, ch // width, n), 'ctx', split_axis=0,...  21.7 us
    all_to_all x1, blocking collectives, local(): lax.all_to_all(jnp.broadcast_to(total[None], (width, 1, n)), 'ctx', split...  19.3 us
    psum x1, blocking collectives, local(): total = lax.psum(jnp.sum(squares, axis=0, keepdims=True), 'ch')  16.2 us
    pallas_call x1, Pallas kernels, main(): pl.pallas_call(main_kernel, grid=(ch // CB,), in_specs=[SMEM, SMEM, wide,...  10.5 us
    pallas_call x1, Pallas kernels, tail(): pl.pallas_call(tail_kernel, grid=(ch // CB,), in_specs=[SMEM, SMEM, wide,...  6.65 us
    ppermute x1, waiting for transfers between devices, local(): halo = lax.ppermute(ends, 'ctx', [(i, i + 1) for i in range(width - 1)])  6.42 us
    ppermute x1, starting transfers between devices, local(): halo = lax.ppermute(ends, 'ctx', [(i, i + 1) for i in range(width - 1)])  4.58 us
    pallas_call x1, Pallas kernels, final(): pl.pallas_call(final_kernel, grid=(k // per,), in_specs=[pl.BlockSpec((pe...  3.45 us
  transfers between devices with their start and end apart: 1, of which 1 were waited for; matrix products, arithmetic and copies ran while one was open for 0% of the time, Pallas kernels for 0%

profile of v1, /device:TPU:1, one launch (start us, length us, event | category | flops | bytes accessed | tf_op | source)
XLA Modules:
  0.0 90.0 jit_solution(10412859177599121809)
XLA Ops:
  0.0 0.0 copy-start
  0.0 0.0 copy-start.1
  0.0 0.0 copy-start.2
  0.0 0.0 copy-start.4
  0.0 0.0 copy-start.5
  0.0 0.0 copy-start.6
  0.0 0.0 copy-start.7
  0.0 0.0 copy-start.8
  0.1 6.7 %tail.1 = bf16[1024,256]{1,0:T(8,128)(2,1)} custom-call(s32[64]{0:T(128)} %docs_ref.3, s32[1]{0:T(128)} %bitcast.base_ref, bf16[1024,512]{1,0:T(8,128)(2,1)} %gate_ref.3, bf16[1024,512]{1,0:T(8,128)(2,1)} %key_ref.3, bf16[1024,512]{1,0:T(8,128)(2,1)} %value_ref.3, f32[3,3,1024]{2,1,0:T(4,128)} %sf_ref.3, f32[1,1024]{1,0:T(1,128)} %bitcast.5, f32[1,1024]{1,0:T(1,128)} %bitcast.7), custom_call_target="tpu_custom_call" | custom-call | tf_op jit(solution)/shard_map/tail/pallas_call | solution.py:125
  6.7 4.6 %collective-permute-start = (bf16[1024,256]{1,0:T(8,128)(2,1)}, bf16[1024,256]{1,0:T(8,128)(2,1)S(1)}, u32[]{:S(2)}, u32[]{:S(2)}) collective-permute-start(bf16[1024,256]{1,0:T(8,128)(2,1)} %tail.1), channel_id=1, source_target_pairs={{0,8},{8,16},{16,24},{24,32},{32,40},{40,48},{48,56},{56,64},{64,7... | collective-permute-start | bytes 1572872 | tf_op jit(solution)/shard_map/ppermute | solution.py:172
  11.3 6.4 %collective-permute-done.halo_ref = bf16[1024,256]{1,0:T(8,128)(2,1)S(1)} collective-permute-done((bf16[1024,256]{1,0:T(8,128)(2,1)}, bf16[1024,256]{1,0:T(8,128)(2,1)S(1)}, u32[]{:S(2)}, u32[]{:S(2)}) %collective-permute-start) | collective-permute-done | bytes 524320 | tf_op jit(solution)/shard_map/ppermute | solution.py:172
  17.7 0.0 copy-done
  17.7 0.0 copy-done.1
  17.7 0.0 copy-done.2
  17.7 0.0 copy-done.4
  17.7 0.0 copy-done.5
  17.7 0.0 copy-done.6
  17.8 0.0 copy-done.7
  17.8 0.0 copy-done.8
  17.8 10.5 %mixer.1 = (bf16[1024,512]{1,0:T(8,128)(2,1)S(1)}, f32[8,512]{1,0:T(8,128)S(1)}) custom-call(s32[64]{0:T(128)S(1)} %copy-done.8, s32[1]{0:T(128)} %bitcast.base_ref, bf16[1024,512]{1,0:T(8,128)(2,1)S(1)} %copy-done, bf16[1024,512]{1,0:T(8,128)(2,1)S(1)} %copy-done.1, bf16[1024,512]{1,0:T(8,128)(2,1)S(1)} %copy-done.2, ...), custom_call_target="tpu_custom_call" | custom-call | tf_op jit(solution)/shard_map/mixer/pallas_call | solution.py:136
  28.2 0.0 copy-start.3
  28.2 1.0 %copy-done.3 = bf16[1024,512]{1,0:T(8,128)(2,1)} copy-done((bf16[1024,512]{1,0:T(8,128)(2,1)}, bf16[1024,512]{1,0:T(8,128)(2,1)S(1)}, u32[]{:S(2)}) %copy-start.3) | copy-done | bytes 1048600
  29.2 16.2 %psum.7 = f32[512]{0:T(512)S(1)} all-reduce(f32[512]{0:T(512)S(1)} %reduce_sum.9), channel_id=1, replica_groups=mesh['ctx'=32,'ch'=8] {'ch'}, use_global_device_ids=true, to_apply=%region_1.0 | all-reduce | flops 512 | bytes 4096 | tf_op jit(solution)/shard_map/psum | solution.py:175
  45.5 19.3 %all_to_all.10.sums_ref = f32[32,1,512]{2,1,0:T(1,128)} all-to-all(f32[32,1,512]{2,1,0:T(1,128)S(1)} %broadcast_in_dim.13), channel_id=1, replica_groups=mesh['ctx'=32,'ch'=8] {'ctx'}, dimensions={0} | all-to-all | bytes 131072 | tf_op jit(solution)/shard_map/all_to_all | solution.py:176
  64.8 21.7 %all_to_all.11.recv_ref = bf16[32,32,512]{2,1,0:T(8,128)(2,1)} all-to-all(bf16[32,32,512]{2,1,0:T(8,128)(2,1)} %bitcast.4), channel_id=1, replica_groups=mesh['ctx'=32,'ch'=8] {'ctx'}, dimensions={0} | all-to-all | bytes 2097152 | tf_op jit(solution)/shard_map/all_to_all | solution.py:174
  86.5 3.5 %settle.1 = bf16[32,16384]{1,0:T(8,128)(2,1)} custom-call(bf16[32,32,512]{2,1,0:T(8,128)(2,1)} %all_to_all.11.recv_ref, f32[32,1,512]{2,1,0:T(1,128)} %all_to_all.10.sums_ref), custom_call_target="tpu_custom_call" | custom-call | tf_op jit(solution)/shard_map/settle/pallas_call | solution.py:157
  (2 shorter events, 0.1 us)
Async XLA Ops:
  0.0 17.7 %copy-start = (bf16[1024,512]{1,0:T(8,128)(2,1)S(1)}, bf16[1024,512]{1,0:T(8,128)(2,1)}, u32[]{:S(2)}) copy-start(bf16[1024,512]{1,0:T(8,128)(2,1)} %gate_ref.3) | copy-start | bytes 3145732
  0.0 17.7 %copy-start.1 = (bf16[1024,512]{1,0:T(8,128)(2,1)S(1)}, bf16[1024,512]{1,0:T(8,128)(2,1)}, u32[]{:S(2)}) copy-start(bf16[1024,512]{1,0:T(8,128)(2,1)} %key_ref.3) | copy-start | bytes 3145732
  0.0 17.7 %copy-start.2 = (bf16[1024,512]{1,0:T(8,128)(2,1)S(1)}, bf16[1024,512]{1,0:T(8,128)(2,1)}, u32[]{:S(2)}) copy-start(bf16[1024,512]{1,0:T(8,128)(2,1)} %value_ref.3) | copy-start | bytes 3145732
  0.0 17.7 %copy-start.4 = (f32[3,3,1024]{2,1,0:T(4,128)S(1)}, f32[3,3,1024]{2,1,0:T(4,128)}, u32[]{:S(2)}) copy-start(f32[3,3,1024]{2,1,0:T(4,128)} %sf_ref.3) | copy-start | bytes 110596
  0.0 17.7 %copy-start.5 = (f32[64,128]{1,0:T(8,128)S(1)}, f32[64,128]{1,0:T(8,128)}, u32[]{:S(2)}) copy-start(f32[64,128]{1,0:T(8,128)} %taps_ref.1) | copy-start | bytes 98308
  0.0 17.7 %copy-start.6 = (f32[1024]{0:T(1024)S(1)}, f32[1024]{0:T(1024)}, u32[]{:S(2)}) copy-start(f32[1024]{0:T(1024)} %param.13) | copy-start | bytes 12292
  0.0 17.7 %copy-start.7 = (f32[1024]{0:T(1024)S(1)}, f32[1024]{0:T(1024)}, u32[]{:S(2)}) copy-start(f32[1024]{0:T(1024)} %param.14) | copy-start | bytes 12292
  0.0 17.7 %copy-start.8 = (s32[64]{0:T(128)S(1)}, s32[64]{0:T(128)}, u32[]{:S(2)}) copy-start(s32[64]{0:T(128)} %docs_ref.3) | copy-start | bytes 772
  6.7 11.0 %collective-permute-start = (bf16[1024,256]{1,0:T(8,128)(2,1)}, bf16[1024,256]{1,0:T(8,128)(2,1)S(1)}, u32[]{:S(2)}, u32[]{:S(2)}) collective-permute-start(bf16[1024,256]{1,0:T(8,128)(2,1)} %tail.1), channel_id=1, source_target_pairs={{0,8},{8,16},{16,24},{24,32},{32,40},{40,48},{48,56},{56,64},{64,7... | collective-permute-start | bytes 1572872 | tf_op jit(solution)/shard_map/ppermute | solution.py:172
  28.2 1.0 %copy-start.3 = (bf16[1024,512]{1,0:T(8,128)(2,1)}, bf16[1024,512]{1,0:T(8,128)(2,1)S(1)}, u32[]{:S(2)}) copy-start(bf16[1024,512]{1,0:T(8,128)(2,1)S(1)} %get-tuple-element.7) | copy-start | bytes 3145732

commit v2 on v1

v2 whole, which is shorter than its diff:
```python
import functools

import jax
import jax.numpy as jnp
from jax import lax
from jax.experimental import pallas as pl
from jax.experimental.pallas import tpu as pltpu
from jax.sharding import PartitionSpec as P

D = 8192
GROUP = 16
MR = 128
EPS = 1e-6
DOCS = 64
F32 = jnp.float32
BF = jnp.bfloat16
CB = 128
ENDS = 144
SMEM = pl.BlockSpec(memory_space=pltpu.SMEM)


def starts_row(docs_ref, base, count):
    pos = lax.broadcasted_iota(jnp.int32, (1, count), 1) + base
    first = jnp.int32(0)
    start = jnp.zeros((1, count), jnp.int32)
    for d in range(DOCS):
        start = jnp.where(pos >= first, first, start)
        first = first + docs_ref[d]
    return pos, start


def set_keeps(keeps, pos, start):
    n = pos.shape[1]
    for lag in (1, 2):
        keeps[lag - 1] = jnp.broadcast_to((pos - lag >= start).astype(F32), (8, n))


def columns(sf, skip, gain):
    rows = [sf[0], sf[1], sf[2], skip, gain, jnp.zeros((5, CB), F32)]
    return jnp.concatenate(rows, axis=0).T


def conv3(ext, cols, first, keep):
    w = ext.shape[1] - 128
    one = pltpu.roll(ext, 1, 1)[:, 128:].reshape(CB // 8, 8, w) * keep[0][None]
    two = pltpu.roll(ext, 2, 1)[:, 128:].reshape(CB // 8, 8, w) * keep[1][None]
    return (cols[:, first:first + 1] * ext[:, 128:]
            + cols[:, first + 1:first + 2] * one.reshape(CB, w)
            + cols[:, first + 2:first + 3] * two.reshape(CB, w))


def tail_kernel(docs_ref, base_ref, gate_ref, key_ref, value_ref, sf_ref, out_ref, keeps):
    @pl.when(pl.program_id(0) == 0)
    def _():
        set_keeps(keeps, *starts_row(docs_ref, base_ref[0] + 384, 128))

    row = lax.broadcasted_iota(jnp.int32, (16, 128), 0)
    lane = lax.broadcasted_iota(jnp.int32, (16, 128), 1)
    for b in range(gate_ref.shape[0] // CB):
        here = slice(CB * b, CB * (b + 1))
        none = jnp.zeros((1, CB), F32)
        cols = columns(sf_ref[:, :, here], none, none)
        kc = conv3(key_ref[here].astype(F32), cols, 3, keeps)
        vc = conv3(value_ref[here].astype(F32), cols, 6, keeps)
        out_ref[b, :CB] = (kc * vc).astype(BF)
        raw = jnp.zeros((16, CB), F32)
        for i, ref in enumerate((gate_ref, key_ref, value_ref)):
            pick = ((lane == 126 + row - 2 * i) & (row >= 2 * i) & (row < 2 * i + 2)).astype(F32).astype(BF)
            raw = raw + lax.dot_general(pick, ref[here, 128:], (((1,), (1,)), ((), ())), preferred_element_type=F32)
        out_ref[b, CB:] = raw.astype(BF)


def main_kernel(later, docs_ref, base_ref, gate_ref, key_ref, value_ref, *refs):
    if later:
        sf_ref, skip_ref, gain_ref, taps_ref, out_ref, sq_ref, masks, keeps, prod, mixed, acc = refs
    else:
        (halo_ref, sq_later, _, sf_ref, skip_ref, gain_ref, taps_ref, out_ref, sq_ref,
         masks, keeps, prod, mixed, acc) = refs
    at = 256 if later else 0
    n = 256
    step = pl.program_id(0)

    @pl.when(step == 0)
    def _():
        base = base_ref[0] + at
        pos, start = starts_row(docs_ref, base - 128, n + 128)
        set_keeps(keeps, pos, start)
        s = lax.broadcasted_iota(jnp.int32, (128, 128), 0)
        t = lax.broadcasted_iota(jnp.int32, (128, 128), 1)
        for j in range(2):
            first = jnp.broadcast_to(start[:, 128 * (j + 1):128 * (j + 2)] - (base + 128 * j), (128, 128))
            masks[j, :128, :] = ((s > t) & (s - 128 >= first)).astype(F32).astype(BF)
            masks[j, 128:, :] = ((s <= t) & (s >= first)).astype(F32).astype(BF)
        acc[...] = jnp.zeros_like(acc)

    cols = columns(sf_ref[...], skip_ref[...], gain_ref[...])
    if later:
        kc = conv3(key_ref[...].astype(F32), cols, 3, keeps)
        vc = conv3(value_ref[...].astype(F32), cols, 6, keeps)
        prod[...] = (kc * vc).astype(BF)
        gate = gate_ref[:, 128:].astype(F32)
    else:
        row = lax.broadcasted_iota(jnp.int32, (16, 128), 0)
        lane = lax.broadcasted_iota(jnp.int32, (16, 128), 1)

        def before(i):
            put = ((lane == 126 + row - 2 * i) & (row >= 2 * i) & (row < 2 * i + 2)).astype(F32).astype(BF)
            return lax.dot_general(halo_ref[0, CB:], put, (((0,), (0,)), ((), ())), preferred_element_type=F32)

        keep = keeps[:, :, 128:]
        kc = conv3(jnp.concatenate([before(1), key_ref[...].astype(F32)], axis=1), cols, 3, keep)
        vc = conv3(jnp.concatenate([before(2), value_ref[...].astype(F32)], axis=1), cols, 6, keep)
        prod[:, :128] = halo_ref[0, :CB]
        prod[:, 128:] = (kc * vc).astype(BF)
        gate = jnp.concatenate([before(0), gate_ref[...].astype(F32)], axis=1)

    taps = taps_ref[...].astype(BF).astype(F32)
    for g in range(CB // GROUP):
        ring = pltpu.roll(jnp.broadcast_to(taps[g:g + 1], (128, 128)), 0, 1, stride=1, stride_axis=0).astype(BF)
        both = jnp.concatenate([ring, ring], axis=0)
        for j in range(2):
            mixed[GROUP * g:GROUP * (g + 1), 128 * j:128 * (j + 1)] = jnp.dot(
                prod[GROUP * g:GROUP * (g + 1), 128 * j:128 * j + 256], both * masks[j],
                preferred_element_type=F32)

    gc = conv3(gate, cols, 0, keeps[:, :, 128:])
    gated = gc * (mixed[...] + cols[:, 9:10] * prod[:, 128:].astype(F32))
    acc[...] += jnp.sum((gated * gated).reshape(CB // 8, 8, n), axis=0)
    out_ref[...] = (gated * cols[:, 10:11]).astype(BF)

    @pl.when(step == pl.num_programs(0) - 1)
    def _():
        row = jnp.sum(acc[...], axis=0, keepdims=True)
        sq_ref[...] = row if later else jnp.concatenate([row, sq_later[...]], axis=1)


def sf_spec(c):
    return pl.BlockSpec((3, 3, c), lambda i: (0, 0, i))


def tail(docs, base, gate, key, value, sf):
    ch, n = gate.shape
    c = min(512, ch)
    wide = pl.BlockSpec((c, 256), lambda i: (i, n // 256 - 1))
    return pl.pallas_call(
        tail_kernel, grid=(ch // c,),
        in_specs=[SMEM, SMEM, wide, wide, wide, sf_spec(c)],
        out_specs=pl.BlockSpec((c // CB, ENDS, 128), lambda i: (i, 0, 0)),
        out_shape=jax.ShapeDtypeStruct((ch // CB, ENDS, 128), BF),
        scratch_shapes=[pltpu.VMEM((2, 8, 128), F32)],
        compiler_params=pltpu.CompilerParams(vmem_limit_bytes=32 << 20), name="tail",
    )(docs, base, gate, key, value, sf)


def mixer(docs, base, gate, key, value, halo, earlier, sf, skip, gain, taps):
    ch, n = gate.shape
    later = halo is None
    row = pl.BlockSpec((1, CB), lambda i: (0, i))
    half = pl.BlockSpec((CB, 256), lambda i: (i, 0))
    raw = pl.BlockSpec((CB, n), lambda i: (i, 0)) if later else half
    extra, specs, alias = (), [], {}
    if not later:
        extra = (halo, earlier[1], earlier[0])
        specs = [pl.BlockSpec((1, ENDS, 128), lambda i: (i, 0, 0)), pl.BlockSpec((1, 256), lambda i: (0, 0)),
                 pl.BlockSpec(memory_space=pl.ANY)]
        alias = {7: 0}
    sq = 256 if later else 512
    return pl.pallas_call(
        functools.partial(main_kernel, later), grid=(ch // CB,),
        in_specs=[SMEM, SMEM, raw, raw, raw] + specs
        + [sf_spec(CB), row, row, pl.BlockSpec((CB // GROUP, MR), lambda i: (i, 0))],
        out_specs=[pl.BlockSpec((CB, 256), lambda i: (i, 1 if later else 0)), pl.BlockSpec((1, sq), lambda i: (0, 0))],
        out_shape=[jax.ShapeDtypeStruct((ch, n), BF), jax.ShapeDtypeStruct((1, sq), F32)],
        scratch_shapes=[pltpu.VMEM((2, 256, 128), BF), pltpu.VMEM((2, 8, 384), F32), pltpu.VMEM((CB, 384), BF),
                        pltpu.VMEM((CB, 256), F32), pltpu.VMEM((8, 256), F32)],
        input_output_aliases=alias,
        cost_estimate=pl.CostEstimate(flops=2 * ch * 256 * 256 * 8, bytes_accessed=6 * ch * 256, transcendentals=0),
        compiler_params=pltpu.CompilerParams(vmem_limit_bytes=32 << 20), name="later" if later else "first",
    )(docs, base, gate, key, value, *extra, sf, skip, gain, taps)


def final_kernel(recv_ref, sums_ref, out_ref):
    per, _, n = recv_ref.shape
    for i in range(per):
        scale = lax.rsqrt(sums_ref[i] / D + EPS)
        out_ref[:, n * i:n * (i + 1)] = (recv_ref[i].astype(F32) * scale).astype(BF)


def final(recv, sums):
    k, c, n = recv.shape
    per = min(k, 8)
    return pl.pallas_call(
        final_kernel, grid=(k // per,),
        in_specs=[pl.BlockSpec((per, c, n), lambda i: (i, 0, 0)), pl.BlockSpec((per, 1, n), lambda i: (i, 0, 0))],
        out_specs=pl.BlockSpec((c, per * n), lambda i: (0, i)),
        out_shape=jax.ShapeDtypeStruct((c, k * n), BF), name="settle",
    )(recv, sums)


def local(gate, key, value, sf, taps, skip, gain, docs):
    place = lax.axis_index("ctx")
    width = lax.axis_size("ctx")
    ch, n = gate.shape
    base = (place * n).astype(jnp.int32).reshape(1)
    skip, gain = skip.reshape(1, ch), gain.reshape(1, ch)
    ends = tail(docs, base, gate, key, value, sf)
    halo = lax.ppermute(ends, "ctx", [(i, i + 1) for i in range(width - 1)])
    later = mixer(docs, base, gate, key, value, None, None, sf, skip, gain, taps)
    rows, squares = mixer(docs, base, gate, key, value, halo, later, sf, skip, gain, taps)
    recv = lax.all_to_all(rows.reshape(width, ch // width, n), "ctx", split_axis=0, concat_axis=0, tiled=True)
    total = lax.psum(squares, "ch")
    total, recv = lax.optimization_barrier((total, recv))
    sums = lax.all_to_all(jnp.broadcast_to(total[None], (width, 1, n)), "ctx", split_axis=0, concat_axis=0, tiled=True)
    return final(recv, sums)


def solution(mesh):
    in_specs = (P("ch", "ctx"),) * 3 + (P(None, None, "ch"), P("ch", None), P("ch"), P("ch"), P())
    return jax.shard_map(local, mesh=mesh, in_specs=in_specs, out_specs=P(("ch", "ctx"), None), check_vma=False)
```

time: 90.6 us -> 73.3 us (0.81)
  blocking collectives: 57.2 us -> 34.7 us
  starting transfers between devices: 4.58 us -> 11.5 us
  waiting for transfers between devices: 6.42 us -> 0.01 us
  local copies, waits for them, and re-layouts: 1.04 us -> 5.17 us
    all_to_all x1 -> x0, blocking collectives: 21.7 us -> none  [local(): lax.all_to_all(rows.reshape(width, ch // width, n), 'ctx', split_axis=0,...]
    all_to_all x0 -> x1, starting transfers between devices: none -> 6.9 us  [local(): lax.all_to_all(rows.reshape(width, ch // width, n), 'ctx', split_axis=0,...]
    ppermute x1, waiting for transfers between devices: 6.42 us -> 0.01 us  [local(): halo = lax.ppermute(ends, 'ctx', [(i, i + 1) for i in range(width - 1)])]
    unnamed x18, local copies, waits for them, and re-layouts: 1 us -> 5.14 us
    all_to_all x1, blocking collectives: 19.3 us -> 17.5 us  [local(): lax.all_to_all(jnp.broadcast_to(total[None], (width, 1, n)), 'ctx', split...]
    pallas_call x2 -> x3, Pallas kernels: 17.1 us -> 17.9 us  [the longest x2 15.3 us: mixer(): pl.pallas_call(functools.partial(main_kernel, later), grid=(ch // CB,), i...]
  transfers between devices with their start and end apart: 1 -> 2, of which waited for: 1 -> 0; matrix products, arithmetic and copies ran while one was open for 0% -> 0% of each run, Pallas kernels for 0% -> 10%
where the time goes in v2:
time: 73.3 us; the launch traced here: 72.8 us
  blocking collectives  34.7 us (47%)
  Pallas kernels  21.4 us (29%)
  starting transfers between devices  11.5 us (16%)
  local copies, waits for them, and re-layouts  5.17 us (7%)
    all_to_all x1, blocking collectives, local(): lax.all_to_all(jnp.broadcast_to(total[None], (width, 1, n)), 'ctx', split...  17.5 us
    psum x1, blocking collectives, local(): total = lax.psum(squares, 'ch')  17.1 us
    pallas_call x2, Pallas kernels, mixer(): pl.pallas_call(functools.partial(main_kernel, later), grid=(ch // CB,), i...  15.3 us
    all_to_all x1, starting transfers between devices, local(): lax.all_to_all(rows.reshape(width, ch // width, n), 'ctx', split_axis=0,...  6.9 us
    unnamed x18, local copies, waits for them, and re-layouts  5.14 us
    ppermute x1, starting transfers between devices, local(): halo = lax.ppermute(ends, 'ctx', [(i, i + 1) for i in range(width - 1)])  4.59 us
    pallas_call x1, Pallas kernels, final(): pl.pallas_call(final_kernel, grid=(k // per,), in_specs=[pl.BlockSpec((pe...  3.45 us
    pallas_call x1, Pallas kernels, tail(): pl.pallas_call(tail_kernel, grid=(ch // c,), in_specs=[SMEM, SMEM, wide,...  2.68 us
  transfers between devices with their start and end apart: 2, of which 0 were waited for; matrix products, arithmetic and copies ran while one was open for 0% of the time, Pallas kernels for 10%

profile of v2, /device:TPU:1, one launch (start us, length us, event | category | flops | bytes accessed | tf_op | source)
XLA Modules:
  0.0 72.8 jit_solution(13526683818955661379)
XLA Ops:
  0.0 0.0 copy-start.7
  0.0 0.7 copy-done.7
  0.7 0.0 copy-start
  0.7 1.2 %copy-done = bf16[1024,512]{1,0:T(8,128)(2,1)S(1)} copy-done((bf16[1024,512]{1,0:T(8,128)(2,1)S(1)}, bf16[1024,512]{1,0:T(8,128)(2,1)}, u32[]{:S(2)}) %copy-start) | copy-done | bytes 1048600
  1.9 0.0 copy-start.1
  1.9 1.2 %copy-done.1 = bf16[1024,512]{1,0:T(8,128)(2,1)S(1)} copy-done((bf16[1024,512]{1,0:T(8,128)(2,1)S(1)}, bf16[1024,512]{1,0:T(8,128)(2,1)}, u32[]{:S(2)}) %copy-start.1) | copy-done | bytes 1048600
  3.1 0.0 copy-start.2
  3.1 1.2 %copy-done.2 = bf16[1024,512]{1,0:T(8,128)(2,1)S(1)} copy-done((bf16[1024,512]{1,0:T(8,128)(2,1)S(1)}, bf16[1024,512]{1,0:T(8,128)(2,1)}, u32[]{:S(2)}) %copy-start.2) | copy-done | bytes 1048600
  4.3 0.0 copy-start.3
  4.3 0.8 %copy-done.3 = f32[3,3,1024]{2,1,0:T(4,128)S(1)} copy-done((f32[3,3,1024]{2,1,0:T(4,128)S(1)}, f32[3,3,1024]{2,1,0:T(4,128)}, u32[]{:S(2)}) %copy-start.3) | copy-done | bytes 36888
  5.1 0.0 copy-start.4
  5.1 0.0 copy-start.5
  5.1 0.0 copy-start.6
  5.1 2.7 %tail.1 = bf16[8,144,128]{2,1,0:T(8,128)(2,1)S(1)} custom-call(s32[64]{0:T(128)S(1)} %copy-done.7, s32[1]{0:T(128)} %bitcast.base_ref, bf16[1024,512]{1,0:T(8,128)(2,1)S(1)} %copy-done, bf16[1024,512]{1,0:T(8,128)(2,1)S(1)} %copy-done.1, bf16[1024,512]{1,0:T(8,128)(2,1)S(1)} %copy-done.2, f32[3,3,1024]{2,1,0:T(4,128)S(1)} %copy-done.3), custom_call_target="tpu_custom_call" | custom-call | tf_op jit(solution)/shard_map/tail/pallas_call | solution.py:145
  7.8 4.6 %collective-permute-start = (bf16[8,144,128]{2,1,0:T(8,128)(2,1)S(1)}, bf16[8,144,128]{2,1,0:T(8,128)(2,1)S(1)}, u32[]{:S(2)}, u32[]{:S(2)}) collective-permute-start(bf16[8,144,128]{2,1,0:T(8,128)(2,1)S(1)} %tail.1), channel_id=1, source_target_pairs={{0,8},{8,16},{16,24},{24,32},{32,40},{40,48},{48,56},{56,64},{64,7... | collective-permute-start | bytes 884744 | tf_op jit(solution)/shard_map/ppermute | solution.py:207
  12.4 0.0 copy-done.4
  12.4 0.0 copy-done.5
  12.4 0.0 copy-done.6
  12.5 7.3 %later.1 = (bf16[1024,512]{1,0:T(8,128)(2,1)}, f32[1,256]{1,0:T(1,128)S(1)}) custom-call(s32[64]{0:T(128)S(1)} %copy-done.7, s32[1]{0:T(128)} %bitcast.base_ref, bf16[1024,512]{1,0:T(8,128)(2,1)S(1)} %copy-done, bf16[1024,512]{1,0:T(8,128)(2,1)S(1)} %copy-done.1, bf16[1024,512]{1,0:T(8,128)(2,1)S(1)} %copy-done.2, f32[3,3,1024]{2,1,0:T(4,128)S(1)} %copy-done.3, ...), custom_call_target="tpu_custom_call" | custom-call | flops 1073741824 | bytes 1572864 | tf_op jit(solution)/shard_map/later/pallas_call | solution.py:168
  19.7 0.0 collective-permute-done.refs_0_
  19.7 8.0 %first.1 = (bf16[1024,512]{1,0:T(8,128)(2,1)}, f32[1,512]{1,0:T(1,128)S(1)}) custom-call(s32[64]{0:T(128)S(1)} %copy-done.7, s32[1]{0:T(128)} %bitcast.base_ref, bf16[1024,512]{1,0:T(8,128)(2,1)S(1)} %copy-done, bf16[1024,512]{1,0:T(8,128)(2,1)S(1)} %copy-done.1, bf16[1024,512]{1,0:T(8,128)(2,1)S(1)} %copy-done.2, ...), custom_call_target="tpu_custom_call", output_to_operand_aliasing={{0}: (7, {})} | custom-call | flops 1073741824 | bytes 1572864 | tf_op jit(solution)/shard_map/first/pallas_call | solution.py:168
  27.7 6.9 %all-to-all-start = ((bf16[32,32,512]{2,1,0:T(8,128)(2,1)}), bf16[32,32,512]{2,1,0:T(8,128)(2,1)S(1)}, u32[]{:S(2)}, u32[]{:S(2)}) async-start(bf16[32,32,512]{2,1,0:T(8,128)(2,1)} %bitcast.3), calls=%async_computation | async-start | bytes 2097152 | tf_op jit(solution)/shard_map/all_to_all | solution.py:210
  34.6 17.1 %psum.7 = f32[1,512]{1,0:T(1,128)S(1)} all-reduce(f32[1,512]{1,0:T(1,128)S(1)} %get-tuple-element.13), channel_id=1, replica_groups=mesh['ctx'=32,'ch'=8] {'ch'}, use_global_device_ids=true, to_apply=%region_0.0 | all-reduce | flops 512 | bytes 4096 | tf_op jit(solution)/shard_map/psum | solution.py:211
  51.8 0.0 all-to-all-done.recv_ref
  51.8 0.0 copy-start.8
  51.8 17.5 %all_to_all.10.sums_ref = f32[32,1,512]{2,1,0:T(1,128)} all-to-all(f32[32,1,512]{2,1,0:T(1,128)S(1)} %broadcast_in_dim.9), channel_id=1, replica_groups=mesh['ctx'=32,'ch'=8] {'ctx'}, dimensions={0} | all-to-all | bytes 131072 | tf_op jit(solution)/shard_map/all_to_all | solution.py:213
  69.3 0.0 copy-done.8
  69.3 3.5 %settle.1 = bf16[32,16384]{1,0:T(8,128)(2,1)} custom-call(bf16[32,32,512]{2,1,0:T(8,128)(2,1)} %copy-done.8, f32[32,1,512]{2,1,0:T(1,128)} %all_to_all.10.sums_ref), custom_call_target="tpu_custom_call" | custom-call | tf_op jit(solution)/shard_map/settle/pallas_call | solution.py:192
  (1 shorter events, 0.0 us)
Async XLA Ops:
  0.0 0.7 copy-start.7
  0.7 1.2 %copy-start = (bf16[1024,512]{1,0:T(8,128)(2,1)S(1)}, bf16[1024,512]{1,0:T(8,128)(2,1)}, u32[]{:S(2)}) copy-start(bf16[1024,512]{1,0:T(8,128)(2,1)} %gate_ref.5) | copy-start | bytes 3145732
  1.9 1.2 %copy-start.1 = (bf16[1024,512]{1,0:T(8,128)(2,1)S(1)}, bf16[1024,512]{1,0:T(8,128)(2,1)}, u32[]{:S(2)}) copy-start(bf16[1024,512]{1,0:T(8,128)(2,1)} %key_ref.5) | copy-start | bytes 3145732
  3.1 1.2 %copy-start.2 = (bf16[1024,512]{1,0:T(8,128)(2,1)S(1)}, bf16[1024,512]{1,0:T(8,128)(2,1)}, u32[]{:S(2)}) copy-start(bf16[1024,512]{1,0:T(8,128)(2,1)} %value_ref.5) | copy-start | bytes 3145732
  4.3 0.8 %copy-start.3 = (f32[3,3,1024]{2,1,0:T(4,128)S(1)}, f32[3,3,1024]{2,1,0:T(4,128)}, u32[]{:S(2)}) copy-start(f32[3,3,1024]{2,1,0:T(4,128)} %refs_3_.3) | copy-start | bytes 110596
  5.1 7.3 %copy-start.4 = (f32[64,128]{1,0:T(8,128)S(1)}, f32[64,128]{1,0:T(8,128)}, u32[]{:S(2)}) copy-start(f32[64,128]{1,0:T(8,128)} %refs_6_.1) | copy-start | bytes 98308
  5.1 7.3 %copy-start.5 = (f32[1024]{0:T(1024)S(1)}, f32[1024]{0:T(1024)}, u32[]{:S(2)}) copy-start(f32[1024]{0:T(1024)} %param.13) | copy-start | bytes 12292
  5.1 7.3 %copy-start.6 = (f32[1024]{0:T(1024)S(1)}, f32[1024]{0:T(1024)}, u32[]{:S(2)}) copy-start(f32[1024]{0:T(1024)} %param.14) | copy-start | bytes 12292
  7.8 11.9 %collective-permute-start = (bf16[8,144,128]{2,1,0:T(8,128)(2,1)S(1)}, bf16[8,144,128]{2,1,0:T(8,128)(2,1)S(1)}, u32[]{:S(2)}, u32[]{:S(2)}) collective-permute-start(bf16[8,144,128]{2,1,0:T(8,128)(2,1)S(1)} %tail.1), channel_id=1, source_target_pairs={{0,8},{8,16},{16,24},{24,32},{32,40},{40,48},{48,56},{56,64},{64,7... | collective-permute-start | bytes 884744 | tf_op jit(solution)/shard_map/ppermute | solution.py:207
  27.7 24.1 %all-to-all-start = ((bf16[32,32,512]{2,1,0:T(8,128)(2,1)}), bf16[32,32,512]{2,1,0:T(8,128)(2,1)S(1)}, u32[]{:S(2)}, u32[]{:S(2)}) async-start(bf16[32,32,512]{2,1,0:T(8,128)(2,1)} %bitcast.3), calls=%async_computation | async-start | bytes 2097152 | tf_op jit(solution)/shard_map/all_to_all | solution.py:210
  51.8 17.6 %copy-start.8 = (bf16[32,32,512]{2,1,0:T(8,128)(2,1)}, bf16[32,32,512]{2,1,0:T(8,128)(2,1)S(1)}, u32[]{:S(2)}) copy-start(bf16[32,32,512]{2,1,0:T(8,128)(2,1)S(1)} %all-to-all-done.recv_ref) | copy-start | bytes 3145732

commit v3 on v2

--- a/solution.py
+++ b/solution.py
@@ -15,6 +15,9 @@
 F32 = jnp.float32
 BF = jnp.bfloat16
 CB = 128
+BL = 256
+BIG = 56 << 20
+PER = 16
 ENDS = 144
 SMEM = pl.BlockSpec(memory_space=pltpu.SMEM)
 
@@ -70,6 +73,46 @@
         out_ref[b, CB:] = raw.astype(BF)
 
 
+def block(later, b, gate_ref, key_ref, value_ref, halo_ref, sf_ref, skip_ref, gain_ref, taps_ref, out_ref,
+          masks, keeps, prod, mixed, acc):
+    n = 256
+    here = slice(CB * b, CB * (b + 1))
+    cols = columns(sf_ref[:, :, here], skip_ref[:, here], gain_ref[:, here])
+    if later:
+        kc = conv3(key_ref[here].astype(F32), cols, 3, keeps)
+        vc = conv3(value_ref[here].astype(F32), cols, 6, keeps)
+        prod[...] = (kc * vc).astype(BF)
+        gate = gate_ref[here, 128:].astype(F32)
+    else:
+        row = lax.broadcasted_iota(jnp.int32, (16, 128), 0)
+        lane = lax.broadcasted_iota(jnp.int32, (16, 128), 1)
+
+        def before(i):
+            put = ((lane == 126 + row - 2 * i) & (row >= 2 * i) & (row < 2 * i + 2)).astype(F32).astype(BF)
+            return lax.dot_general(halo_ref[b, CB:], put, (((0,), (0,)), ((), ())), preferred_element_type=F32)
+
+        keep = keeps[:, :, 128:]
+        kc = conv3(jnp.concatenate([before(1), key_ref[here].astype(F32)], axis=1), cols, 3, keep)
+        vc = conv3(jnp.concatenate([before(2), value_ref[here].astype(F32)], axis=1), cols, 6, keep)
+        prod[:, :128] = halo_ref[b, :CB]
+        prod[:, 128:] = (kc * vc).astype(BF)
+        gate = jnp.concatenate([before(0), gate_ref[here].astype(F32)], axis=1)
+
+    taps = taps_ref[8 * b:8 * (b + 1)].astype(BF).astype(F32)
+    for g in range(CB // GROUP):
+        ring = pltpu.roll(jnp.broadcast_to(taps[g:g + 1], (128, 128)), 0, 1, stride=1, stride_axis=0).astype(BF)
+        both = jnp.concatenate([ring, ring], axis=0)
+        for j in range(2):
+            mixed[GROUP * g:GROUP * (g + 1), 128 * j:128 * (j + 1)] = jnp.dot(
+                prod[GROUP * g:GROUP * (g + 1), 128 * j:128 * j + 256], both * masks[j],
+                preferred_element_type=F32)
+
+    gc = conv3(gate, cols, 0, keeps[:, :, 128:])
+    gated = gc * (mixed[...] + cols[:, 9:10] * prod[:, 128:].astype(F32))
+    acc[...] += jnp.sum((gated * gated).reshape(CB // 8, 8, n), axis=0)
+    out_ref[here] = (gated * cols[:, 10:11]).astype(BF)
+
+
 def main_kernel(later, docs_ref, base_ref, gate_ref, key_ref, value_ref, *refs):
     if later:
         sf_ref, skip_ref, gain_ref, taps_ref, out_ref, sq_ref, masks, keeps, prod, mixed, acc = refs
@@ -93,40 +136,9 @@
             masks[j, 128:, :] = ((s <= t) & (s >= first)).astype(F32).astype(BF)
         acc[...] = jnp.zeros_like(acc)
 
-    cols = columns(sf_ref[...], skip_ref[...], gain_ref[...])
-    if later:
-        kc = conv3(key_ref[...].astype(F32), cols, 3, keeps)
-        vc = conv3(value_ref[...].astype(F32), cols, 6, keeps)
-        prod[...] = (kc * vc).astype(BF)
-        gate = gate_ref[:, 128:].astype(F32)
-    else:
-        row = lax.broadcasted_iota(jnp.int32, (16, 128), 0)
-        lane = lax.broadcasted_iota(jnp.int32, (16, 128), 1)
-
-        def before(i):
-            put = ((lane == 126 + row - 2 * i) & (row >= 2 * i) & (row < 2 * i + 2)).astype(F32).astype(BF)
-            return lax.dot_general(halo_ref[0, CB:], put, (((0,), (0,)), ((), ())), preferred_element_type=F32)
-
-        keep = keeps[:, :, 128:]
-        kc = conv3(jnp.concatenate([before(1), key_ref[...].astype(F32)], axis=1), cols, 3, keep)
-        vc = conv3(jnp.concatenate([before(2), value_ref[...].astype(F32)], axis=1), cols, 6, keep)
-        prod[:, :128] = halo_ref[0, :CB]
-        prod[:, 128:] = (kc * vc).astype(BF)
-        gate = jnp.concatenate([before(0), gate_ref[...].astype(F32)], axis=1)
-
-    taps = taps_ref[...].astype(BF).astype(F32)
-    for g in range(CB // GROUP):
-        ring = pltpu.roll(jnp.broadcast_to(taps[g:g + 1], (128, 128)), 0, 1, stride=1, stride_axis=0).astype(BF)
-        both = jnp.concatenate([ring, ring], axis=0)
-        for j in range(2):
-            mixed[GROUP * g:GROUP * (g + 1), 128 * j:128 * (j + 1)] = jnp.dot(
-                prod[GROUP * g:GROUP * (g + 1), 128 * j:128 * j + 256], both * masks[j],
-                preferred_element_type=F32)
-
-    gc = conv3(gate, cols, 0, keeps[:, :, 128:])
-    gated = gc * (mixed[...] + cols[:, 9:10] * prod[:, 128:].astype(F32))
-    acc[...] += jnp.sum((gated * gated).reshape(CB // 8, 8, n), axis=0)
-    out_ref[...] = (gated * cols[:, 10:11]).astype(BF)
+    for b in range(gate_ref.shape[0] // CB):
+        block(later, b, gate_ref, key_ref, value_ref, None if later else halo_ref, sf_ref, skip_ref, gain_ref, taps_ref,
+              out_ref, masks, keeps, prod.at[b], mixed.at[b], acc)
 
     @pl.when(step == pl.num_programs(0) - 1)
     def _():
@@ -148,34 +160,35 @@
         out_specs=pl.BlockSpec((c // CB, ENDS, 128), lambda i: (i, 0, 0)),
         out_shape=jax.ShapeDtypeStruct((ch // CB, ENDS, 128), BF),
         scratch_shapes=[pltpu.VMEM((2, 8, 128), F32)],
-        compiler_params=pltpu.CompilerParams(vmem_limit_bytes=32 << 20), name="tail",
+        compiler_params=pltpu.CompilerParams(vmem_limit_bytes=BIG), name="tail",
     )(docs, base, gate, key, value, sf)
 
 
 def mixer(docs, base, gate, key, value, halo, earlier, sf, skip, gain, taps):
     ch, n = gate.shape
     later = halo is None
-    row = pl.BlockSpec((1, CB), lambda i: (0, i))
-    half = pl.BlockSpec((CB, 256), lambda i: (i, 0))
-    raw = pl.BlockSpec((CB, n), lambda i: (i, 0)) if later else half
+    bl = min(BL, ch)
+    row = pl.BlockSpec((1, bl), lambda i: (0, i))
+    half = pl.BlockSpec((bl, 256), lambda i: (i, 0))
+    raw = pl.BlockSpec((bl, n), lambda i: (i, 0)) if later else half
     extra, specs, alias = (), [], {}
     if not later:
         extra = (halo, earlier[1], earlier[0])
-        specs = [pl.BlockSpec((1, ENDS, 128), lambda i: (i, 0, 0)), pl.BlockSpec((1, 256), lambda i: (0, 0)),
+        specs = [pl.BlockSpec((bl // CB, ENDS, 128), lambda i: (i, 0, 0)), pl.BlockSpec((1, 256), lambda i: (0, 0)),
                  pl.BlockSpec(memory_space=pl.ANY)]
         alias = {7: 0}
     sq = 256 if later else 512
     return pl.pallas_call(
-        functools.partial(main_kernel, later), grid=(ch // CB,),
+        functools.partial(main_kernel, later), grid=(ch // bl,),
         in_specs=[SMEM, SMEM, raw, raw, raw] + specs
-        + [sf_spec(CB), row, row, pl.BlockSpec((CB // GROUP, MR), lambda i: (i, 0))],
-        out_specs=[pl.BlockSpec((CB, 256), lambda i: (i, 1 if later else 0)), pl.BlockSpec((1, sq), lambda i: (0, 0))],
+        + [sf_spec(bl), row, row, pl.BlockSpec((bl // GROUP, MR), lambda i: (i, 0))],
+        out_specs=[pl.BlockSpec((bl, 256), lambda i: (i, 1 if later else 0)), pl.BlockSpec((1, sq), lambda i: (0, 0))],
         out_shape=[jax.ShapeDtypeStruct((ch, n), BF), jax.ShapeDtypeStruct((1, sq), F32)],
-        scratch_shapes=[pltpu.VMEM((2, 256, 128), BF), pltpu.VMEM((2, 8, 384), F32), pltpu.VMEM((CB, 384), BF),
-                        pltpu.VMEM((CB, 256), F32), pltpu.VMEM((8, 256), F32)],
+        scratch_shapes=[pltpu.VMEM((2, 256, 128), BF), pltpu.VMEM((2, 8, 384), F32), pltpu.VMEM((bl // CB, CB, 384), BF),
+                        pltpu.VMEM((bl // CB, CB, 256), F32), pltpu.VMEM((8, 256), F32)],
         input_output_aliases=alias,
         cost_estimate=pl.CostEstimate(flops=2 * ch * 256 * 256 * 8, bytes_accessed=6 * ch * 256, transcendentals=0),
-        compiler_params=pltpu.CompilerParams(vmem_limit_bytes=32 << 20), name="later" if later else "first",
+        compiler_params=pltpu.CompilerParams(vmem_limit_bytes=BIG), name="later" if later else "first",
     )(docs, base, gate, key, value, *extra, sf, skip, gain, taps)
 
 
@@ -188,13 +201,25 @@
 
 def final(recv, sums):
     k, c, n = recv.shape
-    per = min(k, 8)
+    per = min(k, PER)
     return pl.pallas_call(
         final_kernel, grid=(k // per,),
         in_specs=[pl.BlockSpec((per, c, n), lambda i: (i, 0, 0)), pl.BlockSpec((per, 1, n), lambda i: (i, 0, 0))],
         out_specs=pl.BlockSpec((c, per * n), lambda i: (0, i)),
-        out_shape=jax.ShapeDtypeStruct((c, k * n), BF), name="settle",
+        out_shape=jax.ShapeDtypeStruct((c, k * n), BF),
+        compiler_params=pltpu.CompilerParams(vmem_limit_bytes=BIG), name="settle",
     )(recv, sums)
+
+
+ROUNDS = (((0, 1), (2, 3), (4, 5), (6, 7)), ((1, 2), (3, 4), (5, 6), (7, 0)), ((0, 3), (7, 4), (1, 6), (2, 5)))
+
+
+def channel_sum(x):
+    if lax.axis_size("ch") != 8:
+        return lax.psum(x, "ch")
+    for pairs in ROUNDS:
+        x = x + lax.ppermute(x, "ch", list(pairs) + [(b, a) for a, b in pairs])
+    return x
 
 
 def local(gate, key, value, sf, taps, skip, gain, docs):
@@ -208,7 +233,7 @@
     later = mixer(docs, base, gate, key, value, None, None, sf, skip, gain, taps)
     rows, squares = mixer(docs, base, gate, key, value, halo, later, sf, skip, gain, taps)
     recv = lax.all_to_all(rows.reshape(width, ch // width, n), "ctx", split_axis=0, concat_axis=0, tiled=True)
-    total = lax.psum(squares, "ch")
+    total = channel_sum(squares)
     total, recv = lax.optimization_barrier((total, recv))
     sums = lax.all_to_all(jnp.broadcast_to(total[None], (width, 1, n)), "ctx", split_axis=0, concat_axis=0, tiled=True)
     return final(recv, sums)

time: 73.3 us -> 65.4 us (0.89)
  blocking collectives: 34.7 us -> 14.3 us
  starting transfers between devices: 11.5 us -> 20.5 us
  waiting for transfers between devices: 0.01 us -> 7.87 us
  local copies, waits for them, and re-layouts: 5.17 us -> 0.75 us
    psum x1 -> x0, blocking collectives: 17.1 us -> none  [local(): total = lax.psum(squares, 'ch')]
    ppermute x0 -> x3, starting transfers between devices: none -> 9.01 us  [channel_sum(): x = x + lax.ppermute(x, 'ch', list(pairs) + [(b, a) for a, b in pairs])]
    ppermute x0 -> x3, waiting for transfers between devices: none -> 4.9 us  [channel_sum(): x = x + lax.ppermute(x, 'ch', list(pairs) + [(b, a) for a, b in pairs])]
    unnamed x18 -> x6, local copies, waits for them, and re-layouts: 5.14 us -> 0.71 us
    all_to_all x1, blocking collectives: 17.5 us -> 14.3 us  [local(): lax.all_to_all(jnp.broadcast_to(total[None], (width, 1, n)), 'ctx', split...]
    all_to_all x1, waiting for transfers between devices: 0.01 us -> 2.97 us  [local(): lax.all_to_all(rows.reshape(width, ch // width, n), 'ctx', split_axis=0,...]
    pallas_call x1, Pallas kernels: 3.45 us -> 2.12 us  [final(): pl.pallas_call(final_kernel, grid=(k // per,), in_specs=[pl.BlockSpec((pe...]
    pallas_call x1, Pallas kernels: 2.68 us -> 3.86 us  [tail(): pl.pallas_call(tail_kernel, grid=(ch // c,), in_specs=[SMEM, SMEM, wide,...]
  transfers between devices with their start and end apart: 2 -> 5, of which waited for: 0 -> 4; matrix products, arithmetic and copies ran while one was open for 0% -> 0% of each run, Pallas kernels for 10% -> 11%
where the time goes in v3:
time: 65.4 us; the launch traced here: 65.1 us
  Pallas kernels  21.6 us (33%)
  starting transfers between devices  20.5 us (31%)
  blocking collectives  14.3 us (22%)
  waiting for transfers between devices  7.87 us (12%)
  local copies, waits for them, and re-layouts  0.75 us (1%)
    pallas_call x2, Pallas kernels, mixer(): pl.pallas_call(functools.partial(main_kernel, later), grid=(ch // bl,), i...  15.6 us
    all_to_all x1, blocking collectives, local(): lax.all_to_all(jnp.broadcast_to(total[None], (width, 1, n)), 'ctx', split...  14.3 us
    ppermute x3, starting transfers between devices, channel_sum(): x = x + lax.ppermute(x, 'ch', list(pairs) + [(b, a) for a, b in pairs])  9.01 us
    all_to_all x1, starting transfers between devices, local(): lax.all_to_all(rows.reshape(width, ch // width, n), 'ctx', split_axis=0,...  6.92 us
    ppermute x3, waiting for transfers between devices, channel_sum(): x = x + lax.ppermute(x, 'ch', list(pairs) + [(b, a) for a, b in pairs])  4.9 us
    ppermute x1, starting transfers between devices, local(): halo = lax.ppermute(ends, 'ctx', [(i, i + 1) for i in range(width - 1)])  4.58 us
    pallas_call x1, Pallas kernels, tail(): pl.pallas_call(tail_kernel, grid=(ch // c,), in_specs=[SMEM, SMEM, wide,...  3.86 us
    all_to_all x1, waiting for transfers between devices, local(): lax.all_to_all(rows.reshape(width, ch // width, n), 'ctx', split_axis=0,...  2.97 us
  transfers between devices with their start and end apart: 5, of which 4 were waited for; matrix products, arithmetic and copies ran while one was open for 0% of the time, Pallas kernels for 11%

profile of v3, /device:TPU:1, one launch (start us, length us, event | category | flops | bytes accessed | tf_op | source)
XLA Modules:
  0.0 65.1 jit_solution(13014839508348657961)
XLA Ops:
  0.0 3.9 %tail.1 = bf16[8,144,128]{2,1,0:T(8,128)(2,1)} custom-call(s32[64]{0:T(128)} %docs_ref.5, s32[1]{0:T(128)} %bitcast.base_ref, bf16[1024,512]{1,0:T(8,128)(2,1)} %gate_ref.5, bf16[1024,512]{1,0:T(8,128)(2,1)} %key_ref.5, bf16[1024,512]{1,0:T(8,128)(2,1)} %value_ref.5, f32[3,3,1024]{2,1,0:T(4,128)} %refs_3_.3), custom_call_target="tpu_custom_call" | custom-call | tf_op jit(solution)/shard_map/tail/pallas_call | solution.py:157
  3.9 4.6 %collective-permute-start = (bf16[8,144,128]{2,1,0:T(8,128)(2,1)}, bf16[8,144,128]{2,1,0:T(8,128)(2,1)S(1)}, u32[]{:S(2)}, u32[]{:S(2)}) collective-permute-start(bf16[8,144,128]{2,1,0:T(8,128)(2,1)} %tail.1), channel_id=1, source_target_pairs={{0,8},{8,16},{16,24},{24,32},{32,40},{40,48},{48,56},{56,64},{64,7... | collective-permute-start | bytes 884744 | tf_op jit(solution)/shard_map/ppermute | solution.py:232
  8.5 7.5 %later.1 = (bf16[1024,512]{1,0:T(8,128)(2,1)}, f32[1,256]{1,0:T(1,128)}) custom-call(s32[64]{0:T(128)} %docs_ref.5, s32[1]{0:T(128)} %bitcast.base_ref, bf16[1024,512]{1,0:T(8,128)(2,1)} %gate_ref.5, bf16[1024,512]{1,0:T(8,128)(2,1)} %key_ref.5, bf16[1024,512]{1,0:T(8,128)(2,1)} %value_ref.5, f32[3,3,1024]{2,1,0:T(4,128)} %refs_3_.3, f32[1,1024]{1,0:T(1,128)} %bitcast.7, ...), custom_call_target="tpu_custom_call" | custom-call | flops 1073741824 | bytes 1572864 | tf_op jit(solution)/shard_map/later/pallas_call | solution.py:181
  15.9 0.0 collective-permute-done.refs_0_
  15.9 0.0 copy-start.1
  15.9 0.7 %copy-done.1 = bf16[8,144,128]{2,1,0:T(8,128)(2,1)} copy-done((bf16[8,144,128]{2,1,0:T(8,128)(2,1)}, bf16[8,144,128]{2,1,0:T(8,128)(2,1)S(1)}, u32[]{:S(2)}) %copy-start.1) | copy-done | bytes 294936
  16.6 8.2 %first.1 = (bf16[1024,512]{1,0:T(8,128)(2,1)}, f32[1,512]{1,0:T(1,128)}) custom-call(s32[64]{0:T(128)} %docs_ref.5, s32[1]{0:T(128)} %bitcast.base_ref, bf16[1024,512]{1,0:T(8,128)(2,1)} %gate_ref.5, bf16[1024,512]{1,0:T(8,128)(2,1)} %key_ref.5, bf16[1024,512]{1,0:T(8,128)(2,1)} %value_ref.5, ...), custom_call_target="tpu_custom_call", output_to_operand_aliasing={{0}: (7, {})} | custom-call | flops 1073741824 | bytes 1572864 | tf_op jit(solution)/shard_map/first/pallas_call | solution.py:181
  24.8 0.0 copy-start.2
  24.8 6.9 %all-to-all-start = ((bf16[32,32,512]{2,1,0:T(8,128)(2,1)}), bf16[32,32,512]{2,1,0:T(8,128)(2,1)S(1)}, u32[]{:S(2)}, u32[]{:S(2)}) async-start(bf16[32,32,512]{2,1,0:T(8,128)(2,1)} %bitcast.5), calls=%async_computation | async-start | bytes 2097152 | tf_op jit(solution)/shard_map/all_to_all | solution.py:235
  31.7 0.0 copy-done.2
  31.7 1.7 %collective-permute-start.1 = (f32[1,512]{1,0:T(1,128)S(1)}, f32[1,512]{1,0:T(1,128)S(1)}, u32[]{:S(2)}, u32[]{:S(2)}) collective-permute-start(f32[1,512]{1,0:T(1,128)S(1)} %copy-done.2), channel_id=1, source_target_pairs={{0,1},{2,3},{4,5},{6,7},{1,0},{3,2},{5,4},{7,6},{8,9},{10,11},{12,... | collective-permute-start | bytes 6152 | tf_op jit(solution)/shard_map/ppermute | solution.py:221
  33.5 1.3 %collective-permute-done.1 = f32[1,512]{1,0:T(1,128)S(1)} collective-permute-done((f32[1,512]{1,0:T(1,128)S(1)}, f32[1,512]{1,0:T(1,128)S(1)}, u32[]{:S(2)}, u32[]{:S(2)}) %collective-permute-start.1) | collective-permute-done | bytes 2080 | tf_op jit(solution)/shard_map/ppermute | solution.py:221
  34.7 5.4 %collective-permute-start.2 = (f32[1,512]{1,0:T(1,128)S(1)}, f32[1,512]{1,0:T(1,128)S(1)}, u32[]{:S(2)}, u32[]{:S(2)}) collective-permute-start(f32[1,512]{1,0:T(1,128)S(1)} %add.9), channel_id=1, source_target_pairs={{1,2},{3,4},{5,6},{7,0},{2,1},{4,3},{6,5},{0,7},{9,10},{11,12},{13... | collective-permute-start | bytes 6152 | tf_op jit(solution)/shard_map/ppermute | solution.py:221
  40.1 1.0 %collective-permute-done.2 = f32[1,512]{1,0:T(1,128)S(1)} collective-permute-done((f32[1,512]{1,0:T(1,128)S(1)}, f32[1,512]{1,0:T(1,128)S(1)}, u32[]{:S(2)}, u32[]{:S(2)}) %collective-permute-start.2) | collective-permute-done | bytes 2080 | tf_op jit(solution)/shard_map/ppermute | solution.py:221
  41.1 1.9 %collective-permute-start.3 = (f32[1,512]{1,0:T(1,128)S(1)}, f32[1,512]{1,0:T(1,128)S(1)}, u32[]{:S(2)}, u32[]{:S(2)}) collective-permute-start(f32[1,512]{1,0:T(1,128)S(1)} %add.10), channel_id=1, source_target_pairs={{0,3},{7,4},{1,6},{2,5},{3,0},{4,7},{6,1},{5,2},{8,11},{15,12},{9,... | collective-permute-start | bytes 6152 | tf_op jit(solution)/shard_map/ppermute | solution.py:221
  43.0 2.6 %collective-permute-done.3 = f32[1,512]{1,0:T(1,128)S(1)} collective-permute-done((f32[1,512]{1,0:T(1,128)S(1)}, f32[1,512]{1,0:T(1,128)S(1)}, u32[]{:S(2)}, u32[]{:S(2)}) %collective-permute-start.3) | collective-permute-done | bytes 2080 | tf_op jit(solution)/shard_map/ppermute | solution.py:221
  45.7 3.0 %all-to-all-done.recv_ref = bf16[32,32,512]{2,1,0:T(8,128)(2,1)S(1)} async-done(((bf16[32,32,512]{2,1,0:T(8,128)(2,1)}), bf16[32,32,512]{2,1,0:T(8,128)(2,1)S(1)}, u32[]{:S(2)}, u32[]{:S(2)}) %all-to-all-start) | async-done | bytes 1048608 | tf_op jit(solution)/shard_map/all_to_all | solution.py:235
  48.7 0.0 copy-start
  48.7 14.3 %all_to_all.10.sums_ref = f32[32,1,512]{2,1,0:T(1,128)} all-to-all(f32[32,1,512]{2,1,0:T(1,128)S(1)} %broadcast_in_dim.9), channel_id=1, replica_groups=mesh['ctx'=32,'ch'=8] {'ctx'}, dimensions={0} | all-to-all | bytes 131072 | tf_op jit(solution)/shard_map/all_to_all | solution.py:238
  63.0 0.0 copy-done
  63.0 2.1 %settle.1 = bf16[32,16384]{1,0:T(8,128)(2,1)} custom-call(bf16[32,32,512]{2,1,0:T(8,128)(2,1)} %copy-done, f32[32,1,512]{2,1,0:T(1,128)} %all_to_all.10.sums_ref), custom_call_target="tpu_custom_call" | custom-call | tf_op jit(solution)/shard_map/settle/pallas_call | solution.py:205
  (4 shorter events, 0.0 us)
Async XLA Ops:
  3.9 12.1 %collective-permute-start = (bf16[8,144,128]{2,1,0:T(8,128)(2,1)}, bf16[8,144,128]{2,1,0:T(8,128)(2,1)S(1)}, u32[]{:S(2)}, u32[]{:S(2)}) collective-permute-start(bf16[8,144,128]{2,1,0:T(8,128)(2,1)} %tail.1), channel_id=1, source_target_pairs={{0,8},{8,16},{16,24},{24,32},{32,40},{40,48},{48,56},{56,64},{64,7... | collective-permute-start | bytes 884744 | tf_op jit(solution)/shard_map/ppermute | solution.py:232
  15.9 0.7 %copy-start.1 = (bf16[8,144,128]{2,1,0:T(8,128)(2,1)}, bf16[8,144,128]{2,1,0:T(8,128)(2,1)S(1)}, u32[]{:S(2)}) copy-start(bf16[8,144,128]{2,1,0:T(8,128)(2,1)S(1)} %collective-permute-done.refs_0_) | copy-start | bytes 884740
  24.8 6.9 %copy-start.2 = (f32[1,512]{1,0:T(1,128)S(1)}, f32[1,512]{1,0:T(1,128)}, u32[]{:S(2)}) copy-start(f32[1,512]{1,0:T(1,128)} %get-tuple-element.13) | copy-start | bytes 6148
  24.8 23.8 %all-to-all-start = ((bf16[32,32,512]{2,1,0:T(8,128)(2,1)}), bf16[32,32,512]{2,1,0:T(8,128)(2,1)S(1)}, u32[]{:S(2)}, u32[]{:S(2)}) async-start(bf16[32,32,512]{2,1,0:T(8,128)(2,1)} %bitcast.5), calls=%async_computation | async-start | bytes 2097152 | tf_op jit(solution)/shard_map/all_to_all | solution.py:235
  31.7 3.0 %collective-permute-start.1 = (f32[1,512]{1,0:T(1,128)S(1)}, f32[1,512]{1,0:T(1,128)S(1)}, u32[]{:S(2)}, u32[]{:S(2)}) collective-permute-start(f32[1,512]{1,0:T(1,128)S(1)} %copy-done.2), channel_id=1, source_target_pairs={{0,1},{2,3},{4,5},{6,7},{1,0},{3,2},{5,4},{7,6},{8,9},{10,11},{12,... | collective-permute-start | bytes 6152 | tf_op jit(solution)/shard_map/ppermute | solution.py:221
  34.7 6.4 %collective-permute-start.2 = (f32[1,512]{1,0:T(1,128)S(1)}, f32[1,512]{1,0:T(1,128)S(1)}, u32[]{:S(2)}, u32[]{:S(2)}) collective-permute-start(f32[1,512]{1,0:T(1,128)S(1)} %add.9), channel_id=1, source_target_pairs={{1,2},{3,4},{5,6},{7,0},{2,1},{4,3},{6,5},{0,7},{9,10},{11,12},{13... | collective-permute-start | bytes 6152 | tf_op jit(solution)/shard_map/ppermute | solution.py:221
  41.1 4.5 %collective-permute-start.3 = (f32[1,512]{1,0:T(1,128)S(1)}, f32[1,512]{1,0:T(1,128)S(1)}, u32[]{:S(2)}, u32[]{:S(2)}) collective-permute-start(f32[1,512]{1,0:T(1,128)S(1)} %add.10), channel_id=1, source_target_pairs={{0,3},{7,4},{1,6},{2,5},{3,0},{4,7},{6,1},{5,2},{8,11},{15,12},{9,... | collective-permute-start | bytes 6152 | tf_op jit(solution)/shard_map/ppermute | solution.py:221
  48.7 14.3 %copy-start = (bf16[32,32,512]{2,1,0:T(8,128)(2,1)}, bf16[32,32,512]{2,1,0:T(8,128)(2,1)S(1)}, u32[]{:S(2)}) copy-start(bf16[32,32,512]{2,1,0:T(8,128)(2,1)S(1)} %all-to-all-done.recv_ref) | copy-start | bytes 3145732

commit v4 on v3

v4 whole, which is shorter than its diff:
```python
import jax
import jax.numpy as jnp
from jax import lax
from jax.experimental import pallas as pl
from jax.experimental.pallas import tpu as pltpu
from jax.sharding import PartitionSpec as P

D = 8192
GROUP = 16
MR = 128
EPS = 1e-6
DOCS = 64
F32 = jnp.float32
BF = jnp.bfloat16
CB = 128
BL = 512
ENDS = 144
PER = 16
BIG = 56 << 20
SMEM = pl.BlockSpec(memory_space=pltpu.SMEM)


def starts_row(docs_ref, base, count):
    pos = lax.broadcasted_iota(jnp.int32, (1, count), 1) + base
    first = jnp.int32(0)
    start = jnp.zeros((1, count), jnp.int32)
    for d in range(DOCS):
        start = jnp.where(pos >= first, first, start)
        first = first + docs_ref[d]
    return pos, start


def as_bf(flag, shape):
    return jnp.broadcast_to(flag.astype(F32), shape).astype(BF)


def tile_masks(first):
    s = lax.broadcasted_iota(jnp.int32, (128, 128), 0)
    t = lax.broadcasted_iota(jnp.int32, (128, 128), 1)
    return (((s > t) & (s - 128 >= first)).astype(F32).astype(BF), ((s <= t) & (s >= first)).astype(F32).astype(BF))


def columns(rows):
    rows = rows + [jnp.zeros((16 - sum(r.shape[0] for r in rows), CB), F32)]
    return jnp.concatenate(rows, axis=0).T


def conv3(raw, keeps, cols, first):
    one = pltpu.roll(raw, 1, 1) * keeps[0]
    two = pltpu.roll(raw, 2, 1) * keeps[1]
    return (cols[:, first:first + 1] * raw.astype(F32) + cols[:, first + 1:first + 2] * one.astype(F32)
            + cols[:, first + 2:first + 3] * two.astype(F32))


def ring_of(taps):
    return pltpu.roll(jnp.broadcast_to(taps, (128, 128)), 0, 1, stride=1, stride_axis=0).astype(BF)


def pick(here, *wanted):
    row = lax.broadcasted_iota(jnp.int32, (16, 128), 0)
    lane = lax.broadcasted_iota(jnp.int32, (16, 128), 1)
    out = jnp.zeros((16, CB), F32)
    for ref, lanes, at, first, count in wanted:
        one_hot = ((lane - first == row - at) & (row >= at) & (row < at + count)).astype(F32).astype(BF)
        out = out + lax.dot_general(one_hot, ref[here, lanes], (((1,), (1,)), ((), ())), preferred_element_type=F32)
    return out.astype(BF)


def tail_kernel(docs_ref, base_ref, gate_ref, key_ref, value_ref, sf_ref, out_ref, keeps):
    @pl.when(pl.program_id(0) == 0)
    def _():
        pos, start = starts_row(docs_ref, base_ref[0] + 384, 128)
        for lag in (1, 2):
            keeps[lag - 1] = as_bf(pos - lag >= start, (GROUP, 128))

    last = lax.broadcasted_iota(jnp.int32, (GROUP, 128), 1) == 127

    def filtered(ref, at, cols, i):
        raw = ref[at, 128:]
        one = pltpu.roll(raw, 1, 1) * keeps[0]
        two = pltpu.roll(jnp.where(last, ref[at, :128], raw), 2, 1) * keeps[1]
        return (cols[:, i:i + 1] * raw.astype(F32) + cols[:, i + 1:i + 2] * one.astype(F32)
                + cols[:, i + 2:i + 3] * two.astype(F32))

    for b in range(gate_ref.shape[0] // CB):
        here = slice(CB * b, CB * (b + 1))
        sf = sf_ref[:, :, here]
        cols = columns([sf[1], sf[2]])
        for g in range(CB // GROUP):
            at = slice(CB * b + GROUP * g, CB * b + GROUP * (g + 1))
            c = cols[GROUP * g:GROUP * (g + 1)]
            out_ref[b, GROUP * g:GROUP * (g + 1)] = (filtered(key_ref, at, c, 0) * filtered(value_ref, at, c, 3)).astype(BF)
        lanes = slice(128, 256)
        out_ref[b, CB:] = pick(here, (gate_ref, lanes, 0, 126, 2), (key_ref, lanes, 2, 126, 2), (value_ref, lanes, 4, 126, 2))


def later_kernel(docs_ref, base_ref, gate_ref, key_ref, value_ref, sf_ref, skip_ref, taps_ref,
                 out_ref, aux_ref, prod_ref, own_ref, ring_ref, sq_ref, masks, keeps, inner, acc):
    step = pl.program_id(0)

    @pl.when(step == 0)
    def _():
        pos, start = starts_row(docs_ref, base_ref[0], 512)
        rel = pos - base_ref[0]
        for lag in (1, 2):
            keeps[lag - 1] = as_bf((pos - lag >= start) & (rel >= lag), (GROUP, 512))
        inner[...] = as_bf(rel[:, :128] >= 2, (GROUP, 128))
        for j in range(3):
            first = start[:, 128 * (j + 1):128 * (j + 2)] - (base_ref[0] + 128 * (j + 1))
            masks[j, :128, :], masks[j, 128:, :] = tile_masks(jnp.broadcast_to(first, (128, 128)))
        acc[...] = jnp.zeros_like(acc)

    total = acc[...]
    for b in range(gate_ref.shape[0] // CB):
        here = slice(CB * b, CB * (b + 1))
        sf = sf_ref[:, :, here]
        cols = columns([sf[0], sf[1], sf[2], skip_ref[:, here]])
        taps = taps_ref[8 * b:8 * (b + 1)].astype(BF).astype(F32)
        for g in range(CB // GROUP):
            at = slice(CB * b + GROUP * g, CB * b + GROUP * (g + 1))
            c = cols[GROUP * g:GROUP * (g + 1)]
            product = (conv3(key_ref[at], keeps, c, 3) * conv3(value_ref[at], keeps, c, 6)).astype(BF)
            product = jnp.concatenate([product[:, :128] * inner[...], product[:, 128:]], axis=1)
            prod_ref[at] = product[:, :128]
            gate = conv3(gate_ref[at], keeps, c, 0)
            ring = ring_of(taps[g:g + 1])
            ring_ref[8 * b + g] = ring
            both = jnp.concatenate([ring, ring], axis=0)
            mixed = jnp.concatenate([
                jnp.dot(product[:, 128 * j:128 * j + 256], both * masks[j], preferred_element_type=F32)
                for j in range(3)], axis=1)
            mixed = mixed + c[:, 9:10] * product[:, 128:].astype(F32)
            gated = gate[:, 128:] * mixed
            aux_ref[at] = gate[:, :128]
            square = gated * gated
            total = total + square[:8] + square[8:]
            out_ref[at, 128:] = gated.astype(BF)
            out_ref[at, :128] = jnp.zeros((GROUP, 128), BF)
        tile0, tile1 = slice(0, 128), slice(128, 256)
        own_ref[b] = pick(here, (gate_ref, tile0, 0, 0, 2), (key_ref, tile0, 2, 0, 2), (value_ref, tile0, 4, 0, 2),
                          (gate_ref, tile0, 6, 126, 2), (gate_ref, tile1, 8, 0, 1))
    acc[...] = total

    @pl.when(step == pl.num_programs(0) - 1)
    def _():
        sq_ref[...] = jnp.sum(acc[...], axis=0, keepdims=True)


def first_kernel(docs_ref, base_ref, halo_ref, rows_ref, aux_ref, prod_ref, own_ref, ring_ref, later_ref, sf_ref, skip_ref,
                 taps_ref, out_ref, sq_ref, masks, keeps, acc):
    step = pl.program_id(0)

    @pl.when(step == 0)
    def _():
        pos, start = starts_row(docs_ref, base_ref[0], 256)
        for lag in (1, 2):
            keeps[lag - 1:lag] = (pos[:, :128] - lag >= start[:, :128]).astype(F32)
        for lag in (1, 2, 127):
            row = 1 + lag if lag < 3 else 4
            keeps[row:row + 1] = (pos[:, 128:] - lag >= start[:, 128:]).astype(F32)
        masks[:128], masks[128:] = tile_masks(jnp.broadcast_to(start[:, :128] - base_ref[0], (128, 128)))
        acc[...] = jnp.zeros_like(acc)

    lane = lax.broadcasted_iota(jnp.int32, (GROUP, 128), 1)
    one_hot = (lax.broadcasted_iota(jnp.int32, (16, 128), 0) == lane).astype(F32).astype(BF)
    total0, total1 = acc[0], acc[1]
    for b in range(halo_ref.shape[0]):
        here = slice(CB * b, CB * (b + 1))
        own = own_ref[b].astype(F32)
        past = halo_ref[b, CB:].astype(F32)

        def both_positions(i):
            t = [sf_ref[i, lag:lag + 1, here] for lag in range(3)]
            x = own[2 * i:2 * i + 2]
            h = past[2 * i:2 * i + 2]
            at0 = t[0] * x[:1] + keeps[0:1, 0:1] * (t[1] * h[1:]) + keeps[1:2, 0:1] * (t[2] * h[:1])
            at1 = t[0] * x[1:] + keeps[0:1, 1:2] * (t[1] * x[:1]) + keeps[1:2, 1:2] * (t[2] * h[1:])
            return jnp.concatenate([at0, at1], axis=0)

        two = (both_positions(1) * both_positions(2)).astype(BF).astype(F32)
        t = [sf_ref[0, lag:lag + 1, here] for lag in range(3)]
        gate = t[0] * own[8:9] + keeps[2:3, 0:1] * (t[1] * own[7:8]) + keeps[3:4, 0:1] * (t[2] * own[6:7])
        cols = columns([skip_ref[:, here], both_positions(0), keeps[4:5, 0:1] * two[1:] * gate])
        put = lax.dot_general(jnp.concatenate([two, jnp.zeros((14, CB), F32)], axis=0).astype(BF), one_hot,
                              (((0,), (0,)), ((), ())), preferred_element_type=F32)
        taps = taps_ref[8 * b:8 * (b + 1)].astype(BF).astype(F32)
        for g in range(CB // GROUP):
            at = slice(CB * b + GROUP * g, CB * b + GROUP * (g + 1))
            inside = slice(GROUP * g, GROUP * (g + 1))
            c = cols[inside]
            product = prod_ref[at] + put[inside].astype(BF)
            ring = ring_ref[8 * b + g]
            mixed = jnp.dot(jnp.concatenate([halo_ref[b, inside], product], axis=1),
                            jnp.concatenate([ring, ring], axis=0) * masks[...], preferred_element_type=F32)
            mixed = mixed + c[:, 0:1] * product.astype(F32)
            gated = jnp.where(lane == 0, c[:, 1:2], jnp.where(lane == 1, c[:, 2:3], aux_ref[at])) * mixed
            old = rows_ref[at, 128:].astype(F32)
            after = jnp.where(lane == 0, old + c[:, 3:4] * taps[g:g + 1, 127:128], old)
            square = gated * gated
            total0 = total0 + square[:8] + square[8:]
            square = after * after
            total1 = total1 + square[:8] + square[8:]
            out_ref[at, :128] = gated.astype(BF)
            out_ref[at, 128:] = after.astype(BF)
    acc[0], acc[1] = total0, total1

    @pl.when(step == pl.num_programs(0) - 1)
    def _():
        row0 = jnp.sum(acc[0], axis=0, keepdims=True)
        row1 = jnp.sum(acc[1], axis=0, keepdims=True)
        one = lax.broadcasted_iota(jnp.int32, (1, 128), 1)
        sq_ref[...] = jnp.concatenate(
            [row0, jnp.where(one == 0, row1, later_ref[:, :128]), later_ref[:, 128:]], axis=1)


def sf_spec(c):
    return pl.BlockSpec((3, 3, c), lambda i: (0, 0, i))


def tail(docs, base, gate, key, value, sf):
    ch, n = gate.shape
    c = min(BL, ch)
    wide = pl.BlockSpec((c, 256), lambda i: (i, n // 256 - 1))
    return pl.pallas_call(
        tail_kernel, grid=(ch // c,),
        in_specs=[SMEM, SMEM, wide, wide, wide, sf_spec(c)],
        out_specs=pl.BlockSpec((c // CB, ENDS, 128), lambda i: (i, 0, 0)),
        out_shape=jax.ShapeDtypeStruct((ch // CB, ENDS, 128), BF),
        scratch_shapes=[pltpu.VMEM((2, GROUP, 128), BF)],
        compiler_params=pltpu.CompilerParams(vmem_limit_bytes=BIG), name="tail",
    )(docs, base, gate, key, value, sf)


def param_specs(c):
    row = pl.BlockSpec((1, c), lambda i: (0, i))
    return [sf_spec(c), row, pl.BlockSpec((c // GROUP, MR), lambda i: (i, 0))]


def later(docs, base, gate, key, value, sf, skip, taps):
    ch, n = gate.shape
    c = min(BL, ch)
    wide = pl.BlockSpec((c, n), lambda i: (i, 0))
    tile = pl.BlockSpec((c, 128), lambda i: (i, 0))
    return pl.pallas_call(
        later_kernel, grid=(ch // c,),
        in_specs=[SMEM, SMEM, wide, wide, wide] + param_specs(c),
        out_specs=[wide, tile, tile, pl.BlockSpec((c // CB, 16, CB), lambda i: (i, 0, 0)),
                   pl.BlockSpec((c // GROUP, MR, MR), lambda i: (i, 0, 0)), pl.BlockSpec((1, n - 128), lambda i: (0, 0))],
        out_shape=[jax.ShapeDtypeStruct((ch, n), BF), jax.ShapeDtypeStruct((ch, 128), F32),
                   jax.ShapeDtypeStruct((ch, 128), BF), jax.ShapeDtypeStruct((ch // CB, 16, CB), BF),
                   jax.ShapeDtypeStruct((ch // GROUP, MR, MR), BF), jax.ShapeDtypeStruct((1, n - 128), F32)],
        scratch_shapes=[pltpu.VMEM((3, 256, 128), BF), pltpu.VMEM((2, GROUP, n), BF), pltpu.VMEM((GROUP, 128), BF),
                        pltpu.VMEM((8, n - 128), F32)],
        cost_estimate=pl.CostEstimate(flops=2 * ch * 384 * 256 * 8, bytes_accessed=8 * ch * n, transcendentals=0),
        compiler_params=pltpu.CompilerParams(vmem_limit_bytes=BIG), name="later",
    )(docs, base, gate, key, value, sf, skip, taps)


def first(docs, base, halo, done, sf, skip, taps):
    rows, aux, prod, own, rings, squares = done
    ch, n = rows.shape
    c = min(BL, ch)
    half = pl.BlockSpec((c, 256), lambda i: (i, 0))
    tile = pl.BlockSpec((c, 128), lambda i: (i, 0))
    whole = lambda w: pl.BlockSpec((1, w), lambda i: (0, 0))
    return pl.pallas_call(
        first_kernel, grid=(ch // c,),
        in_specs=[SMEM, SMEM, pl.BlockSpec((c // CB, ENDS, 128), lambda i: (i, 0, 0)), half, tile, tile,
                  pl.BlockSpec((c // CB, 16, CB), lambda i: (i, 0, 0)),
                  pl.BlockSpec((c // GROUP, MR, MR), lambda i: (i, 0, 0)), whole(n - 128)] + param_specs(c),
        out_specs=[half, whole(n)],
        out_shape=[jax.ShapeDtypeStruct((ch, n), BF), jax.ShapeDtypeStruct((1, n), F32)],
        scratch_shapes=[pltpu.VMEM((256, 128), BF), pltpu.VMEM((8, 128), F32), pltpu.VMEM((2, 8, 128), F32)],
        input_output_aliases={3: 0},
        cost_estimate=pl.CostEstimate(flops=2 * ch * 128 * 256 * 8, bytes_accessed=4 * ch * n, transcendentals=0),
        compiler_params=pltpu.CompilerParams(vmem_limit_bytes=FIRST_VMEM), name="first",
    )(docs, base, halo, rows, aux, prod, own, rings, squares, sf, skip, taps)


FIRST_VMEM = 56 << 20
def final_kernel(recv_ref, sums_ref, gain_ref, out_ref):
    per, c, n = recv_ref.shape
    gain = jnp.broadcast_to(gain_ref[...], (c, n))
    for i in range(per):
        scale = lax.rsqrt(sums_ref[i] / D + EPS)
        out_ref[:, n * i:n * (i + 1)] = (recv_ref[i].astype(F32) * scale * gain).astype(BF)


def final(recv, sums, gain):
    k, c, n = recv.shape
    per = min(k, PER)
    return pl.pallas_call(
        final_kernel, grid=(k // per,),
        in_specs=[pl.BlockSpec((per, c, n), lambda i: (i, 0, 0)), pl.BlockSpec((per, 1, n), lambda i: (i, 0, 0)),
                  pl.BlockSpec((c, 1), lambda i: (0, 0))],
        out_specs=pl.BlockSpec((c, per * n), lambda i: (0, i)),
        out_shape=jax.ShapeDtypeStruct((c, k * n), BF),
        compiler_params=pltpu.CompilerParams(vmem_limit_bytes=24 << 20), name="settle",
    )(recv, sums, gain)


ROUNDS = (((0, 1), (2, 3), (4, 5), (6, 7)), ((1, 2), (3, 4), (5, 6), (7, 0)), ((0, 3), (7, 4), (1, 6), (2, 5)))


def channel_sum(x):
    if lax.axis_size("ch") != 8:
        return lax.psum(x, "ch")
    for pairs in ROUNDS:
        x = x + lax.ppermute(x, "ch", list(pairs) + [(b, a) for a, b in pairs])
    return x


def local(gate, key, value, sf, taps, skip, gain, docs):
    place = lax.axis_index("ctx")
    width = lax.axis_size("ctx")
    ch, n = gate.shape
    base = (place * n).astype(jnp.int32).reshape(1)
    skip = skip.reshape(1, ch)
    gain = lax.dynamic_slice_in_dim(gain, place * (ch // width), ch // width).reshape(ch // width, 1)
    ends = tail(docs, base, gate, key, value, sf)
    halo = lax.ppermute(ends, "ctx", [(i, i + 1) for i in range(width - 1)])
    done = later(docs, base, gate, key, value, sf, skip, taps)
    rows, squares = first(docs, base, halo, done, sf, skip, taps)
    recv = lax.all_to_all(rows.reshape(width, ch // width, n), "ctx", split_axis=0, concat_axis=0, tiled=True)
    total = channel_sum(squares)
    total, recv = lax.optimization_barrier((total, recv))
    sums = lax.all_to_all(jnp.broadcast_to(total[None], (width, 1, n)), "ctx", split_axis=0, concat_axis=0, tiled=True)
    return final(recv, sums, gain)


def solution(mesh):
    in_specs = (P("ch", "ctx"),) * 3 + (P(None, None, "ch"), P("ch", None), P("ch"), P("ch"), P())
    return jax.shard_map(local, mesh=mesh, in_specs=in_specs, out_specs=P(("ch", "ctx"), None), check_vma=False)
```

time: 65.4 us -> 63.4 us (0.969)
  blocking collectives: 14.3 us -> 0 us
  waiting for transfers between devices: 7.87 us -> 15.1 us
  starting transfers between devices: 20.5 us -> 27.5 us
  Pallas kernels: 21.6 us -> 18.9 us
  local copies, waits for them, and re-layouts: 0.75 us -> 1.56 us
    all_to_all x1 -> x0, blocking collectives: 14.3 us -> none  [local(): lax.all_to_all(jnp.broadcast_to(total[None], (width, 1, n)), 'ctx', split...]
    all_to_all x0 -> x1, waiting for transfers between devices: none -> 7.19 us  [local(): lax.all_to_all(jnp.broadcast_to(total[None], (width, 1, n)), 'ctx', split...]
    all_to_all x0 -> x1, starting transfers between devices: none -> 6.97 us  [local(): lax.all_to_all(jnp.broadcast_to(total[None], (width, 1, n)), 'ctx', split...]
    pallas_call x2, Pallas kernels: 15.6 us -> 14 us  [the longest x1 8.96 us: later(): pl.pallas_call(later_kernel, grid=(ch // c,), in_specs=[SMEM, SMEM, wide,...]
    pallas_call x1, Pallas kernels: 2.12 us -> 1.12 us  [final(): pl.pallas_call(final_kernel, grid=(k // per,), in_specs=[pl.BlockSpec((pe...]
  transfers between devices with their start and end apart: 5 -> 6, of which waited for: 4 -> 5; matrix products, arithmetic and copies ran while one was open for 0% -> 0% of each run, Pallas kernels for 11% -> 14%
where the time goes in v4:
time: 63.4 us; the launch traced here: 63.1 us
  starting transfers between devices  27.5 us (43%)
  Pallas kernels  18.9 us (30%)
  waiting for transfers between devices  15.1 us (24%)
  local copies, waits for them, and re-layouts  1.56 us (2%)
    ppermute x3, starting transfers between devices, channel_sum(): x = x + lax.ppermute(x, 'ch', list(pairs) + [(b, a) for a, b in pairs])  9.01 us
    pallas_call x1, Pallas kernels, later(): pl.pallas_call(later_kernel, grid=(ch // c,), in_specs=[SMEM, SMEM, wide,...  8.96 us
    all_to_all x1, waiting for transfers between devices, local(): lax.all_to_all(jnp.broadcast_to(total[None], (width, 1, n)), 'ctx', split...  7.19 us
    all_to_all x1, starting transfers between devices, local(): lax.all_to_all(jnp.broadcast_to(total[None], (width, 1, n)), 'ctx', split...  6.97 us
    all_to_all x1, starting transfers between devices, local(): lax.all_to_all(rows.reshape(width, ch // width, n), 'ctx', split_axis=0,...  6.92 us
    pallas_call x1, Pallas kernels, first(): pl.pallas_call(first_kernel, grid=(ch // c,), in_specs=[SMEM, SMEM, pl.Bl...  5.03 us
    ppermute x3, waiting for transfers between devices, channel_sum(): x = x + lax.ppermute(x, 'ch', list(pairs) + [(b, a) for a, b in pairs])  4.9 us
    ppermute x1, starting transfers between devices, local(): halo = lax.ppermute(ends, 'ctx', [(i, i + 1) for i in range(width - 1)])  4.58 us
  transfers between devices with their start and end apart: 6, of which 5 were waited for; matrix products, arithmetic and copies ran while one was open for 0% of the time, Pallas kernels for 14%

profile of v4, /device:TPU:1, one launch (start us, length us, event | category | flops | bytes accessed | tf_op | source)
XLA Modules:
  0.0 63.1 jit_solution(3486386834310211328)
XLA Ops:
  0.0 0.0 copy-start
  0.0 3.8 %tail.1 = bf16[8,144,128]{2,1,0:T(8,128)(2,1)} custom-call(s32[64]{0:T(128)} %docs_ref.5, s32[1]{0:T(128)} %bitcast.base_ref, bf16[1024,512]{1,0:T(8,128)(2,1)} %gate_ref.3, bf16[1024,512]{1,0:T(8,128)(2,1)} %key_ref.3, bf16[1024,512]{1,0:T(8,128)(2,1)} %value_ref.3, f32[3,3,1024]{2,1,0:T(4,128)} %sf_ref.5), custom_call_target="tpu_custom_call" | custom-call | tf_op jit(solution)/shard_map/tail/pallas_call | solution.py:224
  3.8 4.6 %collective-permute-start = (bf16[8,144,128]{2,1,0:T(8,128)(2,1)}, bf16[8,144,128]{2,1,0:T(8,128)(2,1)S(1)}, u32[]{:S(2)}, u32[]{:S(2)}) collective-permute-start(bf16[8,144,128]{2,1,0:T(8,128)(2,1)} %tail.1), channel_id=1, source_target_pairs={{0,8},{8,16},{16,24},{24,32},{32,40},{40,48},{48,56},{56,64},{64,7... | collective-permute-start | bytes 884744 | tf_op jit(solution)/shard_map/ppermute | solution.py:321
  8.4 9.0 %later.1 = (bf16[1024,512]{1,0:T(8,128)(2,1)}, f32[1024,128]{1,0:T(8,128)}, bf16[1024,128]{1,0:T(8,128)(2,1)}, bf16[8,16,128]{2,1,0:T(8,128)(2,1)}, bf16[64,128,128]{2,1,0:T(8,128)(2,1)}, /*index=5*/f32[1,384]{1,0:T(1,128)}) custom-call(s32[64]{0:T(128)} %docs_ref.5, s32[1]{0:T(128)} %bitcast.base_ref, bf16[1024,512]{1,0:T(8,128)(2,1)} %gate_ref.3, ...), custom_call_target="tpu_custom_call" | custom-call | flops 1610612736 | bytes 4194304 | tf_op jit(solution)/shard_map/later/pallas_call | solution.py:244
  17.4 0.0 collective-permute-done.halo_ref
  17.4 0.0 copy-start.1
  17.4 0.7 %copy-done.1 = bf16[8,144,128]{2,1,0:T(8,128)(2,1)} copy-done((bf16[8,144,128]{2,1,0:T(8,128)(2,1)}, bf16[8,144,128]{2,1,0:T(8,128)(2,1)S(1)}, u32[]{:S(2)}) %copy-start.1) | copy-done | bytes 294936
  18.1 5.0 %first.1 = (bf16[1024,512]{1,0:T(8,128)(2,1)}, f32[1,512]{1,0:T(1,128)}) custom-call(s32[64]{0:T(128)} %docs_ref.5, s32[1]{0:T(128)} %bitcast.base_ref, bf16[8,144,128]{2,1,0:T(8,128)(2,1)} %copy-done.1, bf16[1024,512]{1,0:T(8,128)(2,1)} %get-tuple-element.15.rows_ref, f32[1024,128]{1,0:T(8,128)} %get-tuple-element.16.aux_ref, ...), custom_call_target="tpu_custom_call", output_to_operand_aliasing={{0}: (3, {})} | custom-call | flops 536870912 | bytes 2097152 | tf_op jit(solution)/shard_map/first/pallas_call | solution.py:266
  23.1 0.0 copy-start.2
  23.1 6.9 %all-to-all-start = ((bf16[32,32,512]{2,1,0:T(8,128)(2,1)}), bf16[32,32,512]{2,1,0:T(8,128)(2,1)S(1)}, u32[]{:S(2)}, u32[]{:S(2)}) async-start(bf16[32,32,512]{2,1,0:T(8,128)(2,1)} %bitcast.6), calls=%async_computation | async-start | bytes 2097152 | tf_op jit(solution)/shard_map/all_to_all | solution.py:324
  30.1 0.0 copy-done.2
  30.1 1.7 %collective-permute-start.1 = (f32[1,512]{1,0:T(1,128)S(1)}, f32[1,512]{1,0:T(1,128)S(1)}, u32[]{:S(2)}, u32[]{:S(2)}) collective-permute-start(f32[1,512]{1,0:T(1,128)S(1)} %copy-done.2), channel_id=1, source_target_pairs={{0,1},{2,3},{4,5},{6,7},{1,0},{3,2},{5,4},{7,6},{8,9},{10,11},{12,... | collective-permute-start | bytes 6152 | tf_op jit(solution)/shard_map/ppermute | solution.py:309
  31.8 1.3 %collective-permute-done.1 = f32[1,512]{1,0:T(1,128)S(1)} collective-permute-done((f32[1,512]{1,0:T(1,128)S(1)}, f32[1,512]{1,0:T(1,128)S(1)}, u32[]{:S(2)}, u32[]{:S(2)}) %collective-permute-start.1) | collective-permute-done | bytes 2080 | tf_op jit(solution)/shard_map/ppermute | solution.py:309
  33.1 5.4 %collective-permute-start.2 = (f32[1,512]{1,0:T(1,128)S(1)}, f32[1,512]{1,0:T(1,128)S(1)}, u32[]{:S(2)}, u32[]{:S(2)}) collective-permute-start(f32[1,512]{1,0:T(1,128)S(1)} %add.12), channel_id=1, source_target_pairs={{1,2},{3,4},{5,6},{7,0},{2,1},{4,3},{6,5},{0,7},{9,10},{11,12},{13... | collective-permute-start | bytes 6152 | tf_op jit(solution)/shard_map/ppermute | solution.py:309
  38.5 1.0 %collective-permute-done.2 = f32[1,512]{1,0:T(1,128)S(1)} collective-permute-done((f32[1,512]{1,0:T(1,128)S(1)}, f32[1,512]{1,0:T(1,128)S(1)}, u32[]{:S(2)}, u32[]{:S(2)}) %collective-permute-start.2) | collective-permute-done | bytes 2080 | tf_op jit(solution)/shard_map/ppermute | solution.py:309
  39.5 1.9 %collective-permute-start.3 = (f32[1,512]{1,0:T(1,128)S(1)}, f32[1,512]{1,0:T(1,128)S(1)}, u32[]{:S(2)}, u32[]{:S(2)}) collective-permute-start(f32[1,512]{1,0:T(1,128)S(1)} %add.13), channel_id=1, source_target_pairs={{0,3},{7,4},{1,6},{2,5},{3,0},{4,7},{6,1},{5,2},{8,11},{15,12},{9,... | collective-permute-start | bytes 6152 | tf_op jit(solution)/shard_map/ppermute | solution.py:309
  41.4 2.6 %collective-permute-done.3 = f32[1,512]{1,0:T(1,128)S(1)} collective-permute-done((f32[1,512]{1,0:T(1,128)S(1)}, f32[1,512]{1,0:T(1,128)S(1)}, u32[]{:S(2)}, u32[]{:S(2)}) %collective-permute-start.3) | collective-permute-done | bytes 2080 | tf_op jit(solution)/shard_map/ppermute | solution.py:309
  44.0 3.0 %all-to-all-done.recv_ref = bf16[32,32,512]{2,1,0:T(8,128)(2,1)S(1)} async-done(((bf16[32,32,512]{2,1,0:T(8,128)(2,1)}), bf16[32,32,512]{2,1,0:T(8,128)(2,1)S(1)}, u32[]{:S(2)}, u32[]{:S(2)}) %all-to-all-start) | async-done | bytes 1048608 | tf_op jit(solution)/shard_map/all_to_all | solution.py:324
  47.0 0.7 %broadcast_in_dim.9 = f32[32,1,512]{2,1,0:T(1,128)} broadcast(f32[512]{0:T(512)S(1)} %bitcast.7), dimensions={2} | broadcast | bytes 67584 | tf_op jit(solution)/shard_map/broadcast_in_dim | solution.py:327
  47.6 7.0 %all-to-all-start.1 = ((f32[32,1,512]{2,1,0:T(1,128)}), f32[32,1,512]{2,1,0:T(1,128)S(1)}, u32[]{:S(2)}, u32[]{:S(2)}) async-start(f32[32,1,512]{2,1,0:T(1,128)} %broadcast_in_dim.9), calls=%async_computation.1 | async-start | bytes 131072 | tf_op jit(solution)/shard_map/all_to_all | solution.py:327
  54.6 0.0 copy-done
  54.6 0.1 dynamic-slice_bitcast_fusion
  54.7 0.1 copy.10.gain_ref
  54.8 7.2 %all-to-all-done.1.sums_ref = f32[32,1,512]{2,1,0:T(1,128)S(1)} async-done(((f32[32,1,512]{2,1,0:T(1,128)}), f32[32,1,512]{2,1,0:T(1,128)S(1)}, u32[]{:S(2)}, u32[]{:S(2)}) %all-to-all-start.1) | async-done | bytes 65568 | tf_op jit(solution)/shard_map/all_to_all | solution.py:327
  62.0 1.1 %settle.1 = bf16[32,16384]{1,0:T(8,128)(2,1)} custom-call(bf16[32,32,512]{2,1,0:T(8,128)(2,1)S(1)} %all-to-all-done.recv_ref, f32[32,1,512]{2,1,0:T(1,128)S(1)} %all-to-all-done.1.sums_ref, f32[32,1]{1,0:T(8,128)S(1)} %copy.10.gain_ref), custom_call_target="tpu_custom_call" | custom-call | tf_op jit(solution)/shard_map/settle/pallas_call | solution.py:292
  (3 shorter events, 0.0 us)
Async XLA Ops:
  0.0 54.6 %copy-start = (f32[1024]{0:T(1024)S(1)}, f32[1024]{0:T(1024)}, u32[]{:S(2)}) copy-start(f32[1024]{0:T(1024)} %param.14) | copy-start | bytes 12292
  3.8 13.6 %collective-permute-start = (bf16[8,144,128]{2,1,0:T(8,128)(2,1)}, bf16[8,144,128]{2,1,0:T(8,128)(2,1)S(1)}, u32[]{:S(2)}, u32[]{:S(2)}) collective-permute-start(bf16[8,144,128]{2,1,0:T(8,128)(2,1)} %tail.1), channel_id=1, source_target_pairs={{0,8},{8,16},{16,24},{24,32},{32,40},{40,48},{48,56},{56,64},{64,7... | collective-permute-start | bytes 884744 | tf_op jit(solution)/shard_map/ppermute | solution.py:321
  17.4 0.7 %copy-start.1 = (bf16[8,144,128]{2,1,0:T(8,128)(2,1)}, bf16[8,144,128]{2,1,0:T(8,128)(2,1)S(1)}, u32[]{:S(2)}) copy-start(bf16[8,144,128]{2,1,0:T(8,128)(2,1)S(1)} %collective-permute-done.halo_ref) | copy-start | bytes 884740
  23.1 6.9 %copy-start.2 = (f32[1,512]{1,0:T(1,128)S(1)}, f32[1,512]{1,0:T(1,128)}, u32[]{:S(2)}) copy-start(f32[1,512]{1,0:T(1,128)} %get-tuple-element.21) | copy-start | bytes 6148
  23.1 23.8 %all-to-all-start = ((bf16[32,32,512]{2,1,0:T(8,128)(2,1)}), bf16[32,32,512]{2,1,0:T(8,128)(2,1)S(1)}, u32[]{:S(2)}, u32[]{:S(2)}) async-start(bf16[32,32,512]{2,1,0:T(8,128)(2,1)} %bitcast.6), calls=%async_computation | async-start | bytes 2097152 | tf_op jit(solution)/shard_map/all_to_all | solution.py:324
  30.1 3.0 %collective-permute-start.1 = (f32[1,512]{1,0:T(1,128)S(1)}, f32[1,512]{1,0:T(1,128)S(1)}, u32[]{:S(2)}, u32[]{:S(2)}) collective-permute-start(f32[1,512]{1,0:T(1,128)S(1)} %copy-done.2), channel_id=1, source_target_pairs={{0,1},{2,3},{4,5},{6,7},{1,0},{3,2},{5,4},{7,6},{8,9},{10,11},{12,... | collective-permute-start | bytes 6152 | tf_op jit(solution)/shard_map/ppermute | solution.py:309
  33.1 6.4 %collective-permute-start.2 = (f32[1,512]{1,0:T(1,128)S(1)}, f32[1,512]{1,0:T(1,128)S(1)}, u32[]{:S(2)}, u32[]{:S(2)}) collective-permute-start(f32[1,512]{1,0:T(1,128)S(1)} %add.12), channel_id=1, source_target_pairs={{1,2},{3,4},{5,6},{7,0},{2,1},{4,3},{6,5},{0,7},{9,10},{11,12},{13... | collective-permute-start | bytes 6152 | tf_op jit(solution)/shard_map/ppermute | solution.py:309
  39.5 4.5 %collective-permute-start.3 = (f32[1,512]{1,0:T(1,128)S(1)}, f32[1,512]{1,0:T(1,128)S(1)}, u32[]{:S(2)}, u32[]{:S(2)}) collective-permute-start(f32[1,512]{1,0:T(1,128)S(1)} %add.13), channel_id=1, source_target_pairs={{0,3},{7,4},{1,6},{2,5},{3,0},{4,7},{6,1},{5,2},{8,11},{15,12},{9,... | collective-permute-start | bytes 6152 | tf_op jit(solution)/shard_map/ppermute | solution.py:309
  47.6 14.3 %all-to-all-start.1 = ((f32[32,1,512]{2,1,0:T(1,128)}), f32[32,1,512]{2,1,0:T(1,128)S(1)}, u32[]{:S(2)}, u32[]{:S(2)}) async-start(f32[32,1,512]{2,1,0:T(1,128)} %broadcast_in_dim.9), calls=%async_computation.1 | async-start | bytes 131072 | tf_op jit(solution)/shard_map/all_to_all | solution.py:327

commit v5 on v4

--- a/solution.py
+++ b/solution.py
@@ -40,16 +40,31 @@
     return (((s > t) & (s - 128 >= first)).astype(F32).astype(BF), ((s <= t) & (s >= first)).astype(F32).astype(BF))
 
 
-def columns(rows):
-    rows = rows + [jnp.zeros((16 - sum(r.shape[0] for r in rows), CB), F32)]
-    return jnp.concatenate(rows, axis=0).T
+def spread(rows):
+    count = sum(r.shape[0] for r in rows)
+    rest = jnp.concatenate(rows + [jnp.zeros((16 - count, CB), F32)], axis=0)
+    pieces = []
+    for _ in range(3):
+        pieces.append(rest.astype(BF))
+        rest = rest - pieces[-1].astype(F32)
+    row = lax.broadcasted_iota(jnp.int32, (16, 128 * count), 0)
+    column = lax.broadcasted_iota(jnp.int32, (16, 128 * count), 1)
+    ones = ((column >= 128 * row) & (column < 128 * row + 128)).astype(F32).astype(BF)
+    return lax.dot_general(jnp.concatenate(pieces, axis=0), jnp.concatenate([ones] * 3, axis=0),
+                           (((0,), (0,)), ((), ())), preferred_element_type=F32)
+
+
+def lanes_of(wide, i, tiles=1):
+    part = wide[:, 128 * i:128 * (i + 1)]
+    return part if tiles == 1 else jnp.concatenate([part] * tiles, axis=1)
 
 
 def conv3(raw, keeps, cols, first):
     one = pltpu.roll(raw, 1, 1) * keeps[0]
     two = pltpu.roll(raw, 2, 1) * keeps[1]
-    return (cols[:, first:first + 1] * raw.astype(F32) + cols[:, first + 1:first + 2] * one.astype(F32)
-            + cols[:, first + 2:first + 3] * two.astype(F32))
+    k = raw.shape[1] // 128
+    return (lanes_of(cols, first, k) * raw.astype(F32) + lanes_of(cols, first + 1, k) * one.astype(F32)
+            + lanes_of(cols, first + 2, k) * two.astype(F32))
 
 
 def ring_of(taps):
@@ -79,13 +94,13 @@
         raw = ref[at, 128:]
         one = pltpu.roll(raw, 1, 1) * keeps[0]
         two = pltpu.roll(jnp.where(last, ref[at, :128], raw), 2, 1) * keeps[1]
-        return (cols[:, i:i + 1] * raw.astype(F32) + cols[:, i + 1:i + 2] * one.astype(F32)
-                + cols[:, i + 2:i + 3] * two.astype(F32))
+        return (lanes_of(cols, i) * raw.astype(F32) + lanes_of(cols, i + 1) * one.astype(F32)
+                + lanes_of(cols, i + 2) * two.astype(F32))
 
     for b in range(gate_ref.shape[0] // CB):
         here = slice(CB * b, CB * (b + 1))
         sf = sf_ref[:, :, here]
-        cols = columns([sf[1], sf[2]])
+        cols = spread([sf[1], sf[2]])
         for g in range(CB // GROUP):
             at = slice(CB * b + GROUP * g, CB * b + GROUP * (g + 1))
             c = cols[GROUP * g:GROUP * (g + 1)]
@@ -114,7 +129,7 @@
     for b in range(gate_ref.shape[0] // CB):
         here = slice(CB * b, CB * (b + 1))
         sf = sf_ref[:, :, here]
-        cols = columns([sf[0], sf[1], sf[2], skip_ref[:, here]])
+        cols = spread([sf[0], sf[1], sf[2], skip_ref[:, here]])
         taps = taps_ref[8 * b:8 * (b + 1)].astype(BF).astype(F32)
         for g in range(CB // GROUP):
             at = slice(CB * b + GROUP * g, CB * b + GROUP * (g + 1))
@@ -129,7 +144,7 @@
             mixed = jnp.concatenate([
                 jnp.dot(product[:, 128 * j:128 * j + 256], both * masks[j], preferred_element_type=F32)
                 for j in range(3)], axis=1)
-            mixed = mixed + c[:, 9:10] * product[:, 128:].astype(F32)
+            mixed = mixed + lanes_of(c, 9, 3) * product[:, 128:].astype(F32)
             gated = gate[:, 128:] * mixed
             aux_ref[at] = gate[:, :128]
             square = gated * gated
@@ -180,7 +195,7 @@
         two = (both_positions(1) * both_positions(2)).astype(BF).astype(F32)
         t = [sf_ref[0, lag:lag + 1, here] for lag in range(3)]
         gate = t[0] * own[8:9] + keeps[2:3, 0:1] * (t[1] * own[7:8]) + keeps[3:4, 0:1] * (t[2] * own[6:7])
-        cols = columns([skip_ref[:, here], both_positions(0), keeps[4:5, 0:1] * two[1:] * gate])
+        cols = spread([skip_ref[:, here], both_positions(0), keeps[4:5, 0:1] * two[1:] * gate])
         put = lax.dot_general(jnp.concatenate([two, jnp.zeros((14, CB), F32)], axis=0).astype(BF), one_hot,
                               (((0,), (0,)), ((), ())), preferred_element_type=F32)
         taps = taps_ref[8 * b:8 * (b + 1)].astype(BF).astype(F32)
@@ -192,10 +207,10 @@
             ring = ring_ref[8 * b + g]
             mixed = jnp.dot(jnp.concatenate([halo_ref[b, inside], product], axis=1),
                             jnp.concatenate([ring, ring], axis=0) * masks[...], preferred_element_type=F32)
-            mixed = mixed + c[:, 0:1] * product.astype(F32)
-            gated = jnp.where(lane == 0, c[:, 1:2], jnp.where(lane == 1, c[:, 2:3], aux_ref[at])) * mixed
+            mixed = mixed + lanes_of(c, 0) * product.astype(F32)
+            gated = jnp.where(lane == 0, lanes_of(c, 1), jnp.where(lane == 1, lanes_of(c, 2), aux_ref[at])) * mixed
             old = rows_ref[at, 128:].astype(F32)
-            after = jnp.where(lane == 0, old + c[:, 3:4] * taps[g:g + 1, 127:128], old)
+            after = jnp.where(lane == 0, old + lanes_of(c, 3) * taps[g:g + 1, 127:128], old)
             square = gated * gated
             total0 = total0 + square[:8] + square[8:]
             square = after * after
@@ -257,6 +272,7 @@
 
 
 def first(docs, base, halo, done, sf, skip, taps):
+    done = [pltpu.with_memory_space_constraint(x, pltpu.HBM) for x in done]
     rows, aux, prod, own, rings, squares = done
     ch, n = rows.shape
     c = min(BL, ch)
@@ -277,7 +293,7 @@
     )(docs, base, halo, rows, aux, prod, own, rings, squares, sf, skip, taps)
 
 
-FIRST_VMEM = 56 << 20
+FIRST_VMEM = 24 << 20
 def final_kernel(recv_ref, sums_ref, gain_ref, out_ref):
     per, c, n = recv_ref.shape
     gain = jnp.broadcast_to(gain_ref[...], (c, n))
@@ -304,10 +320,10 @@
 
 def channel_sum(x):
     if lax.axis_size("ch") != 8:
-        return lax.psum(x, "ch")
-    for pairs in ROUNDS:
+        return lax.psum(x, "ch"), jnp.zeros_like(x)
+    for pairs in ROUNDS[:-1]:
         x = x + lax.ppermute(x, "ch", list(pairs) + [(b, a) for a, b in pairs])
-    return x
+    return x, lax.ppermute(x, "ch", list(ROUNDS[-1]) + [(b, a) for a, b in ROUNDS[-1]])
 
 
 def local(gate, key, value, sf, taps, skip, gain, docs):
@@ -322,9 +338,9 @@
     done = later(docs, base, gate, key, value, sf, skip, taps)
     rows, squares = first(docs, base, halo, done, sf, skip, taps)
     recv = lax.all_to_all(rows.reshape(width, ch // width, n), "ctx", split_axis=0, concat_axis=0, tiled=True)
-    total = channel_sum(squares)
-    total, recv = lax.optimization_barrier((total, recv))
-    sums = lax.all_to_all(jnp.broadcast_to(total[None], (width, 1, n)), "ctx", split_axis=0, concat_axis=0, tiled=True)
+    near, far = channel_sum(squares)
+    far, recv = lax.optimization_barrier((far, recv))
+    sums = lax.all_to_all(jnp.broadcast_to((near + far)[None], (width, 1, n)), "ctx", split_axis=0, concat_axis=0, tiled=True)
     return final(recv, sums, gain)
 
 

time: 63.4 us -> 61.4 us (0.968)
  Pallas kernels: 18.9 us -> 17.5 us
  local copies, waits for them, and re-layouts: 1.56 us -> 0.87 us
    ppermute x0 -> x1, waiting for transfers between devices: none -> 2.65 us  [channel_sum(): lax.ppermute(x, 'ch', list(ROUNDS[-1]) + [(b, a) for a, b in ROUNDS[-1]])]
    ppermute x3 -> x2, waiting for transfers between devices: 4.9 us -> 2.28 us  [channel_sum(): x = x + lax.ppermute(x, 'ch', list(pairs) + [(b, a) for a, b in pairs])]
    ppermute x3 -> x2, starting transfers between devices: 9.01 us -> 7.12 us  [channel_sum(): x = x + lax.ppermute(x, 'ch', list(pairs) + [(b, a) for a, b in pairs])]
    ppermute x0 -> x1, starting transfers between devices: none -> 1.88 us  [channel_sum(): lax.ppermute(x, 'ch', list(ROUNDS[-1]) + [(b, a) for a, b in ROUNDS[-1]])]
    pallas_call x1, Pallas kernels: 3.83 us -> 2.92 us  [tail(): pl.pallas_call(tail_kernel, grid=(ch // c,), in_specs=[SMEM, SMEM, wide,...]
    unnamed x6 -> x10, local copies, waits for them, and re-layouts: 0.72 us -> 0.03 us
where the time goes in v5:
time: 61.4 us; the launch traced here: 61.1 us
  starting transfers between devices  27.4 us (45%)
  Pallas kernels  17.5 us (29%)
  waiting for transfers between devices  15.1 us (25%)
  local copies, waits for them, and re-layouts  0.87 us (1%)
    pallas_call x1, Pallas kernels, later(): pl.pallas_call(later_kernel, grid=(ch // c,), in_specs=[SMEM, SMEM, wide,...  8.73 us
    all_to_all x1, waiting for transfers between devices, local(): lax.all_to_all(jnp.broadcast_to((near + far)[None], (width, 1, n)), 'ctx'...  7.19 us
    ppermute x2, starting transfers between devices, channel_sum(): x = x + lax.ppermute(x, 'ch', list(pairs) + [(b, a) for a, b in pairs])  7.12 us
    all_to_all x1, starting transfers between devices, local(): lax.all_to_all(jnp.broadcast_to((near + far)[None], (width, 1, n)), 'ctx'...  6.95 us
    all_to_all x1, starting transfers between devices, local(): lax.all_to_all(rows.reshape(width, ch // width, n), 'ctx', split_axis=0,...  6.9 us
    pallas_call x1, Pallas kernels, first(): pl.pallas_call(first_kernel, grid=(ch // c,), in_specs=[SMEM, SMEM, pl.Bl...  4.76 us
    ppermute x1, starting transfers between devices, local(): halo = lax.ppermute(ends, 'ctx', [(i, i + 1) for i in range(width - 1)])  4.58 us
    all_to_all x1, waiting for transfers between devices, local(): lax.all_to_all(rows.reshape(width, ch // width, n), 'ctx', split_axis=0,...  2.98 us
  transfers between devices with their start and end apart: 6, of which 5 were waited for; matrix products, arithmetic and copies ran while one was open for 0% of the time, Pallas kernels for 14%

profile of v5, /device:TPU:1, one launch (start us, length us, event | category | flops | bytes accessed | tf_op | source)
XLA Modules:
  0.0 61.1 jit_solution(12729641088384185518)
XLA Ops:
  0.0 0.0 copy-start
  0.0 2.9 %tail.1 = bf16[8,144,128]{2,1,0:T(8,128)(2,1)} custom-call(s32[64]{0:T(128)} %docs_ref.5, s32[1]{0:T(128)} %bitcast.base_ref, bf16[1024,512]{1,0:T(8,128)(2,1)} %gate_ref.3, bf16[1024,512]{1,0:T(8,128)(2,1)} %key_ref.3, bf16[1024,512]{1,0:T(8,128)(2,1)} %value_ref.3, f32[3,3,1024]{2,1,0:T(4,128)} %sf_ref.5), custom_call_target="tpu_custom_call" | custom-call | tf_op jit(solution)/shard_map/tail/pallas_call | solution.py:239
  2.9 4.6 %collective-permute-start = (bf16[8,144,128]{2,1,0:T(8,128)(2,1)}, bf16[8,144,128]{2,1,0:T(8,128)(2,1)S(1)}, u32[]{:S(2)}, u32[]{:S(2)}) collective-permute-start(bf16[8,144,128]{2,1,0:T(8,128)(2,1)} %tail.1), channel_id=1, source_target_pairs={{0,8},{8,16},{16,24},{24,32},{32,40},{40,48},{48,56},{56,64},{64,7... | collective-permute-start | bytes 884744 | tf_op jit(solution)/shard_map/ppermute | solution.py:337
  7.5 0.0 copy-start.1
  7.5 0.0 copy-start.2
  7.5 0.0 copy-start.3
  7.6 0.0 copy-start.4
  7.6 8.7 %later.1 = (bf16[1024,512]{1,0:T(8,128)(2,1)}, f32[1024,128]{1,0:T(8,128)}, bf16[1024,128]{1,0:T(8,128)(2,1)}, bf16[8,16,128]{2,1,0:T(8,128)(2,1)}, bf16[64,128,128]{2,1,0:T(8,128)(2,1)}, /*index=5*/f32[1,384]{1,0:T(1,128)}) custom-call(s32[64]{0:T(128)} %docs_ref.5, s32[1]{0:T(128)} %bitcast.base_ref, bf16[1024,512]{1,0:T(8,128)(2,1)} %gate_ref.3, ...), custom_call_target="tpu_custom_call" | custom-call | flops 1610612736 | bytes 4194304 | tf_op jit(solution)/shard_map/later/pallas_call | solution.py:259
  16.3 0.0 collective-permute-done.halo_ref
  16.3 0.0 copy-done.1
  16.3 0.0 copy-done.2
  16.3 0.0 copy-done.3
  16.3 0.0 copy-done.4
  16.3 4.8 %first.1 = (bf16[1024,512]{1,0:T(8,128)(2,1)}, f32[1,512]{1,0:T(1,128)S(1)}) custom-call(s32[64]{0:T(128)S(1)} %copy-done.4, s32[1]{0:T(128)} %bitcast.base_ref, bf16[8,144,128]{2,1,0:T(8,128)(2,1)S(1)} %collective-permute-done.halo_ref, bf16[1024,512]{1,0:T(8,128)(2,1)} %get-tuple-element.15.rows_ref, ...), custom_call_target="tpu_custom_call", output_to_operand_aliasing={{0}: (3, {})} | custom-call | flops 536870912 | bytes 2097152 | tf_op jit(solution)/shard_map/first/pallas_call | solution.py:282
  21.1 6.9 %all-to-all-start = ((bf16[32,32,512]{2,1,0:T(8,128)(2,1)}), bf16[32,32,512]{2,1,0:T(8,128)(2,1)S(1)}, u32[]{:S(2)}, u32[]{:S(2)}) async-start(bf16[32,32,512]{2,1,0:T(8,128)(2,1)} %bitcast.8), calls=%async_computation | async-start | bytes 2097152 | tf_op jit(solution)/shard_map/all_to_all | solution.py:340
  28.0 1.7 %collective-permute-start.1 = (f32[1,512]{1,0:T(1,128)S(1)}, f32[1,512]{1,0:T(1,128)S(1)}, u32[]{:S(2)}, u32[]{:S(2)}) collective-permute-start(f32[1,512]{1,0:T(1,128)S(1)} %get-tuple-element.21), channel_id=1, source_target_pairs={{0,1},{2,3},{4,5},{6,7},{1,0},{3,2},{5,4},{7,6},{8,9},{10,11},{12,... | collective-permute-start | bytes 6152 | tf_op jit(solution)/shard_map/ppermute | solution.py:325
  29.7 1.3 %collective-permute-done.1 = f32[1,512]{1,0:T(1,128)S(1)} collective-permute-done((f32[1,512]{1,0:T(1,128)S(1)}, f32[1,512]{1,0:T(1,128)S(1)}, u32[]{:S(2)}, u32[]{:S(2)}) %collective-permute-start.1) | collective-permute-done | bytes 2080 | tf_op jit(solution)/shard_map/ppermute | solution.py:325
  31.0 5.4 %collective-permute-start.2 = (f32[1,512]{1,0:T(1,128)S(1)}, f32[1,512]{1,0:T(1,128)S(1)}, u32[]{:S(2)}, u32[]{:S(2)}) collective-permute-start(f32[1,512]{1,0:T(1,128)S(1)} %add.12), channel_id=1, source_target_pairs={{1,2},{3,4},{5,6},{7,0},{2,1},{4,3},{6,5},{0,7},{9,10},{11,12},{13... | collective-permute-start | bytes 6152 | tf_op jit(solution)/shard_map/ppermute | solution.py:325
  36.4 1.0 %collective-permute-done.2 = f32[1,512]{1,0:T(1,128)S(1)} collective-permute-done((f32[1,512]{1,0:T(1,128)S(1)}, f32[1,512]{1,0:T(1,128)S(1)}, u32[]{:S(2)}, u32[]{:S(2)}) %collective-permute-start.2) | collective-permute-done | bytes 2080 | tf_op jit(solution)/shard_map/ppermute | solution.py:325
  37.4 1.9 %collective-permute-start.3 = (f32[1,512]{1,0:T(1,128)S(1)}, f32[1,512]{1,0:T(1,128)S(1)}, u32[]{:S(2)}, u32[]{:S(2)}) collective-permute-start(f32[1,512]{1,0:T(1,128)S(1)} %add.13), channel_id=1, source_target_pairs={{0,3},{7,4},{1,6},{2,5},{3,0},{4,7},{6,1},{5,2},{8,11},{15,12},{9,... | collective-permute-start | bytes 6152 | tf_op jit(solution)/shard_map/ppermute | solution.py:326
  39.3 2.7 %collective-permute-done.3 = f32[1,512]{1,0:T(1,128)S(1)} collective-permute-done((f32[1,512]{1,0:T(1,128)S(1)}, f32[1,512]{1,0:T(1,128)S(1)}, u32[]{:S(2)}, u32[]{:S(2)}) %collective-permute-start.3) | collective-permute-done | bytes 2080 | tf_op jit(solution)/shard_map/ppermute | solution.py:326
  42.0 3.0 %all-to-all-done.recv_ref = bf16[32,32,512]{2,1,0:T(8,128)(2,1)S(1)} async-done(((bf16[32,32,512]{2,1,0:T(8,128)(2,1)}), bf16[32,32,512]{2,1,0:T(8,128)(2,1)S(1)}, u32[]{:S(2)}, u32[]{:S(2)}) %all-to-all-start) | async-done | bytes 1048608 | tf_op jit(solution)/shard_map/all_to_all | solution.py:340
  44.9 0.7 %broadcast_in_dim.9 = f32[32,1,512]{2,1,0:T(1,128)} broadcast(f32[512]{0:T(512)S(1)} %bitcast.9), dimensions={2} | broadcast | bytes 67584 | tf_op jit(solution)/shard_map/broadcast_in_dim | solution.py:343
  45.6 7.0 %all-to-all-start.1 = ((f32[32,1,512]{2,1,0:T(1,128)}), f32[32,1,512]{2,1,0:T(1,128)S(1)}, u32[]{:S(2)}, u32[]{:S(2)}) async-start(f32[32,1,512]{2,1,0:T(1,128)} %broadcast_in_dim.9), calls=%async_computation.1 | async-start | bytes 131072 | tf_op jit(solution)/shard_map/all_to_all | solution.py:343
  52.6 0.0 copy-done
  52.6 0.1 dynamic-slice_bitcast_fusion
  52.7 0.1 copy.10.gain_ref
  52.7 7.2 %all-to-all-done.1.sums_ref = f32[32,1,512]{2,1,0:T(1,128)S(1)} async-done(((f32[32,1,512]{2,1,0:T(1,128)}), f32[32,1,512]{2,1,0:T(1,128)S(1)}, u32[]{:S(2)}, u32[]{:S(2)}) %all-to-all-start.1) | async-done | bytes 65568 | tf_op jit(solution)/shard_map/all_to_all | solution.py:343
  59.9 1.1 %settle.1 = bf16[32,16384]{1,0:T(8,128)(2,1)} custom-call(bf16[32,32,512]{2,1,0:T(8,128)(2,1)S(1)} %all-to-all-done.recv_ref, f32[32,1,512]{2,1,0:T(1,128)S(1)} %all-to-all-done.1.sums_ref, f32[32,1]{1,0:T(8,128)S(1)} %copy.10.gain_ref), custom_call_target="tpu_custom_call" | custom-call | tf_op jit(solution)/shard_map/settle/pallas_call | solution.py:308
  (3 shorter events, 0.0 us)
Async XLA Ops:
  0.0 52.6 %copy-start = (f32[1024]{0:T(1024)S(1)}, f32[1024]{0:T(1024)}, u32[]{:S(2)}) copy-start(f32[1024]{0:T(1024)} %param.14) | copy-start | bytes 12292
  2.9 13.4 %collective-permute-start = (bf16[8,144,128]{2,1,0:T(8,128)(2,1)}, bf16[8,144,128]{2,1,0:T(8,128)(2,1)S(1)}, u32[]{:S(2)}, u32[]{:S(2)}) collective-permute-start(bf16[8,144,128]{2,1,0:T(8,128)(2,1)} %tail.1), channel_id=1, source_target_pairs={{0,8},{8,16},{16,24},{24,32},{32,40},{40,48},{48,56},{56,64},{64,7... | collective-permute-start | bytes 884744 | tf_op jit(solution)/shard_map/ppermute | solution.py:337
  7.5 8.8 %copy-start.1 = (f32[3,3,1024]{2,1,0:T(4,128)S(1)}, f32[3,3,1024]{2,1,0:T(4,128)}, u32[]{:S(2)}) copy-start(f32[3,3,1024]{2,1,0:T(4,128)} %sf_ref.5) | copy-start | bytes 110596
  7.5 8.8 %copy-start.2 = (f32[64,128]{1,0:T(8,128)S(1)}, f32[64,128]{1,0:T(8,128)}, u32[]{:S(2)}) copy-start(f32[64,128]{1,0:T(8,128)} %taps_ref.3) | copy-start | bytes 98308
  7.5 8.8 %copy-start.3 = (f32[1024]{0:T(1024)S(1)}, f32[1024]{0:T(1024)}, u32[]{:S(2)}) copy-start(f32[1024]{0:T(1024)} %param.13) | copy-start | bytes 12292
  7.6 8.8 %copy-start.4 = (s32[64]{0:T(128)S(1)}, s32[64]{0:T(128)}, u32[]{:S(2)}) copy-start(s32[64]{0:T(128)} %docs_ref.5) | copy-start | bytes 772
  21.1 23.8 %all-to-all-start = ((bf16[32,32,512]{2,1,0:T(8,128)(2,1)}), bf16[32,32,512]{2,1,0:T(8,128)(2,1)S(1)}, u32[]{:S(2)}, u32[]{:S(2)}) async-start(bf16[32,32,512]{2,1,0:T(8,128)(2,1)} %bitcast.8), calls=%async_computation | async-start | bytes 2097152 | tf_op jit(solution)/shard_map/all_to_all | solution.py:340
  28.0 3.0 %collective-permute-start.1 = (f32[1,512]{1,0:T(1,128)S(1)}, f32[1,512]{1,0:T(1,128)S(1)}, u32[]{:S(2)}, u32[]{:S(2)}) collective-permute-start(f32[1,512]{1,0:T(1,128)S(1)} %get-tuple-element.21), channel_id=1, source_target_pairs={{0,1},{2,3},{4,5},{6,7},{1,0},{3,2},{5,4},{7,6},{8,9},{10,11},{12,... | collective-permute-start | bytes 6152 | tf_op jit(solution)/shard_map/ppermute | solution.py:325
  31.0 6.4 %collective-permute-start.2 = (f32[1,512]{1,0:T(1,128)S(1)}, f32[1,512]{1,0:T(1,128)S(1)}, u32[]{:S(2)}, u32[]{:S(2)}) collective-permute-start(f32[1,512]{1,0:T(1,128)S(1)} %add.12), channel_id=1, source_target_pairs={{1,2},{3,4},{5,6},{7,0},{2,1},{4,3},{6,5},{0,7},{9,10},{11,12},{13... | collective-permute-start | bytes 6152 | tf_op jit(solution)/shard_map/ppermute | solution.py:325
  37.4 4.5 %collective-permute-start.3 = (f32[1,512]{1,0:T(1,128)S(1)}, f32[1,512]{1,0:T(1,128)S(1)}, u32[]{:S(2)}, u32[]{:S(2)}) collective-permute-start(f32[1,512]{1,0:T(1,128)S(1)} %add.13), channel_id=1, source_target_pairs={{0,3},{7,4},{1,6},{2,5},{3,0},{4,7},{6,1},{5,2},{8,11},{15,12},{9,... | collective-permute-start | bytes 6152 | tf_op jit(solution)/shard_map/ppermute | solution.py:326
  45.6 14.3 %all-to-all-start.1 = ((f32[32,1,512]{2,1,0:T(1,128)}), f32[32,1,512]{2,1,0:T(1,128)S(1)}, u32[]{:S(2)}, u32[]{:S(2)}) async-start(f32[32,1,512]{2,1,0:T(1,128)} %broadcast_in_dim.9), calls=%async_computation.1 | async-start | bytes 131072 | tf_op jit(solution)/shard_map/all_to_all | solution.py:343

commit v6 on v5

--- a/solution.py
+++ b/solution.py
@@ -242,7 +242,7 @@
         out_specs=pl.BlockSpec((c // CB, ENDS, 128), lambda i: (i, 0, 0)),
         out_shape=jax.ShapeDtypeStruct((ch // CB, ENDS, 128), BF),
         scratch_shapes=[pltpu.VMEM((2, GROUP, 128), BF)],
-        compiler_params=pltpu.CompilerParams(vmem_limit_bytes=BIG), name="tail",
+        compiler_params=pltpu.CompilerParams(vmem_limit_bytes=LATER_VMEM), name="tail",
     )(docs, base, gate, key, value, sf)
 
 
@@ -261,18 +261,18 @@
         in_specs=[SMEM, SMEM, wide, wide, wide] + param_specs(c),
         out_specs=[wide, tile, tile, pl.BlockSpec((c // CB, 16, CB), lambda i: (i, 0, 0)),
                    pl.BlockSpec((c // GROUP, MR, MR), lambda i: (i, 0, 0)), pl.BlockSpec((1, n - 128), lambda i: (0, 0))],
-        out_shape=[jax.ShapeDtypeStruct((ch, n), BF), jax.ShapeDtypeStruct((ch, 128), F32),
+        out_shape=[pltpu.HBM((ch, n), BF), jax.ShapeDtypeStruct((ch, 128), F32),
                    jax.ShapeDtypeStruct((ch, 128), BF), jax.ShapeDtypeStruct((ch // CB, 16, CB), BF),
                    jax.ShapeDtypeStruct((ch // GROUP, MR, MR), BF), jax.ShapeDtypeStruct((1, n - 128), F32)],
         scratch_shapes=[pltpu.VMEM((3, 256, 128), BF), pltpu.VMEM((2, GROUP, n), BF), pltpu.VMEM((GROUP, 128), BF),
                         pltpu.VMEM((8, n - 128), F32)],
         cost_estimate=pl.CostEstimate(flops=2 * ch * 384 * 256 * 8, bytes_accessed=8 * ch * n, transcendentals=0),
-        compiler_params=pltpu.CompilerParams(vmem_limit_bytes=BIG), name="later",
+        compiler_params=pltpu.CompilerParams(vmem_limit_bytes=LATER_VMEM), name="later",
     )(docs, base, gate, key, value, sf, skip, taps)
 
 
 def first(docs, base, halo, done, sf, skip, taps):
-    done = [pltpu.with_memory_space_constraint(x, pltpu.HBM) for x in done]
+    done = [pltpu.with_memory_space_constraint(x, pltpu.HBM if i == 0 else pltpu.VMEM) for i, x in enumerate(done)]
     rows, aux, prod, own, rings, squares = done
     ch, n = rows.shape
     c = min(BL, ch)
@@ -294,6 +294,7 @@
 
 
 FIRST_VMEM = 24 << 20
+LATER_VMEM = 40 << 20
 def final_kernel(recv_ref, sums_ref, gain_ref, out_ref):
     per, c, n = recv_ref.shape
     gain = jnp.broadcast_to(gain_ref[...], (c, n))
@@ -333,7 +334,8 @@
     base = (place * n).astype(jnp.int32).reshape(1)
     skip = skip.reshape(1, ch)
     gain = lax.dynamic_slice_in_dim(gain, place * (ch // width), ch // width).reshape(ch // width, 1)
-    ends = tail(docs, base, gate, key, value, sf)
+    gate, key, value = (pltpu.with_memory_space_constraint(x, pltpu.HBM) for x in (gate, key, value))
+    ends = tail(pltpu.with_memory_space_constraint(docs, pltpu.HBM), base, gate, key, value, pltpu.with_memory_space_constraint(sf, pltpu.HBM))
     halo = lax.ppermute(ends, "ctx", [(i, i + 1) for i in range(width - 1)])
     done = later(docs, base, gate, key, value, sf, skip, taps)
     rows, squares = first(docs, base, halo, done, sf, skip, taps)

time: 61.4 us -> 59.4 us (0.967)
  Pallas kernels: 17.5 us -> 15.5 us
    pallas_call x1, Pallas kernels: 8.73 us -> 7.87 us  [later(): pl.pallas_call(later_kernel, grid=(ch // c,), in_specs=[SMEM, SMEM, wide,...]
    pallas_call x1, Pallas kernels: 2.92 us -> 2.3 us  [tail(): pl.pallas_call(tail_kernel, grid=(ch // c,), in_specs=[SMEM, SMEM, wide,...]
  transfers between devices with their start and end apart: 6 -> 6, of which waited for: 5 -> 5; matrix products, arithmetic and copies ran while one was open for 0% -> 0% of each run, Pallas kernels for 14% -> 13%
where the time goes in v6:
time: 59.4 us; the launch traced here: 59.1 us
  starting transfers between devices  27.5 us (46%)
  Pallas kernels  15.5 us (26%)
  waiting for transfers between devices  15.1 us (25%)
  local copies, waits for them, and re-layouts  0.86 us (1%)
    pallas_call x1, Pallas kernels, later(): pl.pallas_call(later_kernel, grid=(ch // c,), in_specs=[SMEM, SMEM, wide,...  7.87 us
    all_to_all x1, waiting for transfers between devices, local(): lax.all_to_all(jnp.broadcast_to((near + far)[None], (width, 1, n)), 'ctx'...  7.19 us
    ppermute x2, starting transfers between devices, channel_sum(): x = x + lax.ppermute(x, 'ch', list(pairs) + [(b, a) for a, b in pairs])  7.12 us
    all_to_all x1, starting transfers between devices, local(): lax.all_to_all(jnp.broadcast_to((near + far)[None], (width, 1, n)), 'ctx'...  6.95 us
    all_to_all x1, starting transfers between devices, local(): lax.all_to_all(rows.reshape(width, ch // width, n), 'ctx', split_axis=0,...  6.91 us
    ppermute x1, starting transfers between devices, local(): halo = lax.ppermute(ends, 'ctx', [(i, i + 1) for i in range(width - 1)])  4.6 us
    pallas_call x1, Pallas kernels, first(): pl.pallas_call(first_kernel, grid=(ch // c,), in_specs=[SMEM, SMEM, pl.Bl...  4.26 us
    all_to_all x1, waiting for transfers between devices, local(): lax.all_to_all(rows.reshape(width, ch // width, n), 'ctx', split_axis=0,...  2.98 us
  transfers between devices with their start and end apart: 6, of which 5 were waited for; matrix products, arithmetic and copies ran while one was open for 0% of the time, Pallas kernels for 13%

profile of v6, /device:TPU:1, one launch (start us, length us, event | category | flops | bytes accessed | tf_op | source)
XLA Modules:
  0.0 59.1 jit_solution(2582961484751286065)
XLA Ops:
  0.0 0.0 copy-start
  0.0 0.0 copy-start.1
  0.0 0.0 copy-start.4
  0.0 0.0 copy-start.3
  0.0 0.0 copy-start.2
  0.0 2.3 %tail.1 = bf16[8,144,128]{2,1,0:T(8,128)(2,1)S(1)} custom-call(s32[64]{0:T(128)} %docs_ref.5, s32[1]{0:T(128)} %bitcast.base_ref, bf16[1024,512]{1,0:T(8,128)(2,1)} %gate_ref.3, bf16[1024,512]{1,0:T(8,128)(2,1)} %key_ref.3, bf16[1024,512]{1,0:T(8,128)(2,1)} %value_ref.3, f32[3,3,1024]{2,1,0:T(4,128)} %sf_ref.5), custom_call_target="tpu_custom_call" | custom-call | tf_op jit(solution)/shard_map/tail/pallas_call | solution.py:239
  2.3 4.6 %collective-permute-start = (bf16[8,144,128]{2,1,0:T(8,128)(2,1)S(1)}, bf16[8,144,128]{2,1,0:T(8,128)(2,1)S(1)}, u32[]{:S(2)}, u32[]{:S(2)}) collective-permute-start(bf16[8,144,128]{2,1,0:T(8,128)(2,1)S(1)} %tail.1), channel_id=1, source_target_pairs={{0,8},{8,16},{16,24},{24,32},{32,40},{40,48},{48,56},{56,64},{64,7... | collective-permute-start | bytes 884744 | tf_op jit(solution)/shard_map/ppermute | solution.py:339
  6.9 0.0 copy-done.1
  7.0 0.0 copy-done.4
  7.0 0.0 copy-done.3
  7.0 0.0 copy-done.2
  7.0 7.9 %later.1 = (bf16[1024,512]{1,0:T(8,128)(2,1)}, f32[1024,128]{1,0:T(8,128)S(1)}, bf16[1024,128]{1,0:T(8,128)(2,1)S(1)}, bf16[8,16,128]{2,1,0:T(8,128)(2,1)S(1)}, ...) custom-call(s32[64]{0:T(128)S(1)} %copy-done.4, s32[1]{0:T(128)} %bitcast.base_ref, bf16[1024,512]{1,0:T(8,128)(2,1)} %gate_ref.3, ...), custom_call_target="tpu_custom_call" | custom-call | flops 1610612736 | bytes 4194304 | tf_op jit(solution)/shard_map/later/pallas_call | solution.py:259
  14.9 0.0 collective-permute-done.halo_ref
  14.9 4.3 %first.1 = (bf16[1024,512]{1,0:T(8,128)(2,1)}, f32[1,512]{1,0:T(1,128)S(1)}) custom-call(s32[64]{0:T(128)S(1)} %copy-done.4, s32[1]{0:T(128)} %bitcast.base_ref, bf16[8,144,128]{2,1,0:T(8,128)(2,1)S(1)} %collective-permute-done.halo_ref, bf16[1024,512]{1,0:T(8,128)(2,1)} %get-tuple-element.15.rows_ref, ...), custom_call_target="tpu_custom_call", output_to_operand_aliasing={{0}: (3, {})} | custom-call | flops 536870912 | bytes 2097152 | tf_op jit(solution)/shard_map/first/pallas_call | solution.py:282
  19.1 6.9 %all-to-all-start = ((bf16[32,32,512]{2,1,0:T(8,128)(2,1)}), bf16[32,32,512]{2,1,0:T(8,128)(2,1)S(1)}, u32[]{:S(2)}, u32[]{:S(2)}) async-start(bf16[32,32,512]{2,1,0:T(8,128)(2,1)} %bitcast.8), calls=%async_computation | async-start | bytes 2097152 | tf_op jit(solution)/shard_map/all_to_all | solution.py:342
  26.0 1.7 %collective-permute-start.1 = (f32[1,512]{1,0:T(1,128)S(1)}, f32[1,512]{1,0:T(1,128)S(1)}, u32[]{:S(2)}, u32[]{:S(2)}) collective-permute-start(f32[1,512]{1,0:T(1,128)S(1)} %get-tuple-element.21), channel_id=1, source_target_pairs={{0,1},{2,3},{4,5},{6,7},{1,0},{3,2},{5,4},{7,6},{8,9},{10,11},{12,... | collective-permute-start | bytes 6152 | tf_op jit(solution)/shard_map/ppermute | solution.py:326
  27.7 1.3 %collective-permute-done.1 = f32[1,512]{1,0:T(1,128)S(1)} collective-permute-done((f32[1,512]{1,0:T(1,128)S(1)}, f32[1,512]{1,0:T(1,128)S(1)}, u32[]{:S(2)}, u32[]{:S(2)}) %collective-permute-start.1) | collective-permute-done | bytes 2080 | tf_op jit(solution)/shard_map/ppermute | solution.py:326
  29.0 5.4 %collective-permute-start.2 = (f32[1,512]{1,0:T(1,128)S(1)}, f32[1,512]{1,0:T(1,128)S(1)}, u32[]{:S(2)}, u32[]{:S(2)}) collective-permute-start(f32[1,512]{1,0:T(1,128)S(1)} %add.12), channel_id=1, source_target_pairs={{1,2},{3,4},{5,6},{7,0},{2,1},{4,3},{6,5},{0,7},{9,10},{11,12},{13... | collective-permute-start | bytes 6152 | tf_op jit(solution)/shard_map/ppermute | solution.py:326
  34.4 1.0 %collective-permute-done.2 = f32[1,512]{1,0:T(1,128)S(1)} collective-permute-done((f32[1,512]{1,0:T(1,128)S(1)}, f32[1,512]{1,0:T(1,128)S(1)}, u32[]{:S(2)}, u32[]{:S(2)}) %collective-permute-start.2) | collective-permute-done | bytes 2080 | tf_op jit(solution)/shard_map/ppermute | solution.py:326
  35.4 1.9 %collective-permute-start.3 = (f32[1,512]{1,0:T(1,128)S(1)}, f32[1,512]{1,0:T(1,128)S(1)}, u32[]{:S(2)}, u32[]{:S(2)}) collective-permute-start(f32[1,512]{1,0:T(1,128)S(1)} %add.13), channel_id=1, source_target_pairs={{0,3},{7,4},{1,6},{2,5},{3,0},{4,7},{6,1},{5,2},{8,11},{15,12},{9,... | collective-permute-start | bytes 6152 | tf_op jit(solution)/shard_map/ppermute | solution.py:327
  37.3 2.7 %collective-permute-done.3 = f32[1,512]{1,0:T(1,128)S(1)} collective-permute-done((f32[1,512]{1,0:T(1,128)S(1)}, f32[1,512]{1,0:T(1,128)S(1)}, u32[]{:S(2)}, u32[]{:S(2)}) %collective-permute-start.3) | collective-permute-done | bytes 2080 | tf_op jit(solution)/shard_map/ppermute | solution.py:327
  40.0 3.0 %all-to-all-done.recv_ref = bf16[32,32,512]{2,1,0:T(8,128)(2,1)S(1)} async-done(((bf16[32,32,512]{2,1,0:T(8,128)(2,1)}), bf16[32,32,512]{2,1,0:T(8,128)(2,1)S(1)}, u32[]{:S(2)}, u32[]{:S(2)}) %all-to-all-start) | async-done | bytes 1048608 | tf_op jit(solution)/shard_map/all_to_all | solution.py:342
  42.9 0.7 %broadcast_in_dim.9 = f32[32,1,512]{2,1,0:T(1,128)} broadcast(f32[512]{0:T(512)S(1)} %bitcast.9), dimensions={2} | broadcast | bytes 67584 | tf_op jit(solution)/shard_map/broadcast_in_dim | solution.py:345
  43.6 7.0 %all-to-all-start.1 = ((f32[32,1,512]{2,1,0:T(1,128)}), f32[32,1,512]{2,1,0:T(1,128)S(1)}, u32[]{:S(2)}, u32[]{:S(2)}) async-start(f32[32,1,512]{2,1,0:T(1,128)} %broadcast_in_dim.9), calls=%async_computation.1 | async-start | bytes 131072 | tf_op jit(solution)/shard_map/all_to_all | solution.py:345
  50.6 0.0 copy-done
  50.6 0.1 dynamic-slice_bitcast_fusion
  50.7 0.1 copy.10.gain_ref
  50.8 7.2 %all-to-all-done.1.sums_ref = f32[32,1,512]{2,1,0:T(1,128)S(1)} async-done(((f32[32,1,512]{2,1,0:T(1,128)}), f32[32,1,512]{2,1,0:T(1,128)S(1)}, u32[]{:S(2)}, u32[]{:S(2)}) %all-to-all-start.1) | async-done | bytes 65568 | tf_op jit(solution)/shard_map/all_to_all | solution.py:345
  57.9 1.1 %settle.1 = bf16[32,16384]{1,0:T(8,128)(2,1)} custom-call(bf16[32,32,512]{2,1,0:T(8,128)(2,1)S(1)} %all-to-all-done.recv_ref, f32[32,1,512]{2,1,0:T(1,128)S(1)} %all-to-all-done.1.sums_ref, f32[32,1]{1,0:T(8,128)S(1)} %copy.10.gain_ref), custom_call_target="tpu_custom_call" | custom-call | tf_op jit(solution)/shard_map/settle/pallas_call | solution.py:309
  (3 shorter events, 0.0 us)
Async XLA Ops:
  0.0 50.6 %copy-start = (f32[1024]{0:T(1024)S(1)}, f32[1024]{0:T(1024)}, u32[]{:S(2)}) copy-start(f32[1024]{0:T(1024)} %param.14) | copy-start | bytes 12292
  0.0 6.9 %copy-start.1 = (f32[3,3,1024]{2,1,0:T(4,128)S(1)}, f32[3,3,1024]{2,1,0:T(4,128)}, u32[]{:S(2)}) copy-start(f32[3,3,1024]{2,1,0:T(4,128)} %sf_ref.5) | copy-start | bytes 110596
  0.0 7.0 %copy-start.4 = (s32[64]{0:T(128)S(1)}, s32[64]{0:T(128)}, u32[]{:S(2)}) copy-start(s32[64]{0:T(128)} %docs_ref.5) | copy-start | bytes 772
  0.0 7.0 %copy-start.3 = (f32[1024]{0:T(1024)S(1)}, f32[1024]{0:T(1024)}, u32[]{:S(2)}) copy-start(f32[1024]{0:T(1024)} %param.13) | copy-start | bytes 12292
  0.0 7.0 %copy-start.2 = (f32[64,128]{1,0:T(8,128)S(1)}, f32[64,128]{1,0:T(8,128)}, u32[]{:S(2)}) copy-start(f32[64,128]{1,0:T(8,128)} %taps_ref.3) | copy-start | bytes 98308
  2.3 12.5 %collective-permute-start = (bf16[8,144,128]{2,1,0:T(8,128)(2,1)S(1)}, bf16[8,144,128]{2,1,0:T(8,128)(2,1)S(1)}, u32[]{:S(2)}, u32[]{:S(2)}) collective-permute-start(bf16[8,144,128]{2,1,0:T(8,128)(2,1)S(1)} %tail.1), channel_id=1, source_target_pairs={{0,8},{8,16},{16,24},{24,32},{32,40},{40,48},{48,56},{56,64},{64,7... | collective-permute-start | bytes 884744 | tf_op jit(solution)/shard_map/ppermute | solution.py:339
  19.1 23.8 %all-to-all-start = ((bf16[32,32,512]{2,1,0:T(8,128)(2,1)}), bf16[32,32,512]{2,1,0:T(8,128)(2,1)S(1)}, u32[]{:S(2)}, u32[]{:S(2)}) async-start(bf16[32,32,512]{2,1,0:T(8,128)(2,1)} %bitcast.8), calls=%async_computation | async-start | bytes 2097152 | tf_op jit(solution)/shard_map/all_to_all | solution.py:342
  26.0 3.0 %collective-permute-start.1 = (f32[1,512]{1,0:T(1,128)S(1)}, f32[1,512]{1,0:T(1,128)S(1)}, u32[]{:S(2)}, u32[]{:S(2)}) collective-permute-start(f32[1,512]{1,0:T(1,128)S(1)} %get-tuple-element.21), channel_id=1, source_target_pairs={{0,1},{2,3},{4,5},{6,7},{1,0},{3,2},{5,4},{7,6},{8,9},{10,11},{12,... | collective-permute-start | bytes 6152 | tf_op jit(solution)/shard_map/ppermute | solution.py:326
  29.0 6.4 %collective-permute-start.2 = (f32[1,512]{1,0:T(1,128)S(1)}, f32[1,512]{1,0:T(1,128)S(1)}, u32[]{:S(2)}, u32[]{:S(2)}) collective-permute-start(f32[1,512]{1,0:T(1,128)S(1)} %add.12), channel_id=1, source_target_pairs={{1,2},{3,4},{5,6},{7,0},{2,1},{4,3},{6,5},{0,7},{9,10},{11,12},{13... | collective-permute-start | bytes 6152 | tf_op jit(solution)/shard_map/ppermute | solution.py:326
  35.4 4.5 %collective-permute-start.3 = (f32[1,512]{1,0:T(1,128)S(1)}, f32[1,512]{1,0:T(1,128)S(1)}, u32[]{:S(2)}, u32[]{:S(2)}) collective-permute-start(f32[1,512]{1,0:T(1,128)S(1)} %add.13), channel_id=1, source_target_pairs={{0,3},{7,4},{1,6},{2,5},{3,0},{4,7},{6,1},{5,2},{8,11},{15,12},{9,... | collective-permute-start | bytes 6152 | tf_op jit(solution)/shard_map/ppermute | solution.py:327
  43.6 14.3 %all-to-all-start.1 = ((f32[32,1,512]{2,1,0:T(1,128)}), f32[32,1,512]{2,1,0:T(1,128)S(1)}, u32[]{:S(2)}, u32[]{:S(2)}) async-start(f32[32,1,512]{2,1,0:T(1,128)} %broadcast_in_dim.9), calls=%async_computation.1 | async-start | bytes 131072 | tf_op jit(solution)/shard_map/all_to_all | solution.py:345

commit v7 on v6

--- a/solution.py
+++ b/solution.py
@@ -177,7 +177,6 @@
         acc[...] = jnp.zeros_like(acc)
 
     lane = lax.broadcasted_iota(jnp.int32, (GROUP, 128), 1)
-    one_hot = (lax.broadcasted_iota(jnp.int32, (16, 128), 0) == lane).astype(F32).astype(BF)
     total0, total1 = acc[0], acc[1]
     for b in range(halo_ref.shape[0]):
         here = slice(CB * b, CB * (b + 1))
@@ -195,19 +194,21 @@
         two = (both_positions(1) * both_positions(2)).astype(BF).astype(F32)
         t = [sf_ref[0, lag:lag + 1, here] for lag in range(3)]
         gate = t[0] * own[8:9] + keeps[2:3, 0:1] * (t[1] * own[7:8]) + keeps[3:4, 0:1] * (t[2] * own[6:7])
-        cols = spread([skip_ref[:, here], both_positions(0), keeps[4:5, 0:1] * two[1:] * gate])
-        put = lax.dot_general(jnp.concatenate([two, jnp.zeros((14, CB), F32)], axis=0).astype(BF), one_hot,
-                              (((0,), (0,)), ((), ())), preferred_element_type=F32)
+        cols = spread([skip_ref[:, here], both_positions(0), keeps[4:5, 0:1] * two[1:] * gate, two])
         taps = taps_ref[8 * b:8 * (b + 1)].astype(BF).astype(F32)
         for g in range(CB // GROUP):
             at = slice(CB * b + GROUP * g, CB * b + GROUP * (g + 1))
             inside = slice(GROUP * g, GROUP * (g + 1))
             c = cols[inside]
-            product = prod_ref[at] + put[inside].astype(BF)
+            product = prod_ref[at]
             ring = ring_ref[8 * b + g]
             mixed = jnp.dot(jnp.concatenate([halo_ref[b, inside], product], axis=1),
                             jnp.concatenate([ring, ring], axis=0) * masks[...], preferred_element_type=F32)
-            mixed = mixed + lanes_of(c, 0) * product.astype(F32)
+            skip = lanes_of(c, 0)
+            near = ring[:16].astype(F32) * masks[128:144].astype(F32)
+            mixed = (mixed + skip * product.astype(F32)
+                     + lanes_of(c, 4) * (near[0:1] + jnp.where(lane == 0, skip, 0.0))
+                     + lanes_of(c, 5) * (near[1:2] + jnp.where(lane == 1, skip, 0.0)))
             gated = jnp.where(lane == 0, lanes_of(c, 1), jnp.where(lane == 1, lanes_of(c, 2), aux_ref[at])) * mixed
             old = rows_ref[at, 128:].astype(F32)
             after = jnp.where(lane == 0, old + lanes_of(c, 3) * taps[g:g + 1, 127:128], old)

time: 59.4 us -> 58.6 us (0.987)
  Pallas kernels: 15.5 us -> 14.8 us
    pallas_call x1, Pallas kernels: 4.26 us -> 3.5 us  [first(): pl.pallas_call(first_kernel, grid=(ch // c,), in_specs=[SMEM, SMEM, pl.Bl...]
where the time goes in v7:
time: 58.6 us; the launch traced here: 58.3 us
  starting transfers between devices  27.5 us (47%)
  waiting for transfers between devices  15.1 us (26%)
  Pallas kernels  14.8 us (25%)
  local copies, waits for them, and re-layouts  0.86 us (1%)
    pallas_call x1, Pallas kernels, later(): pl.pallas_call(later_kernel, grid=(ch // c,), in_specs=[SMEM, SMEM, wide,...  7.87 us
    all_to_all x1, waiting for transfers between devices, local(): lax.all_to_all(jnp.broadcast_to((near + far)[None], (width, 1, n)), 'ctx'...  7.19 us
    ppermute x2, starting transfers between devices, channel_sum(): x = x + lax.ppermute(x, 'ch', list(pairs) + [(b, a) for a, b in pairs])  7.12 us
    all_to_all x1, starting transfers between devices, local(): lax.all_to_all(jnp.broadcast_to((near + far)[None], (width, 1, n)), 'ctx'...  6.96 us
    all_to_all x1, starting transfers between devices, local(): lax.all_to_all(rows.reshape(width, ch // width, n), 'ctx', split_axis=0,...  6.9 us
    ppermute x1, starting transfers between devices, local(): halo = lax.ppermute(ends, 'ctx', [(i, i + 1) for i in range(width - 1)])  4.6 us
    pallas_call x1, Pallas kernels, first(): pl.pallas_call(first_kernel, grid=(ch // c,), in_specs=[SMEM, SMEM, pl.Bl...  3.5 us
    all_to_all x1, waiting for transfers between devices, local(): lax.all_to_all(rows.reshape(width, ch // width, n), 'ctx', split_axis=0,...  2.98 us
  transfers between devices with their start and end apart: 6, of which 5 were waited for; matrix products, arithmetic and copies ran while one was open for 0% of the time, Pallas kernels for 13%

profile of v7, /device:TPU:1, one launch (start us, length us, event | category | flops | bytes accessed | tf_op | source)
XLA Modules:
  0.0 58.3 jit_solution(7172561128532277041)
XLA Ops:
  0.0 0.0 copy-start
  0.0 0.0 copy-start.1
  0.0 0.0 copy-start.4
  0.0 0.0 copy-start.3
  0.0 0.0 copy-start.2
  0.0 2.3 %tail.1 = bf16[8,144,128]{2,1,0:T(8,128)(2,1)S(1)} custom-call(s32[64]{0:T(128)} %docs_ref.5, s32[1]{0:T(128)} %bitcast.base_ref, bf16[1024,512]{1,0:T(8,128)(2,1)} %gate_ref.3, bf16[1024,512]{1,0:T(8,128)(2,1)} %key_ref.3, bf16[1024,512]{1,0:T(8,128)(2,1)} %value_ref.3, f32[3,3,1024]{2,1,0:T(4,128)} %sf_ref.5), custom_call_target="tpu_custom_call" | custom-call | tf_op jit(solution)/shard_map/tail/pallas_call | solution.py:240
  2.3 4.6 %collective-permute-start = (bf16[8,144,128]{2,1,0:T(8,128)(2,1)S(1)}, bf16[8,144,128]{2,1,0:T(8,128)(2,1)S(1)}, u32[]{:S(2)}, u32[]{:S(2)}) collective-permute-start(bf16[8,144,128]{2,1,0:T(8,128)(2,1)S(1)} %tail.1), channel_id=1, source_target_pairs={{0,8},{8,16},{16,24},{24,32},{32,40},{40,48},{48,56},{56,64},{64,7... | collective-permute-start | bytes 884744 | tf_op jit(solution)/shard_map/ppermute | solution.py:340
  6.9 0.0 copy-done.1
  7.0 0.0 copy-done.4
  7.0 0.0 copy-done.3
  7.0 0.0 copy-done.2
  7.0 7.9 %later.1 = (bf16[1024,512]{1,0:T(8,128)(2,1)}, f32[1024,128]{1,0:T(8,128)S(1)}, bf16[1024,128]{1,0:T(8,128)(2,1)S(1)}, bf16[8,16,128]{2,1,0:T(8,128)(2,1)S(1)}, ...) custom-call(s32[64]{0:T(128)S(1)} %copy-done.4, s32[1]{0:T(128)} %bitcast.base_ref, bf16[1024,512]{1,0:T(8,128)(2,1)} %gate_ref.3, ...), custom_call_target="tpu_custom_call" | custom-call | flops 1610612736 | bytes 4194304 | tf_op jit(solution)/shard_map/later/pallas_call | solution.py:260
  14.9 0.0 collective-permute-done.halo_ref
  14.9 3.5 %first.1 = (bf16[1024,512]{1,0:T(8,128)(2,1)}, f32[1,512]{1,0:T(1,128)S(1)}) custom-call(s32[64]{0:T(128)S(1)} %copy-done.4, s32[1]{0:T(128)} %bitcast.base_ref, bf16[8,144,128]{2,1,0:T(8,128)(2,1)S(1)} %collective-permute-done.halo_ref, bf16[1024,512]{1,0:T(8,128)(2,1)} %get-tuple-element.15.rows_ref, ...), custom_call_target="tpu_custom_call", output_to_operand_aliasing={{0}: (3, {})} | custom-call | flops 536870912 | bytes 2097152 | tf_op jit(solution)/shard_map/first/pallas_call | solution.py:283
  18.4 6.9 %all-to-all-start = ((bf16[32,32,512]{2,1,0:T(8,128)(2,1)}), bf16[32,32,512]{2,1,0:T(8,128)(2,1)S(1)}, u32[]{:S(2)}, u32[]{:S(2)}) async-start(bf16[32,32,512]{2,1,0:T(8,128)(2,1)} %bitcast.8), calls=%async_computation | async-start | bytes 2097152 | tf_op jit(solution)/shard_map/all_to_all | solution.py:343
  25.3 1.7 %collective-permute-start.1 = (f32[1,512]{1,0:T(1,128)S(1)}, f32[1,512]{1,0:T(1,128)S(1)}, u32[]{:S(2)}, u32[]{:S(2)}) collective-permute-start(f32[1,512]{1,0:T(1,128)S(1)} %get-tuple-element.21), channel_id=1, source_target_pairs={{0,1},{2,3},{4,5},{6,7},{1,0},{3,2},{5,4},{7,6},{8,9},{10,11},{12,... | collective-permute-start | bytes 6152 | tf_op jit(solution)/shard_map/ppermute | solution.py:327
  27.0 1.3 %collective-permute-done.1 = f32[1,512]{1,0:T(1,128)S(1)} collective-permute-done((f32[1,512]{1,0:T(1,128)S(1)}, f32[1,512]{1,0:T(1,128)S(1)}, u32[]{:S(2)}, u32[]{:S(2)}) %collective-permute-start.1) | collective-permute-done | bytes 2080 | tf_op jit(solution)/shard_map/ppermute | solution.py:327
  28.3 5.4 %collective-permute-start.2 = (f32[1,512]{1,0:T(1,128)S(1)}, f32[1,512]{1,0:T(1,128)S(1)}, u32[]{:S(2)}, u32[]{:S(2)}) collective-permute-start(f32[1,512]{1,0:T(1,128)S(1)} %add.12), channel_id=1, source_target_pairs={{1,2},{3,4},{5,6},{7,0},{2,1},{4,3},{6,5},{0,7},{9,10},{11,12},{13... | collective-permute-start | bytes 6152 | tf_op jit(solution)/shard_map/ppermute | solution.py:327
  33.7 1.0 %collective-permute-done.2 = f32[1,512]{1,0:T(1,128)S(1)} collective-permute-done((f32[1,512]{1,0:T(1,128)S(1)}, f32[1,512]{1,0:T(1,128)S(1)}, u32[]{:S(2)}, u32[]{:S(2)}) %collective-permute-start.2) | collective-permute-done | bytes 2080 | tf_op jit(solution)/shard_map/ppermute | solution.py:327
  34.7 1.9 %collective-permute-start.3 = (f32[1,512]{1,0:T(1,128)S(1)}, f32[1,512]{1,0:T(1,128)S(1)}, u32[]{:S(2)}, u32[]{:S(2)}) collective-permute-start(f32[1,512]{1,0:T(1,128)S(1)} %add.13), channel_id=1, source_target_pairs={{0,3},{7,4},{1,6},{2,5},{3,0},{4,7},{6,1},{5,2},{8,11},{15,12},{9,... | collective-permute-start | bytes 6152 | tf_op jit(solution)/shard_map/ppermute | solution.py:328
  36.6 2.6 %collective-permute-done.3 = f32[1,512]{1,0:T(1,128)S(1)} collective-permute-done((f32[1,512]{1,0:T(1,128)S(1)}, f32[1,512]{1,0:T(1,128)S(1)}, u32[]{:S(2)}, u32[]{:S(2)}) %collective-permute-start.3) | collective-permute-done | bytes 2080 | tf_op jit(solution)/shard_map/ppermute | solution.py:328
  39.2 3.0 %all-to-all-done.recv_ref = bf16[32,32,512]{2,1,0:T(8,128)(2,1)S(1)} async-done(((bf16[32,32,512]{2,1,0:T(8,128)(2,1)}), bf16[32,32,512]{2,1,0:T(8,128)(2,1)S(1)}, u32[]{:S(2)}, u32[]{:S(2)}) %all-to-all-start) | async-done | bytes 1048608 | tf_op jit(solution)/shard_map/all_to_all | solution.py:343
  42.2 0.7 %broadcast_in_dim.9 = f32[32,1,512]{2,1,0:T(1,128)} broadcast(f32[512]{0:T(512)S(1)} %bitcast.9), dimensions={2} | broadcast | bytes 67584 | tf_op jit(solution)/shard_map/broadcast_in_dim | solution.py:346
  42.9 7.0 %all-to-all-start.1 = ((f32[32,1,512]{2,1,0:T(1,128)}), f32[32,1,512]{2,1,0:T(1,128)S(1)}, u32[]{:S(2)}, u32[]{:S(2)}) async-start(f32[32,1,512]{2,1,0:T(1,128)} %broadcast_in_dim.9), calls=%async_computation.1 | async-start | bytes 131072 | tf_op jit(solution)/shard_map/all_to_all | solution.py:346
  49.8 0.0 copy-done
  49.8 0.1 dynamic-slice_bitcast_fusion
  49.9 0.1 copy.10.gain_ref
  50.0 7.2 %all-to-all-done.1.sums_ref = f32[32,1,512]{2,1,0:T(1,128)S(1)} async-done(((f32[32,1,512]{2,1,0:T(1,128)}), f32[32,1,512]{2,1,0:T(1,128)S(1)}, u32[]{:S(2)}, u32[]{:S(2)}) %all-to-all-start.1) | async-done | bytes 65568 | tf_op jit(solution)/shard_map/all_to_all | solution.py:346
  57.2 1.1 %settle.1 = bf16[32,16384]{1,0:T(8,128)(2,1)} custom-call(bf16[32,32,512]{2,1,0:T(8,128)(2,1)S(1)} %all-to-all-done.recv_ref, f32[32,1,512]{2,1,0:T(1,128)S(1)} %all-to-all-done.1.sums_ref, f32[32,1]{1,0:T(8,128)S(1)} %copy.10.gain_ref), custom_call_target="tpu_custom_call" | custom-call | tf_op jit(solution)/shard_map/settle/pallas_call | solution.py:310
  (3 shorter events, 0.0 us)
Async XLA Ops:
  0.0 49.8 %copy-start = (f32[1024]{0:T(1024)S(1)}, f32[1024]{0:T(1024)}, u32[]{:S(2)}) copy-start(f32[1024]{0:T(1024)} %param.14) | copy-start | bytes 12292
  0.0 6.9 %copy-start.1 = (f32[3,3,1024]{2,1,0:T(4,128)S(1)}, f32[3,3,1024]{2,1,0:T(4,128)}, u32[]{:S(2)}) copy-start(f32[3,3,1024]{2,1,0:T(4,128)} %sf_ref.5) | copy-start | bytes 110596
  0.0 7.0 %copy-start.4 = (s32[64]{0:T(128)S(1)}, s32[64]{0:T(128)}, u32[]{:S(2)}) copy-start(s32[64]{0:T(128)} %docs_ref.5) | copy-start | bytes 772
  0.0 7.0 %copy-start.3 = (f32[1024]{0:T(1024)S(1)}, f32[1024]{0:T(1024)}, u32[]{:S(2)}) copy-start(f32[1024]{0:T(1024)} %param.13) | copy-start | bytes 12292
  0.0 7.0 %copy-start.2 = (f32[64,128]{1,0:T(8,128)S(1)}, f32[64,128]{1,0:T(8,128)}, u32[]{:S(2)}) copy-start(f32[64,128]{1,0:T(8,128)} %taps_ref.3) | copy-start | bytes 98308
  2.3 12.5 %collective-permute-start = (bf16[8,144,128]{2,1,0:T(8,128)(2,1)S(1)}, bf16[8,144,128]{2,1,0:T(8,128)(2,1)S(1)}, u32[]{:S(2)}, u32[]{:S(2)}) collective-permute-start(bf16[8,144,128]{2,1,0:T(8,128)(2,1)S(1)} %tail.1), channel_id=1, source_target_pairs={{0,8},{8,16},{16,24},{24,32},{32,40},{40,48},{48,56},{56,64},{64,7... | collective-permute-start | bytes 884744 | tf_op jit(solution)/shard_map/ppermute | solution.py:340
  18.4 23.8 %all-to-all-start = ((bf16[32,32,512]{2,1,0:T(8,128)(2,1)}), bf16[32,32,512]{2,1,0:T(8,128)(2,1)S(1)}, u32[]{:S(2)}, u32[]{:S(2)}) async-start(bf16[32,32,512]{2,1,0:T(8,128)(2,1)} %bitcast.8), calls=%async_computation | async-start | bytes 2097152 | tf_op jit(solution)/shard_map/all_to_all | solution.py:343
  25.3 3.0 %collective-permute-start.1 = (f32[1,512]{1,0:T(1,128)S(1)}, f32[1,512]{1,0:T(1,128)S(1)}, u32[]{:S(2)}, u32[]{:S(2)}) collective-permute-start(f32[1,512]{1,0:T(1,128)S(1)} %get-tuple-element.21), channel_id=1, source_target_pairs={{0,1},{2,3},{4,5},{6,7},{1,0},{3,2},{5,4},{7,6},{8,9},{10,11},{12,... | collective-permute-start | bytes 6152 | tf_op jit(solution)/shard_map/ppermute | solution.py:327
  28.3 6.4 %collective-permute-start.2 = (f32[1,512]{1,0:T(1,128)S(1)}, f32[1,512]{1,0:T(1,128)S(1)}, u32[]{:S(2)}, u32[]{:S(2)}) collective-permute-start(f32[1,512]{1,0:T(1,128)S(1)} %add.12), channel_id=1, source_target_pairs={{1,2},{3,4},{5,6},{7,0},{2,1},{4,3},{6,5},{0,7},{9,10},{11,12},{13... | collective-permute-start | bytes 6152 | tf_op jit(solution)/shard_map/ppermute | solution.py:327
  34.7 4.5 %collective-permute-start.3 = (f32[1,512]{1,0:T(1,128)S(1)}, f32[1,512]{1,0:T(1,128)S(1)}, u32[]{:S(2)}, u32[]{:S(2)}) collective-permute-start(f32[1,512]{1,0:T(1,128)S(1)} %add.13), channel_id=1, source_target_pairs={{0,3},{7,4},{1,6},{2,5},{3,0},{4,7},{6,1},{5,2},{8,11},{15,12},{9,... | collective-permute-start | bytes 6152 | tf_op jit(solution)/shard_map/ppermute | solution.py:328
  42.9 14.3 %all-to-all-start.1 = ((f32[32,1,512]{2,1,0:T(1,128)}), f32[32,1,512]{2,1,0:T(1,128)S(1)}, u32[]{:S(2)}, u32[]{:S(2)}) async-start(f32[32,1,512]{2,1,0:T(1,128)} %broadcast_in_dim.9), calls=%async_computation.1 | async-start | bytes 131072 | tf_op jit(solution)/shard_map/all_to_all | solution.py:346

commit v8 on v7

--- a/solution.py
+++ b/solution.py
@@ -328,6 +328,19 @@
     return x, lax.ppermute(x, "ch", list(ROUNDS[-1]) + [(b, a) for a, b in ROUNDS[-1]])
 
 
+def copies_kernel(near_ref, far_ref, out_ref):
+    total = near_ref[...] + far_ref[...]
+    for i in range(out_ref.shape[0]):
+        out_ref[i] = total
+
+
+def copies(near, far, count):
+    return pl.pallas_call(
+        copies_kernel, out_shape=jax.ShapeDtypeStruct((count,) + near.shape, F32),
+        compiler_params=pltpu.CompilerParams(vmem_limit_bytes=8 << 20), name="copies",
+    )(near, far)
+
+
 def local(gate, key, value, sf, taps, skip, gain, docs):
     place = lax.axis_index("ctx")
     width = lax.axis_size("ctx")
@@ -342,8 +355,9 @@
     rows, squares = first(docs, base, halo, done, sf, skip, taps)
     recv = lax.all_to_all(rows.reshape(width, ch // width, n), "ctx", split_axis=0, concat_axis=0, tiled=True)
     near, far = channel_sum(squares)
-    far, recv = lax.optimization_barrier((far, recv))
-    sums = lax.all_to_all(jnp.broadcast_to((near + far)[None], (width, 1, n)), "ctx", split_axis=0, concat_axis=0, tiled=True)
+    total = copies(near, far, width)
+    total, recv = lax.optimization_barrier((total, recv))
+    sums = lax.all_to_all(total, "ctx", split_axis=0, concat_axis=0, tiled=True)
     return final(recv, sums, gain)
 
 

time: 58.6 us -> 58.6 us (level)
  local copies, waits for them, and re-layouts: 0.86 us -> 0.19 us
  starting transfers between devices: 27.5 us -> 28.1 us
  Pallas kernels: 14.8 us -> 15.4 us
  waiting for transfers between devices: 15.1 us -> 14.5 us
    broadcast_in_dim x1 -> x0, local copies, waits for them, and re-layouts: 0.67 us -> none  [local(): jnp.broadcast_to((near + far)[None], (width, 1, n))]
    all_to_all x1, starting transfers between devices: 6.96 us -> 7.59 us  [local(): sums = lax.all_to_all(total, 'ctx', split_axis=0, concat_axis=0, tiled=True)]
    all_to_all x1, waiting for transfers between devices: 2.98 us -> 2.35 us  [local(): lax.all_to_all(rows.reshape(width, ch // width, n), 'ctx', split_axis=0,...]
    pallas_call x0 -> x1, Pallas kernels: none -> 0.63 us  [copies(): pl.pallas_call(copies_kernel, out_shape=jax.ShapeDtypeStruct((count,) + n...]
  transfers between devices with their start and end apart: 6 -> 6, of which waited for: 5 -> 5; matrix products, arithmetic and copies ran while one was open for 0% -> 0% of each run, Pallas kernels for 13% -> 15%
where the time goes in v8:
time: 58.6 us; the launch traced here: 58.3 us
  starting transfers between devices  28.1 us (48%)
  Pallas kernels  15.4 us (26%)
  waiting for transfers between devices  14.5 us (25%)
    pallas_call x1, Pallas kernels, later(): pl.pallas_call(later_kernel, grid=(ch // c,), in_specs=[SMEM, SMEM, wide,...  7.87 us
    all_to_all x1, starting transfers between devices, local(): sums = lax.all_to_all(total, 'ctx', split_axis=0, concat_axis=0, tiled=True)  7.59 us
    all_to_all x1, waiting for transfers between devices, local(): sums = lax.all_to_all(total, 'ctx', split_axis=0, concat_axis=0, tiled=True)  7.19 us
    ppermute x2, starting transfers between devices, channel_sum(): x = x + lax.ppermute(x, 'ch', list(pairs) + [(b, a) for a, b in pairs])  7.12 us
    all_to_all x1, starting transfers between devices, local(): lax.all_to_all(rows.reshape(width, ch // width, n), 'ctx', split_axis=0,...  6.9 us
    ppermute x1, starting transfers between devices, local(): halo = lax.ppermute(ends, 'ctx', [(i, i + 1) for i in range(width - 1)])  4.6 us
    pallas_call x1, Pallas kernels, first(): pl.pallas_call(first_kernel, grid=(ch // c,), in_specs=[SMEM, SMEM, pl.Bl...  3.5 us
    ppermute x1, waiting for transfers between devices, channel_sum(): lax.ppermute(x, 'ch', list(ROUNDS[-1]) + [(b, a) for a, b in ROUNDS[-1]])  2.64 us
  transfers between devices with their start and end apart: 6, of which 5 were waited for; matrix products, arithmetic and copies ran while one was open for 0% of the time, Pallas kernels for 15%

profile of v8, /device:TPU:1, one launch (start us, length us, event | category | flops | bytes accessed | tf_op | source)
XLA Modules:
  0.0 58.3 jit_solution(11032814824215984284)
XLA Ops:
  0.0 0.0 copy-start
  0.0 0.0 copy-start.1
  0.0 0.0 copy-start.4
  0.0 0.0 copy-start.3
  0.0 0.0 copy-start.2
  0.0 2.3 %tail.1 = bf16[8,144,128]{2,1,0:T(8,128)(2,1)S(1)} custom-call(s32[64]{0:T(128)} %docs_ref.5, s32[1]{0:T(128)} %bitcast.base_ref, bf16[1024,512]{1,0:T(8,128)(2,1)} %gate_ref.3, bf16[1024,512]{1,0:T(8,128)(2,1)} %key_ref.3, bf16[1024,512]{1,0:T(8,128)(2,1)} %value_ref.3, f32[3,3,1024]{2,1,0:T(4,128)} %sf_ref.5), custom_call_target="tpu_custom_call" | custom-call | tf_op jit(solution)/shard_map/tail/pallas_call | solution.py:240
  2.3 4.6 %collective-permute-start = (bf16[8,144,128]{2,1,0:T(8,128)(2,1)S(1)}, bf16[8,144,128]{2,1,0:T(8,128)(2,1)S(1)}, u32[]{:S(2)}, u32[]{:S(2)}) collective-permute-start(bf16[8,144,128]{2,1,0:T(8,128)(2,1)S(1)} %tail.1), channel_id=1, source_target_pairs={{0,8},{8,16},{16,24},{24,32},{32,40},{40,48},{48,56},{56,64},{64,7... | collective-permute-start | bytes 884744 | tf_op jit(solution)/shard_map/ppermute | solution.py:353
  6.9 0.0 copy-done.1
  7.0 0.0 copy-done.4
  7.0 0.0 copy-done.3
  7.0 0.0 copy-done.2
  7.0 7.9 %later.1 = (bf16[1024,512]{1,0:T(8,128)(2,1)}, f32[1024,128]{1,0:T(8,128)S(1)}, bf16[1024,128]{1,0:T(8,128)(2,1)S(1)}, bf16[8,16,128]{2,1,0:T(8,128)(2,1)S(1)}, ...) custom-call(s32[64]{0:T(128)S(1)} %copy-done.4, s32[1]{0:T(128)} %bitcast.base_ref, bf16[1024,512]{1,0:T(8,128)(2,1)} %gate_ref.3, ...), custom_call_target="tpu_custom_call" | custom-call | flops 1610612736 | bytes 4194304 | tf_op jit(solution)/shard_map/later/pallas_call | solution.py:260
  14.9 0.0 collective-permute-done.halo_ref
  14.9 3.5 %first.1 = (bf16[1024,512]{1,0:T(8,128)(2,1)}, f32[1,512]{1,0:T(1,128)S(1)}) custom-call(s32[64]{0:T(128)S(1)} %copy-done.4, s32[1]{0:T(128)} %bitcast.base_ref, bf16[8,144,128]{2,1,0:T(8,128)(2,1)S(1)} %collective-permute-done.halo_ref, bf16[1024,512]{1,0:T(8,128)(2,1)} %get-tuple-element.15.rows_ref, ...), custom_call_target="tpu_custom_call", output_to_operand_aliasing={{0}: (3, {})} | custom-call | flops 536870912 | bytes 2097152 | tf_op jit(solution)/shard_map/first/pallas_call | solution.py:283
  18.4 6.9 %all-to-all-start = ((bf16[32,32,512]{2,1,0:T(8,128)(2,1)}), bf16[32,32,512]{2,1,0:T(8,128)(2,1)S(1)}, u32[]{:S(2)}, u32[]{:S(2)}) async-start(bf16[32,32,512]{2,1,0:T(8,128)(2,1)} %bitcast.7), calls=%async_computation | async-start | bytes 2097152 | tf_op jit(solution)/shard_map/all_to_all | solution.py:356
  25.3 1.7 %collective-permute-start.1 = (f32[1,512]{1,0:T(1,128)S(1)}, f32[1,512]{1,0:T(1,128)S(1)}, u32[]{:S(2)}, u32[]{:S(2)}) collective-permute-start(f32[1,512]{1,0:T(1,128)S(1)} %get-tuple-element.21), channel_id=1, source_target_pairs={{0,1},{2,3},{4,5},{6,7},{1,0},{3,2},{5,4},{7,6},{8,9},{10,11},{12,... | collective-permute-start | bytes 6152 | tf_op jit(solution)/shard_map/ppermute | solution.py:327
  27.0 1.3 %collective-permute-done.1 = f32[1,512]{1,0:T(1,128)S(1)} collective-permute-done((f32[1,512]{1,0:T(1,128)S(1)}, f32[1,512]{1,0:T(1,128)S(1)}, u32[]{:S(2)}, u32[]{:S(2)}) %collective-permute-start.1) | collective-permute-done | bytes 2080 | tf_op jit(solution)/shard_map/ppermute | solution.py:327
  28.3 5.4 %collective-permute-start.2 = (f32[1,512]{1,0:T(1,128)S(1)}, f32[1,512]{1,0:T(1,128)S(1)}, u32[]{:S(2)}, u32[]{:S(2)}) collective-permute-start(f32[1,512]{1,0:T(1,128)S(1)} %add.9), channel_id=1, source_target_pairs={{1,2},{3,4},{5,6},{7,0},{2,1},{4,3},{6,5},{0,7},{9,10},{11,12},{13... | collective-permute-start | bytes 6152 | tf_op jit(solution)/shard_map/ppermute | solution.py:327
  33.7 1.0 %collective-permute-done.2 = f32[1,512]{1,0:T(1,128)S(1)} collective-permute-done((f32[1,512]{1,0:T(1,128)S(1)}, f32[1,512]{1,0:T(1,128)S(1)}, u32[]{:S(2)}, u32[]{:S(2)}) %collective-permute-start.2) | collective-permute-done | bytes 2080 | tf_op jit(solution)/shard_map/ppermute | solution.py:327
  34.7 1.9 %collective-permute-start.3 = (f32[1,512]{1,0:T(1,128)S(1)}, f32[1,512]{1,0:T(1,128)S(1)}, u32[]{:S(2)}, u32[]{:S(2)}) collective-permute-start(f32[1,512]{1,0:T(1,128)S(1)} %add.10.near_ref), channel_id=1, source_target_pairs={{0,3},{7,4},{1,6},{2,5},{3,0},{4,7},{6,1},{5,2},{8,11},{15,12},{9,... | collective-permute-start | bytes 6152 | tf_op jit(solution)/shard_map/ppermute | solution.py:328
  36.6 2.6 %collective-permute-done.3.far_ref = f32[1,512]{1,0:T(1,128)S(1)} collective-permute-done((f32[1,512]{1,0:T(1,128)S(1)}, f32[1,512]{1,0:T(1,128)S(1)}, u32[]{:S(2)}, u32[]{:S(2)}) %collective-permute-start.3) | collective-permute-done | bytes 2080 | tf_op jit(solution)/shard_map/ppermute | solution.py:328
  39.2 0.6 %copies.1 = f32[32,1,512]{2,1,0:T(1,128)} custom-call(f32[1,512]{1,0:T(1,128)S(1)} %add.10.near_ref, f32[1,512]{1,0:T(1,128)S(1)} %collective-permute-done.3.far_ref), custom_call_target="tpu_custom_call" | custom-call | tf_op jit(solution)/shard_map/copies/pallas_call | solution.py:338
  39.8 2.3 %all-to-all-done.recv_ref = bf16[32,32,512]{2,1,0:T(8,128)(2,1)S(1)} async-done(((bf16[32,32,512]{2,1,0:T(8,128)(2,1)}), bf16[32,32,512]{2,1,0:T(8,128)(2,1)S(1)}, u32[]{:S(2)}, u32[]{:S(2)}) %all-to-all-start) | async-done | bytes 1048608 | tf_op jit(solution)/shard_map/all_to_all | solution.py:356
  42.2 7.6 %all-to-all-start.1 = ((f32[32,1,512]{2,1,0:T(1,128)}), f32[32,1,512]{2,1,0:T(1,128)S(1)}, u32[]{:S(2)}, u32[]{:S(2)}) async-start(f32[32,1,512]{2,1,0:T(1,128)} %copies.1), calls=%async_computation.1 | async-start | bytes 131072 | tf_op jit(solution)/shard_map/all_to_all | solution.py:360
  49.8 0.0 copy-done
  49.8 0.1 dynamic-slice_bitcast_fusion
  49.9 0.1 copy.10.gain_ref
  50.0 7.2 %all-to-all-done.1.sums_ref = f32[32,1,512]{2,1,0:T(1,128)S(1)} async-done(((f32[32,1,512]{2,1,0:T(1,128)}), f32[32,1,512]{2,1,0:T(1,128)S(1)}, u32[]{:S(2)}, u32[]{:S(2)}) %all-to-all-start.1) | async-done | bytes 65568 | tf_op jit(solution)/shard_map/all_to_all | solution.py:360
  57.1 1.1 %settle.1 = bf16[32,16384]{1,0:T(8,128)(2,1)} custom-call(bf16[32,32,512]{2,1,0:T(8,128)(2,1)S(1)} %all-to-all-done.recv_ref, f32[32,1,512]{2,1,0:T(1,128)S(1)} %all-to-all-done.1.sums_ref, f32[32,1]{1,0:T(8,128)S(1)} %copy.10.gain_ref), custom_call_target="tpu_custom_call" | custom-call | tf_op jit(solution)/shard_map/settle/pallas_call | solution.py:310
  (2 shorter events, 0.0 us)
Async XLA Ops:
  0.0 49.8 %copy-start = (f32[1024]{0:T(1024)S(1)}, f32[1024]{0:T(1024)}, u32[]{:S(2)}) copy-start(f32[1024]{0:T(1024)} %param.14) | copy-start | bytes 12292
  0.0 6.9 %copy-start.1 = (f32[3,3,1024]{2,1,0:T(4,128)S(1)}, f32[3,3,1024]{2,1,0:T(4,128)}, u32[]{:S(2)}) copy-start(f32[3,3,1024]{2,1,0:T(4,128)} %sf_ref.5) | copy-start | bytes 110596
  0.0 7.0 %copy-start.4 = (s32[64]{0:T(128)S(1)}, s32[64]{0:T(128)}, u32[]{:S(2)}) copy-start(s32[64]{0:T(128)} %docs_ref.5) | copy-start | bytes 772
  0.0 7.0 %copy-start.3 = (f32[1024]{0:T(1024)S(1)}, f32[1024]{0:T(1024)}, u32[]{:S(2)}) copy-start(f32[1024]{0:T(1024)} %param.13) | copy-start | bytes 12292
  0.0 7.0 %copy-start.2 = (f32[64,128]{1,0:T(8,128)S(1)}, f32[64,128]{1,0:T(8,128)}, u32[]{:S(2)}) copy-start(f32[64,128]{1,0:T(8,128)} %taps_ref.3) | copy-start | bytes 98308
  2.3 12.5 %collective-permute-start = (bf16[8,144,128]{2,1,0:T(8,128)(2,1)S(1)}, bf16[8,144,128]{2,1,0:T(8,128)(2,1)S(1)}, u32[]{:S(2)}, u32[]{:S(2)}) collective-permute-start(bf16[8,144,128]{2,1,0:T(8,128)(2,1)S(1)} %tail.1), channel_id=1, source_target_pairs={{0,8},{8,16},{16,24},{24,32},{32,40},{40,48},{48,56},{56,64},{64,7... | collective-permute-start | bytes 884744 | tf_op jit(solution)/shard_map/ppermute | solution.py:353
  18.4 23.8 %all-to-all-start = ((bf16[32,32,512]{2,1,0:T(8,128)(2,1)}), bf16[32,32,512]{2,1,0:T(8,128)(2,1)S(1)}, u32[]{:S(2)}, u32[]{:S(2)}) async-start(bf16[32,32,512]{2,1,0:T(8,128)(2,1)} %bitcast.7), calls=%async_computation | async-start | bytes 2097152 | tf_op jit(solution)/shard_map/all_to_all | solution.py:356
  25.3 3.0 %collective-permute-start.1 = (f32[1,512]{1,0:T(1,128)S(1)}, f32[1,512]{1,0:T(1,128)S(1)}, u32[]{:S(2)}, u32[]{:S(2)}) collective-permute-start(f32[1,512]{1,0:T(1,128)S(1)} %get-tuple-element.21), channel_id=1, source_target_pairs={{0,1},{2,3},{4,5},{6,7},{1,0},{3,2},{5,4},{7,6},{8,9},{10,11},{12,... | collective-permute-start | bytes 6152 | tf_op jit(solution)/shard_map/ppermute | solution.py:327
  28.3 6.4 %collective-permute-start.2 = (f32[1,512]{1,0:T(1,128)S(1)}, f32[1,512]{1,0:T(1,128)S(1)}, u32[]{:S(2)}, u32[]{:S(2)}) collective-permute-start(f32[1,512]{1,0:T(1,128)S(1)} %add.9), channel_id=1, source_target_pairs={{1,2},{3,4},{5,6},{7,0},{2,1},{4,3},{6,5},{0,7},{9,10},{11,12},{13... | collective-permute-start | bytes 6152 | tf_op jit(solution)/shard_map/ppermute | solution.py:327
  34.7 4.5 %collective-permute-start.3 = (f32[1,512]{1,0:T(1,128)S(1)}, f32[1,512]{1,0:T(1,128)S(1)}, u32[]{:S(2)}, u32[]{:S(2)}) collective-permute-start(f32[1,512]{1,0:T(1,128)S(1)} %add.10.near_ref), channel_id=1, source_target_pairs={{0,3},{7,4},{1,6},{2,5},{3,0},{4,7},{6,1},{5,2},{8,11},{15,12},{9,... | collective-permute-start | bytes 6152 | tf_op jit(solution)/shard_map/ppermute | solution.py:328
  42.2 15.0 %all-to-all-start.1 = ((f32[32,1,512]{2,1,0:T(1,128)}), f32[32,1,512]{2,1,0:T(1,128)S(1)}, u32[]{:S(2)}, u32[]{:S(2)}) async-start(f32[32,1,512]{2,1,0:T(1,128)} %copies.1), calls=%async_computation.1 | async-start | bytes 131072 | tf_op jit(solution)/shard_map/all_to_all | solution.py:360

commit v9 on v7

--- a/solution.py
+++ b/solution.py
@@ -317,7 +317,7 @@
     )(recv, sums, gain)
 
 
-ROUNDS = (((0, 1), (2, 3), (4, 5), (6, 7)), ((1, 2), (3, 4), (5, 6), (7, 0)), ((0, 3), (7, 4), (1, 6), (2, 5)))
+ROUNDS = (((0, 1), (2, 3), (4, 5), (6, 7)), ((0, 2), (1, 3), (4, 6), (5, 7)), ((0, 7), (1, 6), (2, 5), (3, 4)))
 
 
 def channel_sum(x):

time: 58.6 us -> 57.7 us (0.985)
    ppermute x1, starting transfers between devices: 1.88 us -> 4.77 us  [channel_sum(): lax.ppermute(x, 'ch', list(ROUNDS[-1]) + [(b, a) for a, b in ROUNDS[-1]])]
    ppermute x2, starting transfers between devices: 7.12 us -> 4.72 us  [channel_sum(): x = x + lax.ppermute(x, 'ch', list(pairs) + [(b, a) for a, b in pairs])]
    ppermute x1, waiting for transfers between devices: 2.65 us -> 1.27 us  [channel_sum(): lax.ppermute(x, 'ch', list(ROUNDS[-1]) + [(b, a) for a, b in ROUNDS[-1]])]
    all_to_all x1, starting transfers between devices: 6.96 us -> 6.06 us  [local(): lax.all_to_all(jnp.broadcast_to((near + far)[None], (width, 1, n)), 'ctx'...]
    all_to_all x1, waiting for transfers between devices: 2.98 us -> 3.61 us  [local(): lax.all_to_all(rows.reshape(width, ch // width, n), 'ctx', split_axis=0,...]
  transfers between devices with their start and end apart: 6 -> 6, of which waited for: 5 -> 5; matrix products, arithmetic and copies ran while one was open for 0% -> 0% of each run, Pallas kernels for 13% -> 14%
where the time goes in v9:
time: 57.7 us; the launch traced here: 57.4 us
  starting transfers between devices  27 us (47%)
  Pallas kernels  14.8 us (26%)
  waiting for transfers between devices  14.6 us (25%)
  local copies, waits for them, and re-layouts  0.86 us (1%)
    pallas_call x1, Pallas kernels, later(): pl.pallas_call(later_kernel, grid=(ch // c,), in_specs=[SMEM, SMEM, wide,...  7.87 us
    all_to_all x1, waiting for transfers between devices, local(): lax.all_to_all(jnp.broadcast_to((near + far)[None], (width, 1, n)), 'ctx'...  7.19 us
    all_to_all x1, starting transfers between devices, local(): lax.all_to_all(rows.reshape(width, ch // width, n), 'ctx', split_axis=0,...  6.9 us
    all_to_all x1, starting transfers between devices, local(): lax.all_to_all(jnp.broadcast_to((near + far)[None], (width, 1, n)), 'ctx'...  6.06 us
    ppermute x1, starting transfers between devices, channel_sum(): lax.ppermute(x, 'ch', list(ROUNDS[-1]) + [(b, a) for a, b in ROUNDS[-1]])  4.77 us
    ppermute x2, starting transfers between devices, channel_sum(): x = x + lax.ppermute(x, 'ch', list(pairs) + [(b, a) for a, b in pairs])  4.72 us
    ppermute x1, starting transfers between devices, local(): halo = lax.ppermute(ends, 'ctx', [(i, i + 1) for i in range(width - 1)])  4.6 us
    all_to_all x1, waiting for transfers between devices, local(): lax.all_to_all(rows.reshape(width, ch // width, n), 'ctx', split_axis=0,...  3.61 us
  transfers between devices with their start and end apart: 6, of which 5 were waited for; matrix products, arithmetic and copies ran while one was open for 0% of the time, Pallas kernels for 14%

profile of v9, /device:TPU:1, one launch (start us, length us, event | category | flops | bytes accessed | tf_op | source)
XLA Modules:
  0.0 57.4 jit_solution(352002875335139408)
XLA Ops:
  0.0 0.0 copy-start
  0.0 0.0 copy-start.1
  0.0 0.0 copy-start.4
  0.0 0.0 copy-start.3
  0.0 0.0 copy-start.2
  0.0 2.3 %tail.1 = bf16[8,144,128]{2,1,0:T(8,128)(2,1)S(1)} custom-call(s32[64]{0:T(128)} %docs_ref.5, s32[1]{0:T(128)} %bitcast.base_ref, bf16[1024,512]{1,0:T(8,128)(2,1)} %gate_ref.3, bf16[1024,512]{1,0:T(8,128)(2,1)} %key_ref.3, bf16[1024,512]{1,0:T(8,128)(2,1)} %value_ref.3, f32[3,3,1024]{2,1,0:T(4,128)} %sf_ref.5), custom_call_target="tpu_custom_call" | custom-call | tf_op jit(solution)/shard_map/tail/pallas_call | solution.py:240
  2.3 4.6 %collective-permute-start = (bf16[8,144,128]{2,1,0:T(8,128)(2,1)S(1)}, bf16[8,144,128]{2,1,0:T(8,128)(2,1)S(1)}, u32[]{:S(2)}, u32[]{:S(2)}) collective-permute-start(bf16[8,144,128]{2,1,0:T(8,128)(2,1)S(1)} %tail.1), channel_id=1, source_target_pairs={{0,8},{8,16},{16,24},{24,32},{32,40},{40,48},{48,56},{56,64},{64,7... | collective-permute-start | bytes 884744 | tf_op jit(solution)/shard_map/ppermute | solution.py:340
  6.9 0.0 copy-done.1
  7.0 0.0 copy-done.4
  7.0 0.0 copy-done.3
  7.0 0.0 copy-done.2
  7.0 7.9 %later.1 = (bf16[1024,512]{1,0:T(8,128)(2,1)}, f32[1024,128]{1,0:T(8,128)S(1)}, bf16[1024,128]{1,0:T(8,128)(2,1)S(1)}, bf16[8,16,128]{2,1,0:T(8,128)(2,1)S(1)}, ...) custom-call(s32[64]{0:T(128)S(1)} %copy-done.4, s32[1]{0:T(128)} %bitcast.base_ref, bf16[1024,512]{1,0:T(8,128)(2,1)} %gate_ref.3, ...), custom_call_target="tpu_custom_call" | custom-call | flops 1610612736 | bytes 4194304 | tf_op jit(solution)/shard_map/later/pallas_call | solution.py:260
  14.9 0.0 collective-permute-done.halo_ref
  14.9 3.5 %first.1 = (bf16[1024,512]{1,0:T(8,128)(2,1)}, f32[1,512]{1,0:T(1,128)S(1)}) custom-call(s32[64]{0:T(128)S(1)} %copy-done.4, s32[1]{0:T(128)} %bitcast.base_ref, bf16[8,144,128]{2,1,0:T(8,128)(2,1)S(1)} %collective-permute-done.halo_ref, bf16[1024,512]{1,0:T(8,128)(2,1)} %get-tuple-element.15.rows_ref, ...), custom_call_target="tpu_custom_call", output_to_operand_aliasing={{0}: (3, {})} | custom-call | flops 536870912 | bytes 2097152 | tf_op jit(solution)/shard_map/first/pallas_call | solution.py:283
  18.4 6.9 %all-to-all-start = ((bf16[32,32,512]{2,1,0:T(8,128)(2,1)}), bf16[32,32,512]{2,1,0:T(8,128)(2,1)S(1)}, u32[]{:S(2)}, u32[]{:S(2)}) async-start(bf16[32,32,512]{2,1,0:T(8,128)(2,1)} %bitcast.8), calls=%async_computation | async-start | bytes 2097152 | tf_op jit(solution)/shard_map/all_to_all | solution.py:343
  25.3 1.7 %collective-permute-start.1 = (f32[1,512]{1,0:T(1,128)S(1)}, f32[1,512]{1,0:T(1,128)S(1)}, u32[]{:S(2)}, u32[]{:S(2)}) collective-permute-start(f32[1,512]{1,0:T(1,128)S(1)} %get-tuple-element.21), channel_id=1, source_target_pairs={{0,1},{2,3},{4,5},{6,7},{1,0},{3,2},{5,4},{7,6},{8,9},{10,11},{12,... | collective-permute-start | bytes 6152 | tf_op jit(solution)/shard_map/ppermute | solution.py:327
  27.0 1.3 %collective-permute-done.1 = f32[1,512]{1,0:T(1,128)S(1)} collective-permute-done((f32[1,512]{1,0:T(1,128)S(1)}, f32[1,512]{1,0:T(1,128)S(1)}, u32[]{:S(2)}, u32[]{:S(2)}) %collective-permute-start.1) | collective-permute-done | bytes 2080 | tf_op jit(solution)/shard_map/ppermute | solution.py:327
  28.3 3.0 %collective-permute-start.2 = (f32[1,512]{1,0:T(1,128)S(1)}, f32[1,512]{1,0:T(1,128)S(1)}, u32[]{:S(2)}, u32[]{:S(2)}) collective-permute-start(f32[1,512]{1,0:T(1,128)S(1)} %add.12), channel_id=1, source_target_pairs={{0,2},{1,3},{4,6},{5,7},{2,0},{3,1},{6,4},{7,5},{8,10},{9,11},{12,... | collective-permute-start | bytes 6152 | tf_op jit(solution)/shard_map/ppermute | solution.py:327
  31.3 1.3 %collective-permute-done.2 = f32[1,512]{1,0:T(1,128)S(1)} collective-permute-done((f32[1,512]{1,0:T(1,128)S(1)}, f32[1,512]{1,0:T(1,128)S(1)}, u32[]{:S(2)}, u32[]{:S(2)}) %collective-permute-start.2) | collective-permute-done | bytes 2080 | tf_op jit(solution)/shard_map/ppermute | solution.py:327
  32.5 4.8 %collective-permute-start.3 = (f32[1,512]{1,0:T(1,128)S(1)}, f32[1,512]{1,0:T(1,128)S(1)}, u32[]{:S(2)}, u32[]{:S(2)}) collective-permute-start(f32[1,512]{1,0:T(1,128)S(1)} %add.13), channel_id=1, source_target_pairs={{0,7},{1,6},{2,5},{3,4},{7,0},{6,1},{5,2},{4,3},{8,15},{9,14},{10,... | collective-permute-start | bytes 6152 | tf_op jit(solution)/shard_map/ppermute | solution.py:328
  37.3 1.3 %collective-permute-done.3 = f32[1,512]{1,0:T(1,128)S(1)} collective-permute-done((f32[1,512]{1,0:T(1,128)S(1)}, f32[1,512]{1,0:T(1,128)S(1)}, u32[]{:S(2)}, u32[]{:S(2)}) %collective-permute-start.3) | collective-permute-done | bytes 2080 | tf_op jit(solution)/shard_map/ppermute | solution.py:328
  38.6 3.6 %all-to-all-done.recv_ref = bf16[32,32,512]{2,1,0:T(8,128)(2,1)S(1)} async-done(((bf16[32,32,512]{2,1,0:T(8,128)(2,1)}), bf16[32,32,512]{2,1,0:T(8,128)(2,1)S(1)}, u32[]{:S(2)}, u32[]{:S(2)}) %all-to-all-start) | async-done | bytes 1048608 | tf_op jit(solution)/shard_map/all_to_all | solution.py:343
  42.2 0.7 %broadcast_in_dim.9 = f32[32,1,512]{2,1,0:T(1,128)} broadcast(f32[512]{0:T(512)S(1)} %bitcast.9), dimensions={2} | broadcast | bytes 67584 | tf_op jit(solution)/shard_map/broadcast_in_dim | solution.py:346
  42.9 6.1 %all-to-all-start.1 = ((f32[32,1,512]{2,1,0:T(1,128)}), f32[32,1,512]{2,1,0:T(1,128)S(1)}, u32[]{:S(2)}, u32[]{:S(2)}) async-start(f32[32,1,512]{2,1,0:T(1,128)} %broadcast_in_dim.9), calls=%async_computation.1 | async-start | bytes 131072 | tf_op jit(solution)/shard_map/all_to_all | solution.py:346
  48.9 0.0 copy-done
  48.9 0.1 dynamic-slice_bitcast_fusion
  49.0 0.1 copy.10.gain_ref
  49.1 7.2 %all-to-all-done.1.sums_ref = f32[32,1,512]{2,1,0:T(1,128)S(1)} async-done(((f32[32,1,512]{2,1,0:T(1,128)}), f32[32,1,512]{2,1,0:T(1,128)S(1)}, u32[]{:S(2)}, u32[]{:S(2)}) %all-to-all-start.1) | async-done | bytes 65568 | tf_op jit(solution)/shard_map/all_to_all | solution.py:346
  56.3 1.1 %settle.1 = bf16[32,16384]{1,0:T(8,128)(2,1)} custom-call(bf16[32,32,512]{2,1,0:T(8,128)(2,1)S(1)} %all-to-all-done.recv_ref, f32[32,1,512]{2,1,0:T(1,128)S(1)} %all-to-all-done.1.sums_ref, f32[32,1]{1,0:T(8,128)S(1)} %copy.10.gain_ref), custom_call_target="tpu_custom_call" | custom-call | tf_op jit(solution)/shard_map/settle/pallas_call | solution.py:310
  (3 shorter events, 0.0 us)
Async XLA Ops:
  0.0 48.9 %copy-start = (f32[1024]{0:T(1024)S(1)}, f32[1024]{0:T(1024)}, u32[]{:S(2)}) copy-start(f32[1024]{0:T(1024)} %param.14) | copy-start | bytes 12292
  0.0 6.9 %copy-start.1 = (f32[3,3,1024]{2,1,0:T(4,128)S(1)}, f32[3,3,1024]{2,1,0:T(4,128)}, u32[]{:S(2)}) copy-start(f32[3,3,1024]{2,1,0:T(4,128)} %sf_ref.5) | copy-start | bytes 110596
  0.0 7.0 %copy-start.4 = (s32[64]{0:T(128)S(1)}, s32[64]{0:T(128)}, u32[]{:S(2)}) copy-start(s32[64]{0:T(128)} %docs_ref.5) | copy-start | bytes 772
  0.0 7.0 %copy-start.3 = (f32[1024]{0:T(1024)S(1)}, f32[1024]{0:T(1024)}, u32[]{:S(2)}) copy-start(f32[1024]{0:T(1024)} %param.13) | copy-start | bytes 12292
  0.0 7.0 %copy-start.2 = (f32[64,128]{1,0:T(8,128)S(1)}, f32[64,128]{1,0:T(8,128)}, u32[]{:S(2)}) copy-start(f32[64,128]{1,0:T(8,128)} %taps_ref.3) | copy-start | bytes 98308
  2.3 12.5 %collective-permute-start = (bf16[8,144,128]{2,1,0:T(8,128)(2,1)S(1)}, bf16[8,144,128]{2,1,0:T(8,128)(2,1)S(1)}, u32[]{:S(2)}, u32[]{:S(2)}) collective-permute-start(bf16[8,144,128]{2,1,0:T(8,128)(2,1)S(1)} %tail.1), channel_id=1, source_target_pairs={{0,8},{8,16},{16,24},{24,32},{32,40},{40,48},{48,56},{56,64},{64,7... | collective-permute-start | bytes 884744 | tf_op jit(solution)/shard_map/ppermute | solution.py:340
  18.4 23.8 %all-to-all-start = ((bf16[32,32,512]{2,1,0:T(8,128)(2,1)}), bf16[32,32,512]{2,1,0:T(8,128)(2,1)S(1)}, u32[]{:S(2)}, u32[]{:S(2)}) async-start(bf16[32,32,512]{2,1,0:T(8,128)(2,1)} %bitcast.8), calls=%async_computation | async-start | bytes 2097152 | tf_op jit(solution)/shard_map/all_to_all | solution.py:343
  25.3 3.0 %collective-permute-start.1 = (f32[1,512]{1,0:T(1,128)S(1)}, f32[1,512]{1,0:T(1,128)S(1)}, u32[]{:S(2)}, u32[]{:S(2)}) collective-permute-start(f32[1,512]{1,0:T(1,128)S(1)} %get-tuple-element.21), channel_id=1, source_target_pairs={{0,1},{2,3},{4,5},{6,7},{1,0},{3,2},{5,4},{7,6},{8,9},{10,11},{12,... | collective-permute-start | bytes 6152 | tf_op jit(solution)/shard_map/ppermute | solution.py:327
  28.3 4.3 %collective-permute-start.2 = (f32[1,512]{1,0:T(1,128)S(1)}, f32[1,512]{1,0:T(1,128)S(1)}, u32[]{:S(2)}, u32[]{:S(2)}) collective-permute-start(f32[1,512]{1,0:T(1,128)S(1)} %add.12), channel_id=1, source_target_pairs={{0,2},{1,3},{4,6},{5,7},{2,0},{3,1},{6,4},{7,5},{8,10},{9,11},{12,... | collective-permute-start | bytes 6152 | tf_op jit(solution)/shard_map/ppermute | solution.py:327
  32.5 6.0 %collective-permute-start.3 = (f32[1,512]{1,0:T(1,128)S(1)}, f32[1,512]{1,0:T(1,128)S(1)}, u32[]{:S(2)}, u32[]{:S(2)}) collective-permute-start(f32[1,512]{1,0:T(1,128)S(1)} %add.13), channel_id=1, source_target_pairs={{0,7},{1,6},{2,5},{3,4},{7,0},{6,1},{5,2},{4,3},{8,15},{9,14},{10,... | collective-permute-start | bytes 6152 | tf_op jit(solution)/shard_map/ppermute | solution.py:328
  42.9 13.4 %all-to-all-start.1 = ((f32[32,1,512]{2,1,0:T(1,128)}), f32[32,1,512]{2,1,0:T(1,128)S(1)}, u32[]{:S(2)}, u32[]{:S(2)}) async-start(f32[32,1,512]{2,1,0:T(1,128)} %broadcast_in_dim.9), calls=%async_computation.1 | async-start | bytes 131072 | tf_op jit(solution)/shard_map/all_to_all | solution.py:346
